TPU v7x, 32 devices: a whole 2x2x4 slice. The times are simulated.
32 devices in a mesh: ctx: 4 (over x, core), exp: 8 (over z, y).
Axes of the slice: x: 2, y: 2, z: 4, core: 2. Of those that a mesh axis runs over, the one named last changes fastest.
Arguments:
- inputs: bfloat16 [8, 1536, 768], P('exp', 'ctx'), may hold values from -6 to 6
- segments: int32 [8, 1536], P('exp', 'ctx'), may hold values from 0 to 15, as said below
- routes: int32 [8, 1536, 1], P('exp', 'ctx'), may hold values from 0 to 7; in each aligned block of 384 rows (0 to 383, 384 to 767, ..., all dimensions but the last counted through in order) at most 60 rows name the same one
- cotangent: bfloat16 [8, 1536, 768], P('exp', 'ctx'), may hold values from -6 to 6
- norm_gain: bfloat16 [768], P(('ctx', 'exp')), may hold values from 0.5 to 1.5
- in_proj: bfloat16 [768, 3072], P(('ctx', 'exp')), may hold values from -0.21875 to 0.21875
- conv_taps: bfloat16 [1536, 4], P(('ctx', 'exp')), may hold values from -3 to 3
- conv_bias: bfloat16 [1536], P(('ctx', 'exp')), may hold values from -1.5 to 1.5
- x_proj: bfloat16 [1536, 80], P(('ctx', 'exp')), may hold values from -0.15625 to 0.15625
- dt_proj: bfloat16 [48, 1536], P(None, ('ctx', 'exp')), may hold values from -0.875 to 0.875
- dt_bias: bfloat16 [1536], P(('ctx', 'exp')), may hold values from -5.5 to -3.5
- log_decay: bfloat16 [1536, 16], P(('ctx', 'exp')), may hold values from -4 to 1.1953125
- skip_gain: bfloat16 [1536], P(('ctx', 'exp')), may hold values from 0.5 to 1.5
- out_proj: bfloat16 [1536, 768], P(('ctx', 'exp')), may hold values from -0.3125 to 0.3125
- moe_gain: bfloat16 [768], P(('ctx', 'exp')), may hold values from 0.5 to 1.5
- router: bfloat16 [768, 8], P(('ctx', 'exp')), may hold values from -0.15625 to 0.15625
- expert_in: bfloat16 [8, 768, 3072], P('exp', None, 'ctx'), may hold values from -0.21875 to 0.21875
- expert_out: bfloat16 [8, 3072, 768], P('exp', 'ctx'), may hold values from -0.875 to 0.875
Outputs:
- outputs: bfloat16 [8, 1536, 768], P('exp', 'ctx')
- grad_inputs: float32 [8, 1536, 768], P('exp', 'ctx')
- grad_norm_gain: float32 [768], P(('ctx', 'exp'))
- grad_in_proj: float32 [768, 3072], P(('ctx', 'exp'))
- grad_conv_taps: float32 [1536, 4], P(('ctx', 'exp'))
- grad_conv_bias: float32 [1536], P(('ctx', 'exp'))
- grad_x_proj: float32 [1536, 80], P(('ctx', 'exp'))
- grad_dt_proj: float32 [48, 1536], P(None, ('ctx', 'exp'))
- grad_dt_bias: float32 [1536], P(('ctx', 'exp'))
- grad_log_decay: float32 [1536, 16], P(('ctx', 'exp'))
- grad_skip_gain: float32 [1536], P(('ctx', 'exp'))
- grad_out_proj: float32 [1536, 768], P(('ctx', 'exp'))
- grad_moe_gain: float32 [768], P(('ctx', 'exp'))
- grad_router: float32 [768, 8], P(('ctx', 'exp'))
- grad_expert_in: float32 [8, 768, 3072], P('exp', None, 'ctx')
- grad_expert_out: float32 [8, 3072, 768], P('exp', 'ctx')
Inputs may be any that keep to these rules, and one draw needn't show every extreme that they name: `segments`: segment numbers start at 0 and never fall along a sequence; each sequence holds one document that begins among its first 192 positions and ends within its last 192 positions, and each sequence's last document is number 16 - 1. `routes`: among the tokens of one device (aligned blocks of 384 positions), no expert is named more than 60 times, and some expert exactly that many.
All inputs are finite; a program needn't handle non-finite values.
Results may differ from a plain program's by a relative error of at most 0.017.
Values may be sent and summed in bfloat16 or wider, within the bound.
A program may use at most 192 MiB of HBM per device.

v0:
```python
import functools

import jax
import jax.numpy as jnp
from jax import lax
from jax.experimental import pallas as pl
from jax.experimental.pallas import tpu as pltpu
from jax.sharding import PartitionSpec as P

D = 768
DI = 1536
NS = 16
R = 48
KC = 4
LANES = 128
UNROLL = 8
LOG2E = 1.4426950408889634


EPS = 1e-05
MESH = pl.DeviceIdType.MESH
ROWS_AT_ONCE = 16
EDGE = 16

def tile(ref, base, lanes):
    return ref[pl.ds(pl.multiple_of(base, UNROLL), UNROLL), lanes]

def row(rows_now, place):
    return jnp.broadcast_to(rows_now[place : place + 1], (NS, LANES))

def put_row(rows_now, place, value):
    at = lax.broadcasted_iota(jnp.int32, (UNROLL, LANES), 0)
    value = jnp.broadcast_to(value, (UNROLL, LANES))
    return value if rows_now is None else jnp.where(at == place, value, rows_now)

def cost(tokens, channels, share):
    size = tokens * channels * NS
    return pl.CostEstimate(flops=size * share, transcendentals=size, bytes_accessed=size * share)


def pick(channels):
    return 512 if channels % 512 == 0 else 128


def shifted(value, axis, steps):
    count = lax.axis_size(axis)
    initial, last = (max(0, -steps), min(count, count - steps))
    return lax.ppermute(value, axis, [(source, source + steps) for source in range(initial, last)])


def rms_scale(values, gain):
    return values * lax.rsqrt(jnp.mean(values * values, axis=-1, keepdims=True) + EPS) * gain


def conv_local(ext_rows, taps, bias, ext_ids):
    length = ext_rows.shape[0] - (KC - 1)
    own_ids = ext_ids[KC - 1 :]
    result = jnp.zeros((length, ext_rows.shape[1]), jnp.float32) + bias[None, :]
    for offset in range(KC):
        same_doc = (ext_ids[offset : offset + length] == own_ids).astype(jnp.float32)
        result = (
            result
            + taps[:, offset][None, :] * ext_rows[offset : offset + length] * same_doc[:, None]
        )
    return result


def bit_positions(sizes):
    return [(axis, size.bit_length() - 2 - k) for axis, size in sizes for k in range(size.bit_length() - 1)]


def own_bit(place):
    axis, level = place
    return lax.rem(lax.axis_index(axis) // 2**level, 2)


def partner(place):
    axis, level = place
    where = {"ctx": lax.axis_index("ctx"), "exp": lax.axis_index("exp")}
    where[axis] = where[axis] + (1 - 2 * own_bit(place)) * 2**level
    return (where["ctx"], where["exp"])


def meet(places, *others):
    barrier = pltpu.get_barrier_semaphore()
    for device in [partner(place) for place in places] + list(others):
        pl.semaphore_signal(barrier, inc=1, device_id=device, device_id_type=MESH)
    pl.semaphore_wait(barrier, len(places) + len(others))


class GatherFlow:
    def __init__(self, places, streams, shards, wholes, send_sems, recv_sems, local_sems):
        self.places, self.streams, self.shards, self.wholes = places, streams, shards, wholes
        self.sems = send_sems, recv_sems, local_sems
        self.bits = [own_bit(place) for place in places]

    def view(self, number, have):
        array, cols, order = self.streams[number]
        index = tuple(slice(None) if p in have else self.bits[p] for p in range(len(self.places)))
        return self.wholes[array].at[index + (slice(None), cols)]

    def own(self, number):
        array, cols, order = self.streams[number]
        return pltpu.make_async_copy(
            self.shards[array].at[:, cols], self.view(number, ()), self.sems[2].at[number]
        )

    def flight(self, number, stage):
        array, cols, order = self.streams[number]
        target = self.view(number, order[:stage])
        return pltpu.make_async_remote_copy(
            src_ref=self.shards[array].at[:, cols] if stage == 0 else target,
            dst_ref=target,
            send_sem=self.sems[0].at[number, stage],
            recv_sem=self.sems[1].at[number, stage],
            device_id=partner(self.places[order[stage]]),
            device_id_type=MESH,
        )

    def start(self):
        for number in range(len(self.streams)):
            self.flight(number, 0).start()
        for number in range(len(self.streams)):
            self.own(number).start()

    def advance(self, stage):
        for number in range(len(self.streams)):
            if stage == 0:
                self.own(number).wait()
            self.flight(number, stage).wait_recv()
            if stage + 1 < len(self.places):
                self.flight(number, stage + 1).start()

    def finish(self):
        for number in range(len(self.streams)):
            for stage in range(len(self.places)):
                self.flight(number, stage).wait_send()


def gather_kernel(places, streams, count, *refs):
    shards, edge_ref, wholes, prior_ref = refs[:count], refs[count], refs[count + 1 : 2 * count + 1], refs[2 * count + 1]
    send_sems, recv_sems, local_sems, edge_sems = refs[2 * count + 2 :]
    flow = GatherFlow(places, streams, shards, wholes, send_sems, recv_sems, local_sems)
    blocks = lax.axis_size("ctx")
    here, line = lax.axis_index("ctx"), lax.axis_index("exp")
    meet(places, (lax.rem(here + 1, blocks), line), (lax.rem(here + blocks - 1, blocks), line))
    flow.start()
    edge = pltpu.make_async_remote_copy(
        src_ref=edge_ref,
        dst_ref=prior_ref,
        send_sem=edge_sems.at[0],
        recv_sem=edge_sems.at[1],
        device_id=(lax.rem(here + 1, blocks), line),
        device_id_type=MESH,
    )
    edge.start()
    for stage in range(len(places)):
        flow.advance(stage)
    flow.finish()
    edge.wait()


def orders_of(places):
    core = places.index(("ctx", 0))
    rows = [k for k, place in enumerate(places) if place[0] == "ctx" and place[1] > 0]
    near = places.index(("exp", 0))
    far = [k for k, place in sorted(enumerate(places), key=lambda item: item[1][1]) if place[0] == "exp" and place[1] > 0]
    return [core] + rows + [near] + far, [core, near] + rows + far


def streams_of(places, arrays, gathering):
    first, second = [tuple(reversed(order)) if gathering else tuple(order) for order in orders_of(places)]
    streams = []
    for array, values in enumerate(arrays):
        width = values.shape[1]
        if width % 256 == 0:
            streams.append((array, slice(0, width // 2), first))
            streams.append((array, slice(width // 2, width), second))
        else:
            streams.append((array, slice(0, width), first if array % 2 else second))
    return streams


def gather_all(sizes, shards, edge, identity):
    places = bit_positions(sizes)
    streams = streams_of(places, shards, True)
    stages = len(places)
    anywhere = pl.BlockSpec(memory_space=pl.ANY)
    *wholes, prior = pl.pallas_call(
        functools.partial(gather_kernel, places, streams, len(shards)),
        in_specs=[anywhere] * (len(shards) + 1),
        out_specs=[anywhere] * (len(shards) + 1),
        out_shape=[jax.ShapeDtypeStruct((2,) * stages + shard.shape, shard.dtype) for shard in shards]
        + [jax.ShapeDtypeStruct(edge.shape, edge.dtype)],
        scratch_shapes=[
            pltpu.SemaphoreType.DMA((len(streams), stages)),
            pltpu.SemaphoreType.DMA((len(streams), stages)),
            pltpu.SemaphoreType.DMA((len(streams),)),
            pltpu.SemaphoreType.DMA((2,)),
        ],
        compiler_params=pltpu.CompilerParams(collective_id=identity, has_side_effects=True),
        name="gather_all",
    )(*shards, edge)
    return [whole.reshape((-1,) + whole.shape[stages + 1 :]) for whole in wholes], prior


class ReduceFlow:
    def __init__(self, places, streams, parts, totals, landing, send_sems, recv_sems):
        self.places, self.streams, self.parts, self.totals = places, streams, parts, totals
        self.landing, self.sems = landing, (send_sems, recv_sems)
        self.bits = [own_bit(place) for place in places]

    def spot(self, number, stage):
        return self.landing[number * len(self.places) + stage]

    def side(self, number, stage, value):
        array, cols, order = self.streams[number]
        left = [p for p in range(len(self.places)) if p not in order[:stage]]
        index = tuple(value if p == order[stage] else slice(None) for p in left)
        if stage == 0:
            return self.parts[array].at[index + (slice(None), cols)]
        return self.spot(number, stage - 1).at[index]

    def flight(self, number, stage):
        order = self.streams[number][2]
        return pltpu.make_async_remote_copy(
            src_ref=self.side(number, stage, 1 - self.bits[order[stage]]),
            dst_ref=self.spot(number, stage),
            send_sem=self.sems[0].at[number, stage],
            recv_sem=self.sems[1].at[number, stage],
            device_id=partner(self.places[order[stage]]),
            device_id_type=MESH,
        )

    def start(self):
        for number in range(len(self.streams)):
            self.flight(number, 0).start()

    def advance(self, stage):
        stages = len(self.places)
        for number, (array, cols, order) in enumerate(self.streams):
            self.flight(number, stage).wait_recv()
            mine = self.side(number, stage, self.bits[order[stage]])
            there = self.spot(number, stage)
            if stage + 1 == stages:
                self.totals[array][:, cols] = there[...].astype(jnp.float32) + mine[...].astype(jnp.float32)
                continue
            depth = stages - stage - 1

            def add(index, unused, there=there, mine=mine, depth=depth):
                at = tuple(lax.rem(index // 2 ** (depth - 1 - k), 2) for k in range(depth))
                there[at] = (there[at].astype(jnp.float32) + mine[at].astype(jnp.float32)).astype(there.dtype)
                return unused

            lax.fori_loop(0, 2**depth, add, 0)
            self.flight(number, stage + 1).start()

    def finish(self):
        for number in range(len(self.streams)):
            for stage in range(len(self.places)):
                self.flight(number, stage).wait_send()


def reduce_kernel(places, streams, count, *refs):
    parts, totals = refs[:count], refs[count : 2 * count]
    landing = refs[2 * count : 2 * count + len(streams) * len(places)]
    send_sems, recv_sems = refs[2 * count + len(streams) * len(places) :]
    flow = ReduceFlow(places, streams, parts, totals, landing, send_sems, recv_sems)
    meet(places)
    flow.start()
    for stage in range(len(places)):
        flow.advance(stage)
    flow.finish()


def landing_of(places, streams, divided):
    stages = len(places)
    landing = []
    for array, cols, order in streams:
        for stage in range(stages):
            rows = divided[array].shape[-2]
            landing.append(pltpu.VMEM((2,) * (stages - stage - 1) + (rows, cols.stop - cols.start), jnp.bfloat16))
    return landing


def reduce_all(sizes, parts, identity):
    places = bit_positions(sizes)
    stages = len(places)
    streams = streams_of(places, parts, False)
    divided = [part.reshape((2,) * stages + (-1, part.shape[1])) for part in parts]
    inside = pl.BlockSpec(memory_space=pltpu.VMEM)
    return pl.pallas_call(
        functools.partial(reduce_kernel, places, streams, len(parts)),
        in_specs=[inside] * len(parts),
        out_specs=[inside] * len(parts),
        out_shape=[jax.ShapeDtypeStruct(block.shape[-2:], jnp.float32) for block in divided],
        scratch_shapes=landing_of(places, streams, divided)
        + [
            pltpu.SemaphoreType.DMA((len(streams), stages)),
            pltpu.SemaphoreType.DMA((len(streams), stages)),
        ],
        compiler_params=pltpu.CompilerParams(
            collective_id=identity, has_side_effects=True, vmem_limit_bytes=48 * 1024 * 1024
        ),
        name="reduce_all",
    )(*divided)


def dot(left, right):
    return jnp.dot(left, right, preferred_element_type=jnp.float32)


def contract(left, right, left_dim, right_dim):
    return lax.dot_general(left, right, (((left_dim,), (right_dim,)), ((), ())), preferred_element_type=jnp.float32)


def lanes_of(group, width, k):
    return pl.ds(pl.multiple_of(group * width + k * LANES, LANES), LANES)


def spread_columns(source_ref, wide_ref):
    def chunk(index, unused):
        base = pl.multiple_of(index * LANES, LANES)
        now = source_ref[:, pl.ds(base, LANES)]
        for place in range(LANES):
            wide_ref[base + place] = jnp.broadcast_to(now[:, place : place + 1], (NS, LANES))
        return unused

    lax.fori_loop(0, source_ref.shape[1] // LANES, chunk, 0)


def end_pass(width, step_ref, push_ref, wide_b, rate_ref, state_ref, hook):
    rows, channels = step_ref.shape
    count = width // LANES

    def group_body(group, unused):
        pieces = [lanes_of(group, width, k) for k in range(count)]
        rates = [rate_ref[:, lanes] for lanes in pieces]

        def block(index, states):
            states = list(states)
            steps = [tile(step_ref, index * UNROLL, lanes) for lanes in pieces]
            pushes = [tile(push_ref, index * UNROLL, lanes) for lanes in pieces]
            for place in range(UNROLL):
                b_now = wide_b[index * UNROLL + place]
                for k in range(count):
                    decay = jnp.exp2(row(steps[k], place) * rates[k])
                    states[k] = decay * states[k] + b_now * row(pushes[k], place)
            return tuple(states)

        zero = jnp.zeros((NS, LANES), jnp.float32)
        states = lax.fori_loop(0, rows // UNROLL, block, (zero,) * count)
        for k, lanes in enumerate(pieces):
            state_ref[:, lanes] = states[k]
        hook(group)
        return unused

    lax.fori_loop(0, channels // width, group_body, 0)


def out_pass(width, step_ref, push_ref, wide_b, wide_c, rate_ref, state_ref, y_ref, kept_buf, kept_copy, hook):
    rows, channels = step_ref.shape
    count = width // LANES
    span = kept_buf.shape[1]
    blocks = rows // span

    def time_body(number, unused):
        slot = lax.rem(number, 2)

        @pl.when(number >= 2)
        def _():
            kept_copy(number - 2, slot).wait()

        def group_body(group, unused_inner):
            pieces = [lanes_of(group, width, k) for k in range(count)]
            rates = [rate_ref[:, lanes] for lanes in pieces]

            def block(index, states):
                states = list(states)
                base = number * span + index * UNROLL
                steps = [tile(step_ref, base, lanes) for lanes in pieces]
                pushes = [tile(push_ref, base, lanes) for lanes in pieces]
                outs = [None] * count
                for place in range(UNROLL):
                    b_now = wide_b[base + place]
                    c_now = wide_c[base + place]
                    for k, lanes in enumerate(pieces):
                        decay = jnp.exp2(row(steps[k], place) * rates[k])
                        states[k] = decay * states[k] + b_now * row(pushes[k], place)
                        kept_buf[slot, index * UNROLL + place, :, lanes] = states[k].astype(kept_buf.dtype)
                        outs[k] = put_row(outs[k], place, jnp.sum(states[k] * c_now, axis=0, keepdims=True))
                for k, lanes in enumerate(pieces):
                    y_ref[pl.ds(pl.multiple_of(base, UNROLL), UNROLL), lanes] = outs[k]
                return tuple(states)

            states = lax.fori_loop(0, span // UNROLL, block, tuple(state_ref[:, lanes] for lanes in pieces))
            for k, lanes in enumerate(pieces):
                state_ref[:, lanes] = states[k]
            return unused_inner

        lax.fori_loop(0, channels // width, group_body, 0)
        kept_copy(number, slot).start()
        hook(number)
        return unused

    lax.fori_loop(0, blocks, time_body, 0)
    for number in range(max(0, blocks - 2), blocks):
        kept_copy(number, number % 2).wait()


def inflow_pass(width, step_ref, grad_ref, wide_c, rate_ref, flow_ref, hook):
    rows, channels = step_ref.shape
    count = width // LANES

    def group_body(group, unused):
        pieces = [lanes_of(group, width, k) for k in range(count)]
        rates = [rate_ref[:, lanes] for lanes in pieces]

        def block(index, flows):
            flows = list(flows)
            base = rows - UNROLL - index * UNROLL
            steps = [tile(step_ref, base, lanes) for lanes in pieces]
            grads = [tile(grad_ref, base, lanes) for lanes in pieces]
            for place in reversed(range(UNROLL)):
                c_now = wide_c[base + place]
                for k in range(count):
                    decay = jnp.exp2(row(steps[k], place) * rates[k])
                    flows[k] = decay * (c_now * row(grads[k], place) + flows[k])
            return tuple(flows)

        zero = jnp.zeros((NS, LANES), jnp.float32)
        flows = lax.fori_loop(0, rows // UNROLL, block, (zero,) * count)
        for k, lanes in enumerate(pieces):
            flow_ref[:, lanes] = flows[k]
        hook(group)
        return unused

    lax.fori_loop(0, channels // width, group_body, 0)


def lane_sums(part_ref):
    values = part_ref[...].reshape(-1, LANES)
    high = values.astype(jnp.bfloat16)
    low = (values - high.astype(jnp.float32)).astype(jnp.bfloat16)
    ones = jnp.ones((UNROLL, LANES), jnp.bfloat16)
    return contract(ones, high, 1, 1) + contract(ones, low, 1, 1)


def adjoint_pass(width, step_ref, push_ref, grad_ref, wide_b, wide_c, rate_ref, flow_ref, kept_buf, kept_copy,
                 along_ref, slope_ref, gb_ref, gc_ref, ga_ref, part_b, part_c, hook):
    rows, channels = step_ref.shape
    count = width // LANES
    span = kept_buf.shape[1] - 1
    blocks = rows // span
    ga_ref[...] = jnp.zeros_like(ga_ref)

    def time_body(order, unused):
        slot = lax.rem(order, 2)
        number = blocks - 1 - order
        kept_copy(number, slot).wait()
        part_b[...] = jnp.zeros_like(part_b)
        part_c[...] = jnp.zeros_like(part_c)

        def group_body(group, unused_inner):
            pieces = [lanes_of(group, width, k) for k in range(count)]
            rates = [rate_ref[:, lanes] for lanes in pieces]

            def block(index, carried):
                flows = list(carried[:count])
                sums = list(carried[count : 2 * count])
                current = list(carried[2 * count :])
                local = span - UNROLL - index * UNROLL
                base = number * span + local
                steps = [tile(step_ref, base, lanes) for lanes in pieces]
                pushes = [tile(push_ref, base, lanes) for lanes in pieces]
                grads = [tile(grad_ref, base, lanes) for lanes in pieces]
                alongs = [None] * count
                slopes = [None] * count
                for place in reversed(range(UNROLL)):
                    b_now = wide_b[base + place]
                    c_now = wide_c[base + place]
                    gb = gc = None
                    for k, lanes in enumerate(pieces):
                        prior = kept_buf[slot, local + place, :, lanes].astype(jnp.float32)
                        step = row(steps[k], place)
                        grad = row(grads[k], place)
                        decay = jnp.exp2(step * rates[k])
                        adjoint = c_now * grad + flows[k]
                        flows[k] = decay * adjoint
                        decay_grad = flows[k] * prior
                        alongs[k] = put_row(alongs[k], place, jnp.sum(adjoint * b_now, axis=0, keepdims=True))
                        slopes[k] = put_row(slopes[k], place, jnp.sum(decay_grad * rates[k], axis=0, keepdims=True))
                        sums[k] = sums[k] + decay_grad * step
                        here_b = adjoint * row(pushes[k], place)
                        here_c = current[k] * grad
                        gb = here_b if gb is None else gb + here_b
                        gc = here_c if gc is None else gc + here_c
                        current[k] = prior
                    part_b[local + place] += gb
                    part_c[local + place] += gc
                where = pl.ds(pl.multiple_of(base, UNROLL), UNROLL)
                for k, lanes in enumerate(pieces):
                    along_ref[where, lanes] = alongs[k]
                    slope_ref[where, lanes] = slopes[k]
                return tuple(flows + sums + current)

            carried = lax.fori_loop(
                0,
                span // UNROLL,
                block,
                tuple(flow_ref[:, lanes] for lanes in pieces)
                + tuple(ga_ref[:, lanes] for lanes in pieces)
                + tuple(kept_buf[slot, span, :, lanes].astype(jnp.float32) for lanes in pieces),
            )
            for k, lanes in enumerate(pieces):
                flow_ref[:, lanes] = carried[k]
                ga_ref[:, lanes] = carried[count + k]
            return unused_inner

        lax.fori_loop(0, channels // width, group_body, 0)
        gb_ref[number] = lane_sums(part_b)
        gc_ref[number] = lane_sums(part_c)

        @pl.when(order + 2 < blocks)
        def _():
            kept_copy(number - 2, slot).start()

        hook(order)
        return unused

    lax.fori_loop(0, blocks, time_body, 0)


def share(source, target, send_sems, recv_sems):
    blocks = lax.axis_size("ctx")
    here, line = lax.axis_index("ctx"), lax.axis_index("exp")
    copies = []
    for step in range(1, blocks):
        copies.append(
            pltpu.make_async_remote_copy(
                src_ref=source,
                dst_ref=target.at[here],
                send_sem=send_sems.at[step],
                recv_sem=recv_sems.at[step],
                device_id=(lax.rem(here + step, blocks), line),
                device_id_type=MESH,
            )
        )
        copies[-1].start()
    target[here] = source[...]
    return copies


def row_peers():
    blocks = lax.axis_size("ctx")
    here, line = lax.axis_index("ctx"), lax.axis_index("exp")
    return [(lax.rem(here + step, blocks), line) for step in range(1, blocks)]


def forward_kernel(places, streams, width, *refs):
    step_ref, push_ref, bt_ref, ct_ref, rate_ref = refs[:5]
    shards = refs[5:7]
    y_ref, start_ref, product_ref, kept_ref = refs[7:11]
    wholes = refs[11:13]
    (wide_b, wide_c, kept_buf, first_buf, state_ref, message, products, ends,
     kept_sems, first_sem, share_sems, send_sems, recv_sems, local_sems) = refs[13:]
    blocks = lax.axis_size("ctx")
    position = lax.axis_index("ctx")
    span = kept_buf.shape[1]
    flow = GatherFlow(places, streams, shards, wholes, send_sems, recv_sems, local_sems)
    meet([place for place in places if place[0] == "exp"], *row_peers())
    flow.start()

    message[0] = jnp.exp2(jnp.sum(step_ref[...], axis=0, keepdims=True) * rate_ref[...]).astype(jnp.bfloat16)
    early = share(message.at[0], products, share_sems.at[0], share_sems.at[1])
    spread_columns(bt_ref, wide_b)
    spread_columns(ct_ref, wide_c)

    def first_hook(group):
        @pl.when(group == 1)
        def _():
            flow.advance(0)

    end_pass(width, step_ref, push_ref, wide_b, rate_ref, state_ref, first_hook)
    message[1] = state_ref[...].astype(jnp.bfloat16)
    late = share(message.at[1], ends, share_sems.at[2], share_sems.at[3])
    for copy in early + late:
        copy.wait_recv()
    start = jnp.zeros(state_ref.shape, jnp.float32)
    for index in range(blocks):
        folded = products[index].astype(jnp.float32) * start + ends[index].astype(jnp.float32)
        start = jnp.where(index < position, folded, start)
    state_ref[...] = start
    start_ref[...] = start
    product_ref[...] = products[...]
    first_buf[0] = start.astype(jnp.bfloat16)
    first_copy = pltpu.make_async_copy(first_buf, kept_ref.at[pl.ds(0, 1)], first_sem)
    first_copy.start()
    flow.advance(1)

    def kept_copy(number, slot):
        return pltpu.make_async_copy(
            kept_buf.at[slot], kept_ref.at[pl.ds(1 + number * span, span)], kept_sems.at[slot]
        )

    def second_hook(number):
        @pl.when(number == 1)
        def _():
            flow.advance(2)

    out_pass(width, step_ref, push_ref, wide_b, wide_c, rate_ref, state_ref, y_ref, kept_buf, kept_copy, second_hook)
    for stage in range(3, len(places)):
        flow.advance(stage)
    flow.finish()
    first_copy.wait()
    for copy in early + late:
        copy.wait_send()


def scan_forward(sizes, step, push, b_turned, c_turned, rates, shards, identity, span=64):
    places = bit_positions(sizes)
    streams = streams_of(places, shards, True)
    stages = len(places)
    tokens, channels = step.shape
    blocks = sizes[0][1]
    inside = pl.BlockSpec(memory_space=pltpu.VMEM)
    anywhere = pl.BlockSpec(memory_space=pl.ANY)
    half = jnp.bfloat16
    y, start, products, kept, *wholes = pl.pallas_call(
        functools.partial(forward_kernel, places, streams, pick(channels)),
        in_specs=[inside] * 5 + [anywhere] * 2,
        out_specs=[inside] * 3 + [anywhere] * 3,
        out_shape=[
            jax.ShapeDtypeStruct((tokens, channels), jnp.float32),
            jax.ShapeDtypeStruct((NS, channels), jnp.float32),
            jax.ShapeDtypeStruct((blocks, NS, channels), half),
            jax.ShapeDtypeStruct((tokens + 1, NS, channels), half),
        ]
        + [jax.ShapeDtypeStruct((2,) * stages + shard.shape, shard.dtype) for shard in shards],
        scratch_shapes=[
            pltpu.VMEM((tokens, NS, LANES), jnp.float32),
            pltpu.VMEM((tokens, NS, LANES), jnp.float32),
            pltpu.VMEM((2, span, NS, channels), half),
            pltpu.VMEM((1, NS, channels), half),
            pltpu.VMEM((NS, channels), jnp.float32),
            pltpu.VMEM((2, NS, channels), half),
            pltpu.VMEM((blocks, NS, channels), half),
            pltpu.VMEM((blocks, NS, channels), half),
            pltpu.SemaphoreType.DMA((2,)),
            pltpu.SemaphoreType.DMA,
            pltpu.SemaphoreType.DMA((4, blocks)),
            pltpu.SemaphoreType.DMA((len(streams), stages)),
            pltpu.SemaphoreType.DMA((len(streams), stages)),
            pltpu.SemaphoreType.DMA((len(streams),)),
        ],
        compiler_params=pltpu.CompilerParams(
            collective_id=identity, has_side_effects=True, vmem_limit_bytes=48 * 1024 * 1024
        ),
        cost_estimate=cost(tokens, channels, 9),
        name="scan_forward",
    )(step, push, b_turned, c_turned, rates, *shards)
    return y, start, products, kept, [whole.reshape((-1,) + whole.shape[stages + 1 :]) for whole in wholes]


def backward_kernel(places, streams, width, moved, *refs):
    step_ref, push_ref, grad_ref, bt_ref, ct_ref, rate_ref, product_ref = refs[:7]
    parts = refs[7:9]
    kept_ref = refs[9]
    leaving = refs[10 : 10 + moved]
    outs = refs[10 + moved :]
    along_ref, slope_ref, gb_ref, gc_ref, ga_ref = outs[:5]
    totals = outs[5:7]
    arriving = outs[7 : 7 + moved]
    scratch = outs[7 + moved :]
    landing = scratch[: len(streams) * len(places)]
    (wide_b, wide_c, part_b, part_c, kept_buf, flow_ref, message, inflows,
     kept_sems, share_sems, moved_sems, send_sems, recv_sems) = scratch[len(streams) * len(places) :]
    blocks = lax.axis_size("ctx")
    position = lax.axis_index("ctx")
    span = kept_buf.shape[1] - 1
    steps = step_ref.shape[0] // span
    flow = ReduceFlow(places, streams, parts, totals, landing, send_sems, recv_sems)

    def kept_copy(number, slot):
        return pltpu.make_async_copy(
            kept_ref.at[pl.ds(number * span, span + 1)], kept_buf.at[slot], kept_sems.at[slot]
        )

    for order in range(min(2, steps)):
        kept_copy(steps - 1 - order, order).start()
    meet([place for place in places if place[0] == "exp"], *row_peers())
    flow.start()
    spread_columns(bt_ref, wide_b)
    spread_columns(ct_ref, wide_c)
    inflow_pass(width, step_ref, grad_ref, wide_c, rate_ref, flow_ref, lambda group: None)
    message[...] = flow_ref[...].astype(jnp.bfloat16)
    copies = share(message, inflows, share_sems.at[0], share_sems.at[1])
    for copy in copies:
        copy.wait_recv()
    end = jnp.zeros(flow_ref.shape, jnp.float32)
    for index in reversed(range(blocks)):
        folded = inflows[index].astype(jnp.float32) + product_ref[index].astype(jnp.float32) * end
        end = jnp.where(index > position, folded, end)
    flow_ref[...] = end
    flow.advance(0)
    last = ("ctx", blocks.bit_length() - 2)
    moves = []
    for k in range(moved):
        moves.append(
            pltpu.make_async_remote_copy(
                src_ref=leaving[k],
                dst_ref=arriving[k],
                send_sem=moved_sems.at[0, k],
                recv_sem=moved_sems.at[1, k],
                device_id=partner(last),
                device_id_type=MESH,
            )
        )
        moves[-1].start()

    def hook(order):
        @pl.when(order == 2)
        def _():
            flow.advance(1)

        @pl.when(order == 4)
        def _():
            flow.advance(2)

    adjoint_pass(width, step_ref, push_ref, grad_ref, wide_b, wide_c, rate_ref, flow_ref, kept_buf, kept_copy,
                 along_ref, slope_ref, gb_ref, gc_ref, ga_ref, part_b, part_c, hook)
    for stage in range(3, len(places)):
        flow.advance(stage)
    flow.finish()
    for copy in copies:
        copy.wait_send()
    for move in moves:
        move.wait()


def scan_backward(sizes, step, push, grad, b_turned, c_turned, rates, products, parts, kept, leaving, identity, span=64):
    places = bit_positions(sizes)
    stages = len(places)
    streams = streams_of(places, parts, False)
    divided = [part.reshape((2,) * stages + (-1, part.shape[1])) for part in parts]
    tokens, channels = step.shape
    blocks = sizes[0][1]
    inside = pl.BlockSpec(memory_space=pltpu.VMEM)
    anywhere = pl.BlockSpec(memory_space=pl.ANY)
    half = jnp.bfloat16
    moved = len(leaving)
    row_sums = jax.ShapeDtypeStruct((tokens // span, UNROLL, span * NS), jnp.float32)
    out = pl.pallas_call(
        functools.partial(backward_kernel, places, streams, pick(channels), moved),
        in_specs=[inside] * 9 + [anywhere] * (1 + moved),
        out_specs=[inside] * 7 + [anywhere] * moved,
        out_shape=[jax.ShapeDtypeStruct((tokens, channels), jnp.float32)] * 2
        + [row_sums, row_sums, jax.ShapeDtypeStruct((NS, channels), jnp.float32)]
        + [jax.ShapeDtypeStruct(block.shape[-2:], jnp.float32) for block in divided]
        + [jax.ShapeDtypeStruct(value.shape, value.dtype) for value in leaving],
        scratch_shapes=landing_of(places, streams, divided)
        + [
            pltpu.VMEM((tokens, NS, LANES), jnp.float32),
            pltpu.VMEM((tokens, NS, LANES), jnp.float32),
            pltpu.VMEM((span, NS, LANES), jnp.float32),
            pltpu.VMEM((span, NS, LANES), jnp.float32),
            pltpu.VMEM((2, span + 1, NS, channels), half),
            pltpu.VMEM((NS, channels), jnp.float32),
            pltpu.VMEM((NS, channels), half),
            pltpu.VMEM((blocks, NS, channels), half),
            pltpu.SemaphoreType.DMA((2,)),
            pltpu.SemaphoreType.DMA((2, blocks)),
            pltpu.SemaphoreType.DMA((2, max(1, moved))),
            pltpu.SemaphoreType.DMA((len(streams), stages)),
            pltpu.SemaphoreType.DMA((len(streams), stages)),
        ],
        compiler_params=pltpu.CompilerParams(
            collective_id=identity, has_side_effects=True, vmem_limit_bytes=56 * 1024 * 1024
        ),
        cost_estimate=cost(tokens, channels, 15),
        name="scan_backward",
    )(step, push, grad, b_turned, c_turned, rates, products, *divided, kept, *leaving)
    along, slope, wide_b, wide_c, grad_a = out[:5]
    grad_bs, grad_cs = [values[:, 0].reshape(tokens, NS) for values in (wide_b, wide_c)]
    return along, slope, grad_bs, grad_cs, grad_a, out[5:7], list(out[7:])


def expert_kernel(slices, *refs):
    tokens_ref, grads_ref, column_ref, row_ref = refs[:4]
    weights_in, weights_out = refs[4 : 4 + slices], refs[4 + slices : 4 + 2 * slices]
    outs = refs[4 + 2 * slices :]
    picked_ref, back_ref = outs[:2]
    sums_in, sums_out = outs[2 : 2 + slices], outs[2 + slices : 2 + 2 * slices]
    (sent, got, answer, returned, w_in, w_out, hidden, total, active, slope, inner,
     send_sems, recv_sems, weight_sems, sum_sems) = outs[2 + 2 * slices :]
    experts, room, width = sent.shape[1:]
    places = experts * room
    me = lax.axis_index("exp")
    here = lax.axis_index("ctx")

    loads = []
    for s in range(slices):
        loads.append(pltpu.make_async_copy(weights_in[s], w_in.at[s], weight_sems.at[0, s]))
        loads.append(pltpu.make_async_copy(weights_out[s], w_out.at[s], weight_sems.at[1, s]))
    for load in loads:
        load.start()

    barrier = pltpu.get_barrier_semaphore()
    for step in range(1, experts):
        pl.semaphore_signal(barrier, inc=1, device_id=(here, lax.rem(me + step, experts)), device_id_type=MESH)
    pl.semaphore_wait(barrier, experts - 1)

    def exchange(source, target, kind):
        copies = []
        for step in range(1, experts):
            peer = lax.rem(me + step, experts)
            copy = pltpu.make_async_remote_copy(
                src_ref=source.at[peer],
                dst_ref=target.at[me],
                send_sem=send_sems.at[kind, step],
                recv_sem=recv_sems.at[kind, step],
                device_id=(here, peer),
                device_id_type=MESH,
            )
            copy.start()
            copies.append(copy)
        target[me] = source[me]
        return copies

    def arrive(copies):
        for copy in copies:
            copy.wait_recv()

    chooser = (lax.broadcasted_iota(jnp.int32, (places, row_ref.shape[1]), 0) == row_ref[...]).astype(jnp.float32).astype(jnp.bfloat16)
    sent[0] = dot(chooser, tokens_ref[...]).astype(jnp.bfloat16).reshape(experts, room, width)
    first = exchange(sent.at[0], got.at[0], 0)
    sent[1] = dot(chooser, grads_ref[...]).astype(jnp.bfloat16).reshape(experts, room, width)
    second = exchange(sent.at[1], got.at[1], 1)

    for load in loads:
        load.wait()
    arrive(first)
    rows = got[0].reshape(places, width)
    for s in range(slices):
        hidden[...] = dot(rows, w_in[s])

        def curve(index, unused):
            at = pl.ds(pl.multiple_of(index * ROWS_AT_ONCE, ROWS_AT_ONCE), ROWS_AT_ONCE)
            value = hidden[at, :]
            bell = 0.5 + 0.5 * lax.erf(value * 0.7071067811865476)
            active[s, at, :] = (value * bell).astype(jnp.bfloat16)
            slope[s, at, :] = bell + value * (jnp.exp(-0.5 * value * value) * 0.3989422804014327)
            return unused

        lax.fori_loop(0, places // ROWS_AT_ONCE, curve, 0)
        product = dot(active[s], w_out[s])
        total[...] = product if s == 0 else total[...] + product
    answer[0] = total[...].astype(jnp.bfloat16).reshape(experts, room, width)
    third = exchange(answer.at[0], returned.at[0], 2)

    arrive(second)
    pulled = got[1].reshape(places, width)
    for s in range(slices):
        inner[s] = (contract(pulled, w_out[s], 1, 1) * slope[s]).astype(jnp.bfloat16)
        product = contract(inner[s], w_in[s], 1, 1)
        total[...] = product if s == 0 else total[...] + product
    answer[1] = total[...].astype(jnp.bfloat16).reshape(experts, room, width)
    fourth = exchange(answer.at[1], returned.at[1], 3)

    stores = []
    for s in range(slices):
        w_out[s] = contract(active[s], pulled, 0, 0).astype(jnp.bfloat16)
        stores.append(pltpu.make_async_copy(w_out.at[s], sums_out[s], sum_sems.at[0, s]))
        stores[-1].start()
        w_in[s] = contract(rows, inner[s], 0, 0).astype(jnp.bfloat16)
        stores.append(pltpu.make_async_copy(w_in.at[s], sums_in[s], sum_sems.at[1, s]))
        stores[-1].start()

    finder = (lax.broadcasted_iota(jnp.int32, (column_ref.shape[0], places), 1) == column_ref[...]).astype(jnp.float32).astype(jnp.bfloat16)
    arrive(third)
    picked_ref[...] = dot(finder, returned[0].reshape(places, width)).astype(jnp.bfloat16)
    arrive(fourth)
    back_ref[...] = dot(finder, returned[1].reshape(places, width)).astype(jnp.bfloat16)
    for store in stores:
        store.wait()
    for copies in (first, second, third, fourth):
        for copy in copies:
            copy.wait_send()


def run_experts(rows, grads, target, weights_in, weights_out, experts, room, identity):
    slices = len(weights_in)
    tokens, width = rows.shape
    inner_width = weights_in[0].shape[1]
    places = experts * room
    inside = pl.BlockSpec(memory_space=pltpu.VMEM)
    anywhere = pl.BlockSpec(memory_space=pl.ANY)
    half = jnp.bfloat16
    out = pl.pallas_call(
        functools.partial(expert_kernel, slices),
        in_specs=[inside] * 4 + [anywhere] * (2 * slices),
        out_specs=[inside] * 2 + [anywhere] * (2 * slices),
        out_shape=[jax.ShapeDtypeStruct(rows.shape, half)] * 2
        + [jax.ShapeDtypeStruct(weight.shape, half) for weight in weights_in + weights_out],
        scratch_shapes=[pltpu.VMEM((2, experts, room, width), half)] * 4
        + [
            pltpu.VMEM((slices, width, inner_width), half),
            pltpu.VMEM((slices, inner_width, width), half),
            pltpu.VMEM((places, inner_width), jnp.float32),
            pltpu.VMEM((places, width), jnp.float32),
            pltpu.VMEM((slices, places, inner_width), half),
            pltpu.VMEM((slices, places, inner_width), jnp.float32),
            pltpu.VMEM((slices, places, inner_width), half),
            pltpu.SemaphoreType.DMA((4, experts)),
            pltpu.SemaphoreType.DMA((4, experts)),
            pltpu.SemaphoreType.DMA((2, slices)),
            pltpu.SemaphoreType.DMA((2, slices)),
        ],
        compiler_params=pltpu.CompilerParams(
            collective_id=identity, has_side_effects=True, vmem_limit_bytes=52 * 1024 * 1024
        ),
        name="run_experts",
    )(rows, grads, target[:, None], target[None, :], *weights_in, *weights_out)
    return out[0], out[1], list(out[2 : 2 + slices]), list(out[2 + slices :])


def flipped(value, level):
    count = lax.axis_size("ctx")
    return lax.ppermute(value, "ctx", [(source, source ^ (1 << level)) for source in range(count)])


def spread_slices(own):
    levels = lax.axis_size("ctx").bit_length() - 1
    slices = {0: own}
    for level in reversed(range(levels)):
        for offset in sorted(slices):
            slices[offset + (1 << level)] = flipped(slices[offset], level)
    return [slices[offset] for offset in sorted(slices)]


def collect_slices(sums, levels):
    for level in levels:
        step = 1 << level
        kept = {}
        for offset in range(0, len(sums), 2 * step):
            arrived = flipped(sums[offset + step].astype(jnp.bfloat16), level)
            kept[offset] = sums[offset].astype(jnp.float32) + arrived.astype(jnp.float32)
        sums = [kept.get(offset) for offset in range(len(sums))]
    return sums


def body(
    inputs,
    segments,
    routes,
    cotangent,
    norm_gain,
    in_proj,
    conv_taps,
    conv_bias,
    x_proj,
    dt_proj,
    dt_bias,
    log_decay,
    skip_gain,
    out_proj,
    moe_gain,
    router,
    expert_in,
    expert_out,
):
    experts = router.shape[1]
    half_rows = norm_gain.shape[0]
    columns = (
        x_proj,
        dt_proj.T,
        conv_taps,
        conv_bias[:, None],
        dt_bias[:, None],
        log_decay,
        skip_gain[:, None],
        jnp.concatenate([norm_gain, moe_gain])[:, None],
        router.reshape(2 * half_rows, experts // 2),
    )
    widths = [part.shape[1] for part in columns]
    ends = [sum(widths[: k + 1]) for k in range(len(widths))]
    sizes = [(name, lax.axis_size(name)) for name in ("ctx", "exp")]
    tail_ids = segments[0, -EDGE:, None].astype(jnp.bfloat16)
    edge = jnp.concatenate([inputs[0, -EDGE:], jnp.broadcast_to(tail_ids, (EDGE, LANES))], axis=1)
    (full_conv, full_small), prior = gather_all(
        sizes, (in_proj[:, :DI], jnp.concatenate(columns, axis=1)), edge, 0
    )
    later_in, later_out, full_small = lax.optimization_barrier((expert_in[0], expert_out[0], full_small))
    weights_in = spread_slices(later_in)
    weights_out = spread_slices(later_out)
    full_xproj, full_dt, full_taps, full_bias, full_dtbias, full_decay, full_skip, gains, full_router = [
        full_small[:, end - width : end] for end, width in zip(ends, widths)
    ]
    full_dt = full_dt.T
    full_bias, full_dtbias, full_skip = full_bias[:, 0], full_dtbias[:, 0], full_skip[:, 0]
    gains = gains.reshape(-1, 2, half_rows)
    full_norm, full_moe = gains[:, 0].reshape(-1), gains[:, 1].reshape(-1)
    full_router = full_router.reshape(-1, experts)
    tokens_here = inputs.shape[1]
    capacity = 5 * tokens_here // (4 * experts)
    flat_in = inputs[0].astype(jnp.float32)
    seg_row = segments[0]
    position = lax.axis_index("ctx")
    norm_one_value, norm_one_pull = jax.vjp(rms_scale, flat_in, full_norm.astype(jnp.float32))
    normed_one = norm_one_value.astype(jnp.bfloat16)
    conv_in = dot(normed_one, full_conv).astype(jnp.bfloat16)
    edge_one = rms_scale(prior[:, :D].astype(jnp.float32), full_norm.astype(jnp.float32)).astype(jnp.bfloat16)
    edge_rows = dot(edge_one, full_conv)[EDGE - (KC - 1) :].astype(jnp.bfloat16)
    prior_ids = jnp.where(position > 0, prior[EDGE - (KC - 1) :, D].astype(jnp.int32), -1)
    ext_ids = jnp.concatenate([prior_ids, seg_row])
    ext_rows = jnp.concatenate([edge_rows, conv_in], axis=0).astype(jnp.float32)
    conv_out, conv_pull = jax.vjp(
        lambda rows_in, taps_in, bias_in: conv_local(rows_in, taps_in, bias_in, ext_ids),
        ext_rows,
        full_taps.astype(jnp.float32),
        full_bias.astype(jnp.float32),
    )
    silu_value, silu_pull = jax.vjp(jax.nn.silu, conv_out)
    xs_val = silu_value.astype(jnp.bfloat16)
    xs_wide = xs_val.astype(jnp.float32)
    projected = jnp.dot(xs_val, full_xproj, preferred_element_type=jnp.float32)
    delta_low = projected[:, :R].astype(jnp.bfloat16)
    b_rows = projected[:, R : R + NS]
    c_rows = projected[:, R + NS :]
    dt_pre = jnp.dot(delta_low, full_dt, preferred_element_type=jnp.float32) + full_dtbias.astype(
        jnp.float32
    )
    step_size = jax.nn.softplus(dt_pre)
    a_swap = -jnp.exp(full_decay.astype(jnp.float32)).T
    earlier = jnp.concatenate([prior_ids[KC - 2 :], seg_row[:-1]])
    keep_mask = (earlier == seg_row).astype(jnp.float32)
    masked_step = jnp.where(keep_mask[:, None] > 0, step_size, 1e30)
    push = step_size * xs_wide
    rates = a_swap * LOG2E
    b_turned, c_turned = b_rows.T, c_rows.T
    scan_rows, start_state, products, kept, (full_gate, full_out) = scan_forward(
        sizes, masked_step, push, b_turned, c_turned, rates, (in_proj[:, DI:], out_proj), 3
    )
    gate_z = dot(normed_one, full_gate)
    skip_wide = full_skip.astype(jnp.float32)
    scanned_y = scan_rows + skip_wide * xs_wide
    gated_wide, gated_pull = jax.vjp(
        lambda scan_in, gate_in: scan_in * jax.nn.silu(gate_in), scanned_y, gate_z
    )
    gated = gated_wide.astype(jnp.bfloat16)
    mixed = jnp.dot(gated, full_out, preferred_element_type=jnp.float32)
    residual = flat_in + mixed
    norm_two_value, norm_two_pull = jax.vjp(rms_scale, residual, full_moe.astype(jnp.float32))
    normed_two = norm_two_value.astype(jnp.bfloat16)
    logits = jnp.dot(normed_two, full_router, preferred_element_type=jnp.float32)
    probability = jax.nn.softmax(logits, axis=-1)
    route_ids = routes[0, :, 0]
    one_hot = route_ids[:, None] == jnp.arange(experts, dtype=jnp.int32)[None, :]
    one_float = one_hot.astype(jnp.float32)
    gate_val = jnp.sum(probability * one_float, axis=1)
    running = jnp.cumsum(one_hot.astype(jnp.int32), axis=0)
    slot_index = jnp.sum(running * one_hot.astype(jnp.int32), axis=1) - 1
    room = -(-capacity // 16) * 16
    target = route_ids * room + slot_index
    grad_out = cotangent[0].astype(jnp.float32)
    grad_pick = (grad_out * gate_val[:, None]).astype(jnp.bfloat16)
    picked, grad_from_experts, grad_expert_in, grad_expert_out = run_experts(
        normed_two, grad_pick, target, weights_in, weights_out, experts, room, 2
    )
    picked = picked.astype(jnp.float32)
    grad_from_experts = grad_from_experts.astype(jnp.float32)
    outcome = residual + gate_val[:, None] * picked
    out_block = outcome.astype(jnp.bfloat16)[None]
    grad_gate = jnp.sum(grad_out * picked, axis=1)
    levels = lax.axis_size("ctx").bit_length() - 1
    grad_expert_in = collect_slices(grad_expert_in, range(1))
    grad_expert_out = collect_slices(grad_expert_out, range(1))
    grad_probs = grad_gate[:, None] * one_float
    grad_logits = (
        probability * (grad_probs - jnp.sum(grad_probs * probability, axis=1, keepdims=True))
    ).astype(jnp.bfloat16)
    grad_router = jnp.dot(normed_two.T, grad_logits, preferred_element_type=jnp.float32)
    grad_normed_two = grad_from_experts + jnp.dot(
        grad_logits, full_router.T, preferred_element_type=jnp.float32
    )
    grad_resid_norm, grad_moe_gain = norm_two_pull(grad_normed_two)
    grad_resid = grad_out + grad_resid_norm
    grad_mixed = grad_resid.astype(jnp.bfloat16)
    grad_gated = jnp.dot(grad_mixed, full_out.T, preferred_element_type=jnp.float32)
    grad_out_proj = jnp.dot(gated.T, grad_mixed, preferred_element_type=jnp.float32)
    grad_y, grad_z = gated_pull(grad_gated)
    grad_skip = jnp.sum(grad_y * xs_wide, axis=0)
    grad_z = grad_z.astype(jnp.bfloat16)
    grad_y, grad_expert_in, grad_expert_out = lax.optimization_barrier(
        (grad_y, grad_expert_in, grad_expert_out)
    )
    grad_expert_in = collect_slices(grad_expert_in, range(1, levels - 1))
    grad_expert_out = collect_slices(grad_expert_out, range(1, levels - 1))
    last = 1 << (levels - 1)
    leaving = [values[last].astype(jnp.bfloat16) for values in (grad_expert_in, grad_expert_out)]
    along_b, slope, grad_bs, grad_cs, grad_a, (own_gate, own_out), arrived = scan_backward(
        sizes,
        masked_step,
        push,
        grad_y,
        b_turned,
        c_turned,
        rates,
        products,
        (dot(normed_one.T, grad_z).astype(jnp.bfloat16), grad_out_proj.astype(jnp.bfloat16)),
        kept,
        leaving,
        4,
    )
    grad_w_in, grad_w_out = [
        values[0].astype(jnp.float32) + other.astype(jnp.float32)
        for values, other in zip((grad_expert_in, grad_expert_out), arrived)
    ]
    grad_step_all = along_b * xs_wide + slope * (1.0 / LOG2E)
    grad_xss = along_b * step_size
    grad_log_decay = (grad_a * a_swap).T
    soft_slope = jax.nn.sigmoid(dt_pre)
    grad_pre_wide = grad_step_all * soft_slope
    grad_dt_bias = jnp.sum(grad_pre_wide, axis=0)
    grad_dt_pre = grad_pre_wide.astype(jnp.bfloat16)
    grad_dt_proj = jnp.dot(delta_low.T, grad_dt_pre, preferred_element_type=jnp.float32)
    grad_delta = jnp.dot(grad_dt_pre, full_dt.T, preferred_element_type=jnp.float32)
    grad_projected = jnp.concatenate(
        [grad_delta, grad_bs, grad_cs], axis=1
    ).astype(jnp.bfloat16)
    grad_x_proj = jnp.dot(xs_val.T, grad_projected, preferred_element_type=jnp.float32)
    grad_xs_total = (
        skip_wide * grad_y
        + grad_xss
        + jnp.dot(grad_projected, full_xproj.T, preferred_element_type=jnp.float32)
    )
    grad_conv = silu_pull(grad_xs_total)[0]
    grad_ext, grad_taps, grad_cbias = conv_pull(grad_conv)
    from_next = shifted(grad_ext[: KC - 1], "ctx", -1)
    grad_conv_in = grad_ext[KC - 1 :] + jnp.concatenate(
        [jnp.zeros((tokens_here - (KC - 1), DI), jnp.float32), from_next], axis=0
    )
    grad_conv_in = grad_conv_in.astype(jnp.bfloat16)
    grad_normed_one = dot(grad_conv_in, full_conv.T) + dot(grad_z, full_gate.T)
    grad_inputs_norm, grad_norm_gain = norm_one_pull(grad_normed_one)
    grad_inputs = grad_resid + grad_inputs_norm
    sums = (
        grad_x_proj,
        grad_dt_proj.T,
        grad_taps,
        grad_cbias[:, None],
        grad_dt_bias[:, None],
        grad_log_decay,
        grad_skip[:, None],
        jnp.stack(
            [grad_norm_gain.reshape(-1, half_rows), grad_moe_gain.reshape(-1, half_rows)], axis=1
        ).reshape(-1, 1),
        grad_router.reshape(-1, experts // 2),
    )

    own_conv, own_small = reduce_all(
        sizes,
        (
            dot(normed_one.T, grad_conv_in).astype(jnp.bfloat16),
            jnp.concatenate(sums, axis=1).astype(jnp.bfloat16),
        ),
        1,
    )
    own_x, own_dt, own_taps, own_bias, own_dtbias, own_decay, own_skip, own_gains, own_router = [
        own_small[:, end - width : end] for end, width in zip(ends, widths)
    ]
    return (
        out_block,
        grad_inputs[None],
        own_gains[:half_rows, 0],
        jnp.concatenate([own_conv, own_gate], axis=1),
        own_taps,
        own_bias[:, 0],
        own_x,
        own_dt.T,
        own_dtbias[:, 0],
        own_decay,
        own_skip[:, 0],
        own_out,
        own_gains[half_rows:, 0],
        own_router.reshape(half_rows, experts),
        grad_w_in[None],
        grad_w_out[None],
    )


def solution(mesh):
    placed = (
        P("exp", "ctx", None),
        P("exp", "ctx"),
        P("exp", "ctx", None),
        P("exp", "ctx", None),
        P(("ctx", "exp")),
        P(("ctx", "exp"), None),
        P(("ctx", "exp"), None),
        P(("ctx", "exp")),
        P(("ctx", "exp"), None),
        P(None, ("ctx", "exp")),
        P(("ctx", "exp")),
        P(("ctx", "exp"), None),
        P(("ctx", "exp")),
        P(("ctx", "exp"), None),
        P(("ctx", "exp")),
        P(("ctx", "exp"), None),
        P("exp", None, "ctx"),
        P("exp", "ctx", None),
    )
    return jax.shard_map(
        body,
        mesh=mesh,
        in_specs=placed,
        out_specs=(
            P("exp", "ctx", None),
            P("exp", "ctx", None),
            P(("ctx", "exp")),
            P(("ctx", "exp"), None),
            P(("ctx", "exp"), None),
            P(("ctx", "exp")),
            P(("ctx", "exp"), None),
            P(None, ("ctx", "exp")),
            P(("ctx", "exp")),
            P(("ctx", "exp"), None),
            P(("ctx", "exp")),
            P(("ctx", "exp"), None),
            P(("ctx", "exp")),
            P(("ctx", "exp"), None),
            P("exp", None, "ctx"),
            P("exp", "ctx", None),
        ),
        check_vma=False,
    )
```

profile of v0, /device:TPU:0, one launch (start us, length us, event | category | flops | bytes accessed | tf_op | source)
XLA Modules:
  0.0 434.0 jit_solution(4217521743124327452)
XLA Ops:
  8.4 1.6 fusion.91
  10.7 1.4 concatenate.58.refs_1_
  12.1 31.7 %gather_all.1 = (bf16[2,2,2,2,2,24,1536]{6,5,4,3,2,1,0:T(8,128)(2,1)}, bf16[2,2,2,2,2,48,156]{6,5,4,3,2,1,0:T(8,128)(2,1)}, bf16[16,896]{1,0:T(8,128)(2,1)}) custom-call(bf16[24,1536]{1,0:T(8,128)(2,1)} %get-tuple-element.195.refs_0_, bf16[48,156]{1,0:T(8,128)(2,1)} %concatenate.58.refs_1_, bf16[16,896]{1,0:T(8,128)(2,1)} %pad_maximum_fusion.2.refs_2_), custom_call_target="tpu_custom_call" | custom-call | tf_op jit(solution)/shard_map/gather_all/pallas_call | solution.py:189
  44.9 1.2 collective-permute-start.4
  46.2 1.3 fusion.22
  47.5 1.3 slice_reduce_fusion.11
  48.7 1.3 slice_reduce_fusion.4
  50.1 2.8 convert_reduce_fusion
  56.5 2.3 fusion.55
  58.8 2.2 convolution_convert_fusion.3
  61.9 1.5 slice_reduce_fusion.3
  64.9 3.2 multiply_convert_fusion.1
  68.7 4.8 %convert_multiply_fusion.3 = (f32[384,1536]{1,0:T(8,128)}, f32[384,1536]{1,0:T(8,128)}, f32[384,1536]{1,0:T(8,128)}) fusion(bf16[384,1536]{1,0:T(8,128)(2,1)S(1)} %get-tuple-element.181, pred[384]{0:T(512)(128)(4,1)S(1)} %get-tuple-element.205, f32[1536]{0:T(1024)S(1)} %copy-done.42, bf16[1536,156]{1,0:T(8,128)(2,1)S(1)} %bitcast.129, f32[384,80]{0,1:T(8,128)S(1)} %fusion.38), kind=kOutput, calls=%fused_computation.4 | convolution fusion | flops 62521344 | bytes 8696320 | tf_op jit(solution)/shard_map/dot_general | solution.py:1030
  73.6 55.5 %scan_forward.1 = (f32[384,1536]{1,0:T(8,128)S(1)}, f32[16,1536]{1,0:T(8,128)}, bf16[4,16,1536]{2,1,0:T(8,128)(2,1)S(1)}, bf16[385,16,1536]{2,1,0:T(8,128)(2,1)}...) custom-call(f32[384,1536]{1,0:T(8,128)} %get-tuple-element.189.refs_0_, ...), custom_call_target="tpu_custom_call" | custom-call | flops 84934656 | bytes 84934656 | tf_op jit(solution)/shard_map/scan_forward/pallas_call | solution.py:629
  129.2 2.7 multiply_convert_fusion
  131.9 1.0 copy-done.62
  132.9 1.2 multiply_reduce_fusion.6
  136.3 1.5 collective-permute-done.2.refs_7_
  137.9 1.0 copy-done.30
  139.1 69.7 %run_experts.1 = (bf16[384,768]{1,0:T(8,128)(2,1)S(1)}, bf16[384,768]{1,0:T(8,128)(2,1)S(1)}, bf16[768,768]{1,0:T(8,128)(2,1)}, bf16[768,768]{1,0:T(8,128)(2,1)}...) custom-call(bf16[384,768]{1,0:T(8,128)(2,1)S(1)} %multiply_convert_f, ...), custom_call_target="tpu_custom_call" | custom-call | tf_op jit(solution)/shard_map/run_experts/pallas_call | solution.py:899
  209.8 1.3 convert_add_fusion.4
  211.6 1.1 copy-done.65
  212.8 4.2 fusion.8
  218.4 1.5 concatenate.79
  220.9 3.5 fusion.94
  224.4 2.9 convolution_convert_fusion.1
  227.3 2.9 convolution_convert_fusion.2
  230.2 2.7 convert_add_fusion.2.refs_10_
  233.0 1.7 convert_add_fusion.3
  234.7 1.7 convert_add_fusion.1
  236.4 1.4 convert_add_fusion.refs_11_
  237.7 113.5 %scan_backward.1 = (f32[384,1536]{1,0:T(8,128)}, f32[384,1536]{1,0:T(8,128)}, f32[6,8,1024]{2,1,0:T(8,128)}, f32[6,8,1024]{2,1,0:T(8,128)}, f32[16,1536]{1,0:T(8...) custom-call(f32[384,1536]{1,0:T(8,128)} %get-tuple-element.189.refs_0_, ...), custom_call_target="tpu_custom_call" | custom-call | flops 141557760 | bytes 141557760 | tf_op jit(solution)/shard_map/scan_backward/pallas_call | solution.py:753
  351.3 3.2 fusion.88
  354.6 1.0 convolution_convert_fusion.5
  356.2 1.1 fusion.57
  357.7 1.6 convolution_convert_fusion.4
  359.4 7.8 %multiply_reduce_fusion.3 = (f32[1536]{0:T(1024)S(1)}, f32[1536]{0:T(1024)S(1)}, f32[1536]{0:T(1024)S(1)}, f32[1536]{0:T(1024)S(1)}, bf16[1536]{0:T(1024)(128)(2...) fusion(f32[387,1536]{1,0:T(8,128)S(1)} %copy-done.6, ...), kind=kOutput, calls=%fused_computation.30 | convolution fusion | flops 115192320 | bytes 28837376 | tf_op jit(solution)/shard_map/dot_general | solution.py:1135
  367.3 1.1 pad_add_fusion
  368.4 2.4 fusion.54
  370.9 1.3 collective-permute-start.10
  372.2 2.8 add_bitcast_fusion
  378.8 1.5 concatenate.78
  380.3 1.5 concatenate.77
  381.8 4.3 fusion.19
  386.5 4.6 %concatenate.75.refs_1_ = bf16[2,2,2,2,2,48,156]{6,5,4,3,2,1,0:T(8,128)(2,1)S(1)} concatenate(bf16[2,2,2,2,2,48,80]{6,5,4,3,2,1,0:T(8,128)(2,1)} %bitcast.137, bf16[2,2,2,2,2,48,48]{6,5,4,3,2,1,0:T(8,128)(2,1)} %bitcast.138, bf16[2,2,2,2,2,48,4]{6,5,4,3,2,1,0:T(8,128)(2,1)} %bitcast.140, bf16[2,2,2,2,2,48,1]{6,5,4,3,2,1,0:T(8,128)(2,1)} %concatenate.77, ...), dimensions={6} | concatenate | bytes 958464 | tf_op jit(solution)/shard_map/concatenate | solution.py:1165
  391.1 3.2 convolution_convert_fusion
  394.3 30.2 %reduce_all.1 = (f32[24,1536]{1,0:T(8,128)S(1)}, f32[48,156]{1,0:T(8,128)S(1)}) custom-call(bf16[2,2,2,2,2,24,1536]{6,5,4,3,2,1,0:T(8,128)(2,1)S(1)} %bitcast.121, bf16[2,2,2,2,2,48,156]{6,5,4,3,2,1,0:T(8,128)(2,1)S(1)} %concatenate.75.refs_1_), custom_call_target="tpu_custom_call" | custom-call | tf_op jit(solution)/shard_map/reduce_all/pallas_call | solution.py:292
  429.5 2.6 fusion.27
  (239 shorter events, 34.1 us)
Async XLA Ops:
  43.9 9.0 %copy-start.9 = (bf16[2,2,2,2,2,48,156]{6,5,4,3,2,1,0:T(8,128)(2,1)S(1)}, bf16[2,2,2,2,2,48,156]{6,5,4,3,2,1,0:T(8,128)(2,1)}, u32[]{:S(2)}) copy-start(bf16[2,2,2,2,2,48,156]{6,5,4,3,2,1,0:T(8,128)(2,1)} %get-tuple-element.54) | copy-start | bytes 1437700
  43.9 90.3 %collective-permute-start.1 = (bf16[768,768]{1,0:T(8,128)(2,1)}, bf16[768,768]{1,0:T(8,128)(2,1)}, u32[]{:S(2)}, u32[]{:S(2)}) collective-permute-start(bf16[768,768]{1,0:T(8,128)(2,1)} %bitcast.141), channel_id=1, source_target_pairs={{0,16},{8,24},{16,0},{24,8},{1,17},{9,25},{17,1},{25,9},{2,18},{10... | collective-permute-start | bytes 3538952 | tf_op jit(solution)/shard_map/ppermute | solution.py:929
  44.8 91.5 %collective-permute-start = (bf16[768,768]{1,0:T(8,128)(2,1)}, bf16[768,768]{1,0:T(8,128)(2,1)}, u32[]{:S(2)}, u32[]{:S(2)}) collective-permute-start(bf16[768,768]{1,0:T(8,128)(2,1)} %bitcast.142), channel_id=1, source_target_pairs={{0,8},{8,0},{16,24},{24,16},{1,9},{9,1},{17,25},{25,17},{2,10},{10... | collective-permute-start | bytes 3538952 | tf_op jit(solution)/shard_map/ppermute | solution.py:929
  44.9 89.7 %collective-permute-start.4 = (bf16[768,768]{1,0:T(8,128)(2,1)}, bf16[768,768]{1,0:T(8,128)(2,1)}, u32[]{:S(2)}, u32[]{:S(2)}) collective-permute-start(bf16[768,768]{1,0:T(8,128)(2,1)} %bitcast.144), channel_id=1, source_target_pairs={{0,16},{8,24},{16,0},{24,8},{1,17},{9,25},{17,1},{25,9},{2,18},{10... | collective-permute-start | bytes 3538952 | tf_op jit(solution)/shard_map/ppermute | solution.py:929
  46.1 90.2 %collective-permute-start.3 = (bf16[768,768]{1,0:T(8,128)(2,1)}, bf16[768,768]{1,0:T(8,128)(2,1)}, u32[]{:S(2)}, u32[]{:S(2)}) collective-permute-start(bf16[768,768]{1,0:T(8,128)(2,1)} %bitcast.145), channel_id=1, source_target_pairs={{0,8},{8,0},{16,24},{24,16},{1,9},{9,1},{17,25},{25,17},{2,10},{10... | collective-permute-start | bytes 3538952 | tf_op jit(solution)/shard_map/ppermute | solution.py:929
  48.7 4.6 %copy-start.57 = (s32[1,384]{1,0:T(1,128)S(1)}, s32[1,384]{1,0:T(1,128)}, u32[]{:S(2)}) copy-start(s32[1,384]{1,0:T(1,128)} %param.19) | copy-start | bytes 4612
  48.7 4.6 %copy-start.46 = (s32[1,384,1]{1,2,0:T(1,128)S(1)}, s32[1,384,1]{1,2,0:T(1,128)}, u32[]{:S(2)}) copy-start(s32[1,384,1]{1,2,0:T(1,128)} %param.20) | copy-start | bytes 4612
  50.1 4.7 %copy-start.39 = (bf16[16,896]{1,0:T(8,128)(2,1)S(1)}, bf16[16,896]{1,0:T(8,128)(2,1)}, u32[]{:S(2)}) copy-start(bf16[16,896]{1,0:T(8,128)(2,1)} %get-tuple-element.53) | copy-start | bytes 86020
  53.1 5.7 %copy-start.34 = (bf16[1536,156]{0,1:T(8,128)(2,1)}, bf16[1536,156]{0,1:T(8,128)(2,1)S(1)}, u32[]{:S(2)}) copy-start(bf16[1536,156]{0,1:T(8,128)(2,1)S(1)} %copy.115) | copy-start | bytes 1437700
  53.1 5.7 %copy-start.17 = (bf16[1,384,768]{2,1,0:T(8,128)(2,1)S(1)}, bf16[1,384,768]{2,1,0:T(8,128)(2,1)}, u32[]{:S(2)}) copy-start(bf16[1,384,768]{2,1,0:T(8,128)(2,1)} %param.18) | copy-start | bytes 1769476
  53.4 7.6 %copy-start.52 = (f32[384]{0:T(512)}, f32[384]{0:T(512)S(1)}, u32[]{:S(2)}) copy-start(f32[384]{0:T(512)S(1)} %fusion.74) | copy-start | bytes 4612
  58.8 14.7 %copy-start = (f32[16,1536]{1,0:T(8,128)}, f32[16,1536]{1,0:T(8,128)S(1)}, u32[]{:S(2)}) copy-start(f32[16,1536]{1,0:T(8,128)S(1)} %bitcast_multiply_fusion.1.refs_4_.refs_5_) | copy-start | bytes 294916
  63.4 4.7 %copy-start.40 = (f32[1536]{0:T(1024)}, f32[1536]{0:T(1024)S(1)}, u32[]{:S(2)}) copy-start(f32[1536]{0:T(1024)S(1)} %get-tuple-element.169) | copy-start | bytes 18436
  63.9 4.2 copy-start.5
  64.9 3.8 copy-start.42
  68.1 143.0 %copy-start.7 = (bf16[384,1536]{1,0:T(8,128)(2,1)}, bf16[384,1536]{1,0:T(8,128)(2,1)S(1)}, u32[]{:S(2)}) copy-start(bf16[384,1536]{1,0:T(8,128)(2,1)S(1)} %get-tuple-element.181) | copy-start | bytes 3538948
  68.7 4.9 %copy-start.32 = (f32[384,80]{0,1:T(8,128)}, f32[384,80]{0,1:T(8,128)S(1)}, u32[]{:S(2)}) copy-start(f32[384,80]{0,1:T(8,128)S(1)} %fusion.38) | copy-start | bytes 368644
  68.7 4.9 %copy-start.2 = (f32[16,384]{1,0:T(8,128)}, f32[16,384]{1,0:T(8,128)S(1)}, u32[]{:S(2)}) copy-start(f32[16,384]{1,0:T(8,128)S(1)} %get-tuple-element.196.refs_3_.refs_4_) | copy-start | bytes 73732
  68.7 4.9 %copy-start.3 = (f32[16,384]{1,0:T(8,128)}, f32[16,384]{1,0:T(8,128)S(1)}, u32[]{:S(2)}) copy-start(f32[16,384]{1,0:T(8,128)S(1)} %get-tuple-element.197.refs_2_.refs_3_) | copy-start | bytes 73732
  68.7 4.9 %copy-start.4 = (bf16[48,768]{1,0:T(8,128)(2,1)S(1)}, bf16[48,768]{1,0:T(8,128)(2,1)}, u32[]{:S(2)}) copy-start(bf16[48,768]{1,0:T(8,128)(2,1)} %refs_6_.1) | copy-start | bytes 221188
  73.6 55.5 %copy-start.18 = (bf16[1,384,768]{2,1,0:T(8,128)(2,1)S(1)}, bf16[1,384,768]{2,1,0:T(8,128)(2,1)}, u32[]{:S(2)}) copy-start(bf16[1,384,768]{2,1,0:T(8,128)(2,1)} %param.18) | copy-start | bytes 1769476
  73.6 55.5 %copy-start.48 = (f32[1536]{0:T(1024)S(1)}, f32[1536]{0:T(1024)}, u32[]{:S(2)}) copy-start(f32[1536]{0:T(1024)} %get-tuple-element.163) | copy-start | bytes 18436
  73.6 55.5 %copy-start.53 = (f32[384]{0:T(512)S(1)}, f32[384]{0:T(512)}, u32[]{:S(2)}) copy-start(f32[384]{0:T(512)} %copy-done.52) | copy-start | bytes 4612
  129.1 3.8 copy-start.60
  134.2 3.7 collective-permute-start.2
  134.6 4.5 %collective-permute-start.5 = (bf16[768,768]{1,0:T(8,128)(2,1)}, bf16[768,768]{1,0:T(8,128)(2,1)}, u32[]{:S(2)}, u32[]{:S(2)}) collective-permute-start(bf16[768,768]{1,0:T(8,128)(2,1)} %collective-permute-done.4.refs_10_), channel_id=1, source_target_pairs={{0,8},{8,0},{16,24},{24,16},{1,9},{9,1},{17,25},{25,17},{2,10},{10... | collective-permute-start | bytes 3538952 | tf_op jit(solution)/shard_map/ppermute | solution.py:929
  209.7 20.5 %collective-permute-start.7 = (bf16[768,768]{1,0:T(8,128)(2,1)}, bf16[768,768]{1,0:T(8,128)(2,1)}, u32[]{:S(2)}, u32[]{:S(2)}) collective-permute-start(bf16[768,768]{1,0:T(8,128)(2,1)} %get-tuple-element.67), channel_id=1, source_target_pairs={{0,8},{8,0},{16,24},{24,16},{1,9},{9,1},{17,25},{25,17},{2,10},{10... | collective-permute-start | bytes 3538952 | tf_op jit(solution)/shard_map/ppermute | solution.py:929
  211.1 5.8 %copy-start.14 = (f32[384,768]{1,0:T(8,128)}, f32[384,768]{1,0:T(8,128)S(1)}, u32[]{:S(2)}) copy-start(f32[384,768]{1,0:T(8,128)S(1)} %get-tuple-element.190) | copy-start | bytes 3538948
  219.8 13.1 %collective-permute-start.6 = (bf16[768,768]{1,0:T(8,128)(2,1)}, bf16[768,768]{1,0:T(8,128)(2,1)S(1)}, u32[]{:S(2)}, u32[]{:S(2)}) collective-permute-start(bf16[768,768]{1,0:T(8,128)(2,1)} %get-tuple-element.65), channel_id=1, source_target_pairs={{0,8},{8,0},{16,24},{24,16},{1,9},{9,1},{17,25},{25,17},{2,10},{10... | collective-permute-start | bytes 3538952 | tf_op jit(solution)/shard_map/ppermute | solution.py:929
  220.3 14.3 %collective-permute-start.8 = (bf16[768,768]{1,0:T(8,128)(2,1)}, bf16[768,768]{1,0:T(8,128)(2,1)S(1)}, u32[]{:S(2)}, u32[]{:S(2)}) collective-permute-start(bf16[768,768]{1,0:T(8,128)(2,1)} %get-tuple-element.69), channel_id=1, source_target_pairs={{0,8},{8,0},{16,24},{24,16},{1,9},{9,1},{17,25},{25,17},{2,10},{10... | collective-permute-start | bytes 3538952 | tf_op jit(solution)/shard_map/ppermute | solution.py:929
  220.4 16.0 %collective-permute-start.9 = (bf16[768,768]{1,0:T(8,128)(2,1)}, bf16[768,768]{1,0:T(8,128)(2,1)S(1)}, u32[]{:S(2)}, u32[]{:S(2)}) collective-permute-start(bf16[768,768]{1,0:T(8,128)(2,1)} %get-tuple-element.71), channel_id=1, source_target_pairs={{0,8},{8,0},{16,24},{24,16},{1,9},{9,1},{17,25},{25,17},{2,10},{10... | collective-permute-start | bytes 3538952 | tf_op jit(solution)/shard_map/ppermute | solution.py:929
  220.9 3.6 copy-start.63
  237.7 113.5 %copy-start.8 = (bf16[384,1536]{1,0:T(8,128)(2,1)S(1)}, bf16[384,1536]{1,0:T(8,128)(2,1)}, u32[]{:S(2)}) copy-start(bf16[384,1536]{1,0:T(8,128)(2,1)} %copy-done.7) | copy-start | bytes 3538948
  237.7 113.6 %copy-start.12 = (f32[384,1536]{1,0:T(8,128)S(1)}, f32[384,1536]{1,0:T(8,128)}, u32[]{:S(2)}) copy-start(f32[384,1536]{1,0:T(8,128)} %get-tuple-element.206) | copy-start | bytes 7077892
  354.5 4.8 %copy-start.6 = (f32[387,1536]{1,0:T(8,128)S(1)}, f32[387,1536]{1,0:T(8,128)}, u32[]{:S(2)}) copy-start(f32[387,1536]{1,0:T(8,128)} %copy-done.5) | copy-start | bytes 7133188
  354.6 4.8 %copy-start.41 = (f32[1536]{0:T(1024)S(1)}, f32[1536]{0:T(1024)}, u32[]{:S(2)}) copy-start(f32[1536]{0:T(1024)} %copy-done.40) | copy-start | bytes 18436
  367.2 5.0 %copy-start.10 = (f32[768,768]{1,0:T(8,128)S(1)}, f32[768,768]{1,0:T(8,128)}, u32[]{:S(2)}) copy-start(f32[768,768]{1,0:T(8,128)} %convert_add_fusion.3) | copy-start | bytes 7077892
  367.2 5.0 %copy-start.11 = (f32[768,768]{1,0:T(8,128)S(1)}, f32[768,768]{1,0:T(8,128)}, u32[]{:S(2)}) copy-start(f32[768,768]{1,0:T(8,128)} %convert_add_fusion.1) | copy-start | bytes 7077892
  367.2 5.0 %copy-start.24 = (bf16[768,768]{1,0:T(8,128)(2,1)S(1)}, bf16[768,768]{1,0:T(8,128)(2,1)}, u32[]{:S(2)}) copy-start(bf16[768,768]{1,0:T(8,128)(2,1)} %get-tuple-element.87) | copy-start | bytes 3538948
  367.2 5.0 %copy-start.25 = (bf16[768,768]{1,0:T(8,128)(2,1)S(1)}, bf16[768,768]{1,0:T(8,128)(2,1)}, u32[]{:S(2)}) copy-start(bf16[768,768]{1,0:T(8,128)(2,1)} %get-tuple-element.89) | copy-start | bytes 3538948
  368.4 13.4 %copy-start.21 = (f32[387,1536]{1,0:T(8,128)}, f32[387,1536]{1,0:T(8,128)S(1)}, u32[]{:S(2)}) copy-start(f32[387,1536]{1,0:T(8,128)S(1)} %pad_add_fusion) | copy-start | bytes 7133188
  370.9 10.9 %collective-permute-start.10 = (f32[3,1536]{1,0:T(4,128)S(1)}, f32[3,1536]{1,0:T(4,128)}, u32[]{:S(2)}, u32[]{:S(2)}) collective-permute-start(f32[3,1536]{1,0:T(4,128)S(1)} %pad_add_fusion.1), channel_id=1, source_target_pairs={{8,0},{16,8},{24,16},{9,1},{17,9},{25,17},{10,2},{18,10},{26,18},{... | collective-permute-start | bytes 55304 | tf_op jit(solution)/shard_map/ppermute | solution.py:48
  372.2 3.8 copy-start.35
  375.0 5.3 %copy-start.58 = (bf16[1536]{0:T(1024)(128)(2,1)S(1)}, bf16[1536]{0:T(1024)(128)(2,1)}, u32[]{:S(2)}) copy-start(bf16[1536]{0:T(1024)(128)(2,1)} %get-tuple-element.160) | copy-start | bytes 9220
  375.0 6.8 %copy-start.20 = (bf16[1,384,768]{2,1,0:T(8,128)(2,1)S(1)}, bf16[1,384,768]{2,1,0:T(8,128)(2,1)}, u32[]{:S(2)}) copy-start(bf16[1,384,768]{2,1,0:T(8,128)(2,1)} %param.18) | copy-start | bytes 1769476
  375.0 6.8 %copy-start.55 = (f32[384]{0:T(512)S(1)}, f32[384]{0:T(512)}, u32[]{:S(2)}) copy-start(f32[384]{0:T(512)} %copy-done.52) | copy-start | bytes 4612
  394.3 35.2 %copy-start.16 = (f32[384,768]{1,0:T(8,128)S(1)}, f32[384,768]{1,0:T(8,128)}, u32[]{:S(2)}) copy-start(f32[384,768]{1,0:T(8,128)} %copy-done.14) | copy-start | bytes 3538948
  424.5 7.7 %copy-start.37 = (f32[24,1536]{1,0:T(8,128)S(1)}, f32[24,1536]{1,0:T(8,128)}, u32[]{:S(2)}) copy-start(f32[24,1536]{1,0:T(8,128)} %get-tuple-element.84) | copy-start | bytes 442372
  (29 other events, 63.6 us)
where the time goes:
time: 443 us; the launch traced here: 434 us
  Pallas kernels  301 us (68%)
  matrix products  46.8 us (11%)
  local copies, waits for them, and re-layouts  41.6 us (9%)
  other arithmetic  35.9 us (8%)
  starting transfers between devices  5.26 us (1%)
    pallas_call x1, Pallas kernels, scan_backward(): pl.pallas_call(functools.partial(backward_kernel, places, streams, pick(c...  114 us
    pallas_call x1, Pallas kernels, run_experts(): pl.pallas_call(functools.partial(expert_kernel, slices), in_specs=[inside...  69.7 us
    pallas_call x1, Pallas kernels, scan_forward(): pl.pallas_call(functools.partial(forward_kernel, places, streams, pick(ch...  55.5 us
    pallas_call x1, Pallas kernels, gather_all(): pl.pallas_call(functools.partial(gather_kernel, places, streams, len(shar...  31.7 us
    pallas_call x1, Pallas kernels, reduce_all(): pl.pallas_call(functools.partial(reduce_kernel, places, streams, len(part...  30.2 us
    dot_general x7, matrix products, dot(): return jnp.dot(left, right, preferred_element_type=jnp.float32)  21.1 us
    unnamed x141, local copies, waits for them, and re-layouts  10.6 us
    concatenate x6, local copies, waits for them, and re-layouts, body(): jnp.concatenate(sums, axis=1).astype(jnp.bfloat16)  10.2 us
  transfers between devices with their start and end apart: 11, of which 2 were waited for; matrix products, arithmetic and copies ran while one was open for 15% of the time, Pallas kernels for 13%

commit v1 on v0

--- a/solution.py
+++ b/solution.py
@@ -89,33 +89,39 @@
 
 
 class GatherFlow:
-    def __init__(self, places, streams, shards, wholes, send_sems, recv_sems, local_sems):
-        self.places, self.streams, self.shards, self.wholes = places, streams, shards, wholes
+    def __init__(self, places, streams, dims, shards, wholes, send_sems, recv_sems, local_sems):
+        self.places, self.streams, self.dims, self.shards, self.wholes = places, streams, dims, shards, wholes
         self.sems = send_sems, recv_sems, local_sems
         self.bits = [own_bit(place) for place in places]
 
     def view(self, number, have):
-        array, cols, order = self.streams[number]
-        index = tuple(slice(None) if p in have else self.bits[p] for p in range(len(self.places)))
+        array, cols, order, begin = self.streams[number]
+        index = tuple(slice(None) if p in have else self.bits[p] for p in self.dims)
         return self.wholes[array].at[index + (slice(None), cols)]
 
+    def shard(self, number):
+        array, cols, order, begin = self.streams[number]
+        return self.shards[array].at[(slice(None),) * (begin + 1) + (cols,)]
+
     def own(self, number):
-        array, cols, order = self.streams[number]
-        return pltpu.make_async_copy(
-            self.shards[array].at[:, cols], self.view(number, ()), self.sems[2].at[number]
-        )
+        array, cols, order, begin = self.streams[number]
+        return pltpu.make_async_copy(self.shard(number), self.view(number, order[:begin]), self.sems[2].at[number])
 
     def flight(self, number, stage):
-        array, cols, order = self.streams[number]
-        target = self.view(number, order[:stage])
+        array, cols, order, begin = self.streams[number]
+        target = self.view(number, order[: begin + stage])
         return pltpu.make_async_remote_copy(
-            src_ref=self.shards[array].at[:, cols] if stage == 0 else target,
+            src_ref=self.shard(number) if stage == 0 else target,
             dst_ref=target,
             send_sem=self.sems[0].at[number, stage],
             recv_sem=self.sems[1].at[number, stage],
-            device_id=partner(self.places[order[stage]]),
+            device_id=partner(self.places[order[begin + stage]]),
             device_id_type=MESH,
         )
+
+    def stages(self, number):
+        array, cols, order, begin = self.streams[number]
+        return len(order) - begin
 
     def start(self):
         for number in range(len(self.streams)):
@@ -125,22 +131,30 @@
 
     def advance(self, stage):
         for number in range(len(self.streams)):
+            if stage >= self.stages(number):
+                continue
             if stage == 0:
                 self.own(number).wait()
             self.flight(number, stage).wait_recv()
-            if stage + 1 < len(self.places):
+            if stage + 1 < self.stages(number):
                 self.flight(number, stage + 1).start()
 
     def finish(self):
         for number in range(len(self.streams)):
-            for stage in range(len(self.places)):
+            for stage in range(self.stages(number)):
                 self.flight(number, stage).wait_send()
 
 
-def gather_kernel(places, streams, count, *refs):
-    shards, edge_ref, wholes, prior_ref = refs[:count], refs[count], refs[count + 1 : 2 * count + 1], refs[2 * count + 1]
-    send_sems, recv_sems, local_sems, edge_sems = refs[2 * count + 2 :]
-    flow = GatherFlow(places, streams, shards, wholes, send_sems, recv_sems, local_sems)
+def gather_kernel(places, streams, extra_streams, far, count, extra, *refs):
+    both = count + extra
+    shards, edge_ref, wholes, prior_ref = refs[:both], refs[both], refs[both + 1 : 2 * both + 1], refs[2 * both + 1]
+    send_sems, recv_sems, local_sems, late_send, late_recv, late_local, edge_sems = refs[2 * both + 2 :]
+    flow = GatherFlow(
+        places, streams, range(len(places)), shards[:count], wholes[:count], send_sems, recv_sems, local_sems
+    )
+    late = GatherFlow(
+        places, extra_streams, far, shards[count:], wholes[count:], late_send, late_recv, late_local
+    )
     blocks = lax.axis_size("ctx")
     here, line = lax.axis_index("ctx"), lax.axis_index("exp")
     meet(places, (lax.rem(here + 1, blocks), line), (lax.rem(here + blocks - 1, blocks), line))
@@ -154,9 +168,17 @@
         device_id_type=MESH,
     )
     edge.start()
-    for stage in range(len(places)):
+    stages, behind = len(places), len(far)
+    for stage in range(stages):
         flow.advance(stage)
+        if stage == behind - 2:
+            late.start()
+        if stage >= behind and stage - behind < behind:
+            late.advance(stage - behind)
+    for stage in range(stages - behind, behind):
+        late.advance(stage)
     flow.finish()
+    late.finish()
     edge.wait()
 
 
@@ -164,58 +186,76 @@
     core = places.index(("ctx", 0))
     rows = [k for k, place in enumerate(places) if place[0] == "ctx" and place[1] > 0]
     near = places.index(("exp", 0))
-    far = [k for k, place in sorted(enumerate(places), key=lambda item: item[1][1]) if place[0] == "exp" and place[1] > 0]
-    return [core] + rows + [near] + far, [core, near] + rows + far
-
-
-def streams_of(places, arrays, gathering):
-    first, second = [tuple(reversed(order)) if gathering else tuple(order) for order in orders_of(places)]
+    return [core] + rows + [near] + far_of(places), [core, near] + rows + far_of(places)
+
+
+def far_of(places):
+    return [k for k, place in sorted(enumerate(places), key=lambda item: item[1][1]) if place[0] == "exp" and place[1] > 0]
+
+
+def halves(arrays, first, second, begin=None):
     streams = []
     for array, values in enumerate(arrays):
-        width = values.shape[1]
+        width = values.shape[-1]
+        rest = () if begin is None else (begin,)
         if width % 256 == 0:
-            streams.append((array, slice(0, width // 2), first))
-            streams.append((array, slice(width // 2, width), second))
+            streams.append((array, slice(0, width // 2), first) + rest)
+            streams.append((array, slice(width // 2, width), second) + rest)
         else:
-            streams.append((array, slice(0, width), first if array % 2 else second))
+            streams.append((array, slice(0, width), first if array % 2 else second) + rest)
     return streams
 
 
-def gather_all(sizes, shards, edge, identity):
+def gather_orders(places):
+    return [tuple(reversed(order)) for order in orders_of(places)]
+
+
+def gather_all(sizes, shards, extra, edge, identity):
     places = bit_positions(sizes)
-    streams = streams_of(places, shards, True)
     stages = len(places)
+    far = sorted(far_of(places))
+    streams = halves(shards, *gather_orders(places), begin=0)
+    late = [(k, slice(0, part.shape[1]), tuple(reversed(far_of(places))), 0) for k, part in enumerate(extra)]
     anywhere = pl.BlockSpec(memory_space=pl.ANY)
+    total = len(shards) + len(extra)
     *wholes, prior = pl.pallas_call(
-        functools.partial(gather_kernel, places, streams, len(shards)),
-        in_specs=[anywhere] * (len(shards) + 1),
-        out_specs=[anywhere] * (len(shards) + 1),
+        functools.partial(gather_kernel, places, streams, late, far, len(shards), len(extra)),
+        in_specs=[anywhere] * (total + 1),
+        out_specs=[anywhere] * (total + 1),
         out_shape=[jax.ShapeDtypeStruct((2,) * stages + shard.shape, shard.dtype) for shard in shards]
+        + [jax.ShapeDtypeStruct((2,) * len(far) + part.shape, part.dtype) for part in extra]
         + [jax.ShapeDtypeStruct(edge.shape, edge.dtype)],
         scratch_shapes=[
             pltpu.SemaphoreType.DMA((len(streams), stages)),
             pltpu.SemaphoreType.DMA((len(streams), stages)),
             pltpu.SemaphoreType.DMA((len(streams),)),
+            pltpu.SemaphoreType.DMA((len(late), len(far))),
+            pltpu.SemaphoreType.DMA((len(late), len(far))),
+            pltpu.SemaphoreType.DMA((len(late),)),
             pltpu.SemaphoreType.DMA((2,)),
         ],
         compiler_params=pltpu.CompilerParams(collective_id=identity, has_side_effects=True),
         name="gather_all",
-    )(*shards, edge)
-    return [whole.reshape((-1,) + whole.shape[stages + 1 :]) for whole in wholes], prior
+    )(*shards, *extra, edge)
+    ready = [whole.reshape((-1,) + whole.shape[stages + 1 :]) for whole in wholes[: len(shards)]]
+    return ready, wholes[len(shards) :], prior
 
 
 class ReduceFlow:
-    def __init__(self, places, streams, parts, totals, landing, send_sems, recv_sems):
-        self.places, self.streams, self.parts, self.totals = places, streams, parts, totals
+    def __init__(self, places, streams, dims, parts, totals, landing, send_sems, recv_sems):
+        self.places, self.streams, self.dims, self.parts, self.totals = places, streams, dims, parts, totals
         self.landing, self.sems = landing, (send_sems, recv_sems)
         self.bits = [own_bit(place) for place in places]
+        self.first = []
+        for array, cols, order in streams:
+            self.first.append(sum(len(other[2]) for other in streams[: len(self.first)]))
 
     def spot(self, number, stage):
-        return self.landing[number * len(self.places) + stage]
+        return self.landing[self.first[number] + stage]
 
     def side(self, number, stage, value):
         array, cols, order = self.streams[number]
-        left = [p for p in range(len(self.places)) if p not in order[:stage]]
+        left = [p for p in self.dims if p not in order[:stage]]
         index = tuple(value if p == order[stage] else slice(None) for p in left)
         if stage == 0:
             return self.parts[array].at[index + (slice(None), cols)]
@@ -237,73 +277,93 @@
             self.flight(number, 0).start()
 
     def advance(self, stage):
-        stages = len(self.places)
         for number, (array, cols, order) in enumerate(self.streams):
+            if stage >= len(order):
+                continue
             self.flight(number, stage).wait_recv()
             mine = self.side(number, stage, self.bits[order[stage]])
             there = self.spot(number, stage)
-            if stage + 1 == stages:
+            depth = len(self.dims) - stage - 1
+            final = stage + 1 == len(order)
+            if depth == 0:
                 self.totals[array][:, cols] = there[...].astype(jnp.float32) + mine[...].astype(jnp.float32)
                 continue
-            depth = stages - stage - 1
-
-            def add(index, unused, there=there, mine=mine, depth=depth):
+
+            def add(index, unused, there=there, mine=mine, depth=depth, final=final, array=array, cols=cols):
                 at = tuple(lax.rem(index // 2 ** (depth - 1 - k), 2) for k in range(depth))
-                there[at] = (there[at].astype(jnp.float32) + mine[at].astype(jnp.float32)).astype(there.dtype)
+                value = (there[at].astype(jnp.float32) + mine[at].astype(jnp.float32)).astype(there.dtype)
+                if final:
+                    self.totals[array][at + (slice(None), cols)] = value
+                else:
+                    there[at] = value
                 return unused
 
             lax.fori_loop(0, 2**depth, add, 0)
-            self.flight(number, stage + 1).start()
+            if not final:
+                self.flight(number, stage + 1).start()
 
     def finish(self):
         for number in range(len(self.streams)):
-            for stage in range(len(self.places)):
+            for stage in range(len(self.streams[number][2])):
                 self.flight(number, stage).wait_send()
 
 
-def reduce_kernel(places, streams, count, *refs):
-    parts, totals = refs[:count], refs[count : 2 * count]
-    landing = refs[2 * count : 2 * count + len(streams) * len(places)]
-    send_sems, recv_sems = refs[2 * count + len(streams) * len(places) :]
-    flow = ReduceFlow(places, streams, parts, totals, landing, send_sems, recv_sems)
+def landing_of(streams, dims, divided):
+    landing = []
+    for array, cols, order in streams:
+        for stage in range(len(order)):
+            rows = divided[array].shape[-2]
+            landing.append(pltpu.VMEM((2,) * (len(dims) - stage - 1) + (rows, cols.stop - cols.start), jnp.bfloat16))
+    return landing
+
+
+def flights(streams):
+    shape = (len(streams), max(len(order) for array, cols, order in streams))
+    return [pltpu.SemaphoreType.DMA(shape)] * 2
+
+
+def reduce_kernel(places, streams, late, far, count, extra, marks, *refs):
+    both = count + extra
+    parts, totals, scratch = refs[:both], refs[both : 2 * both], refs[2 * both :]
+    landing, late_landing = scratch[: marks[0]], scratch[marks[0] : marks[1]]
+    send_sems, recv_sems, late_send, late_recv = scratch[marks[1] :]
+    flow = ReduceFlow(
+        places, streams, range(len(places)), parts[:count], totals[:count], landing, send_sems, recv_sems
+    )
+    rest = ReduceFlow(places, late, far, parts[count:], totals[count:], late_landing, late_send, late_recv)
     meet(places)
     flow.start()
+    rest.start()
     for stage in range(len(places)):
         flow.advance(stage)
+        rest.advance(stage)
     flow.finish()
-
-
-def landing_of(places, streams, divided):
-    stages = len(places)
-    landing = []
-    for array, cols, order in streams:
-        for stage in range(stages):
-            rows = divided[array].shape[-2]
-            landing.append(pltpu.VMEM((2,) * (stages - stage - 1) + (rows, cols.stop - cols.start), jnp.bfloat16))
-    return landing
-
-
-def reduce_all(sizes, parts, identity):
+    rest.finish()
+
+
+def reduce_all(sizes, parts, extra, identity):
     places = bit_positions(sizes)
     stages = len(places)
-    streams = streams_of(places, parts, False)
+    far = sorted(far_of(places))
+    streams = halves(parts, *[tuple(order) for order in orders_of(places)])
+    late = [(k, slice(0, part.shape[-1]), tuple(far_of(places))) for k, part in enumerate(extra)]
     divided = [part.reshape((2,) * stages + (-1, part.shape[1])) for part in parts]
     inside = pl.BlockSpec(memory_space=pltpu.VMEM)
+    landing = landing_of(streams, range(stages), divided)
+    late_landing = landing_of(late, far, extra)
+    marks = len(landing), len(landing) + len(late_landing)
+    total = len(parts) + len(extra)
     return pl.pallas_call(
-        functools.partial(reduce_kernel, places, streams, len(parts)),
-        in_specs=[inside] * len(parts),
-        out_specs=[inside] * len(parts),
-        out_shape=[jax.ShapeDtypeStruct(block.shape[-2:], jnp.float32) for block in divided],
-        scratch_shapes=landing_of(places, streams, divided)
-        + [
-            pltpu.SemaphoreType.DMA((len(streams), stages)),
-            pltpu.SemaphoreType.DMA((len(streams), stages)),
-        ],
+        functools.partial(reduce_kernel, places, streams, late, far, len(parts), len(extra), marks),
+        in_specs=[inside] * total,
+        out_specs=[inside] * total,
+        out_shape=[jax.ShapeDtypeStruct(block.shape[-2:], jnp.float32) for block in divided + list(extra)],
+        scratch_shapes=landing + late_landing + flights(streams) + flights(late),
         compiler_params=pltpu.CompilerParams(
             collective_id=identity, has_side_effects=True, vmem_limit_bytes=48 * 1024 * 1024
         ),
         name="reduce_all",
-    )(*divided)
+    )(*divided, *extra)
 
 
 def dot(left, right):
@@ -567,7 +627,7 @@
     blocks = lax.axis_size("ctx")
     position = lax.axis_index("ctx")
     span = kept_buf.shape[1]
-    flow = GatherFlow(places, streams, shards, wholes, send_sems, recv_sems, local_sems)
+    flow = GatherFlow(places, streams, range(len(places)), shards, wholes, send_sems, recv_sems, local_sems)
     meet([place for place in places if place[0] == "exp"], *row_peers())
     flow.start()
 
@@ -576,12 +636,7 @@
     spread_columns(bt_ref, wide_b)
     spread_columns(ct_ref, wide_c)
 
-    def first_hook(group):
-        @pl.when(group == 1)
-        def _():
-            flow.advance(0)
-
-    end_pass(width, step_ref, push_ref, wide_b, rate_ref, state_ref, first_hook)
+    end_pass(width, step_ref, push_ref, wide_b, rate_ref, state_ref, lambda group: None)
     message[1] = state_ref[...].astype(jnp.bfloat16)
     late = share(message.at[1], ends, share_sems.at[2], share_sems.at[3])
     for copy in early + late:
@@ -596,7 +651,7 @@
     first_buf[0] = start.astype(jnp.bfloat16)
     first_copy = pltpu.make_async_copy(first_buf, kept_ref.at[pl.ds(0, 1)], first_sem)
     first_copy.start()
-    flow.advance(1)
+    flow.advance(0)
 
     def kept_copy(number, slot):
         return pltpu.make_async_copy(
@@ -604,12 +659,12 @@
         )
 
     def second_hook(number):
-        @pl.when(number == 1)
+        @pl.when(number == 3)
         def _():
-            flow.advance(2)
+            flow.advance(1)
 
     out_pass(width, step_ref, push_ref, wide_b, wide_c, rate_ref, state_ref, y_ref, kept_buf, kept_copy, second_hook)
-    for stage in range(3, len(places)):
+    for stage in range(2, max(flow.stages(number) for number in range(len(streams)))):
         flow.advance(stage)
     flow.finish()
     first_copy.wait()
@@ -619,8 +674,9 @@
 
 def scan_forward(sizes, step, push, b_turned, c_turned, rates, shards, identity, span=64):
     places = bit_positions(sizes)
-    streams = streams_of(places, shards, True)
     stages = len(places)
+    begin = len(far_of(places))
+    streams = halves(shards, *gather_orders(places), begin=begin)
     tokens, channels = step.shape
     blocks = sizes[0][1]
     inside = pl.BlockSpec(memory_space=pltpu.VMEM)
@@ -636,7 +692,7 @@
             jax.ShapeDtypeStruct((blocks, NS, channels), half),
             jax.ShapeDtypeStruct((tokens + 1, NS, channels), half),
         ]
-        + [jax.ShapeDtypeStruct((2,) * stages + shard.shape, shard.dtype) for shard in shards],
+        + [jax.ShapeDtypeStruct((2,) * stages + shard.shape[begin:], shard.dtype) for shard in shards],
         scratch_shapes=[
             pltpu.VMEM((tokens, NS, LANES), jnp.float32),
             pltpu.VMEM((tokens, NS, LANES), jnp.float32),
@@ -662,24 +718,22 @@
     return y, start, products, kept, [whole.reshape((-1,) + whole.shape[stages + 1 :]) for whole in wholes]
 
 
-def backward_kernel(places, streams, width, moved, *refs):
+def backward_kernel(places, streams, marks, width, *refs):
     step_ref, push_ref, grad_ref, bt_ref, ct_ref, rate_ref, product_ref = refs[:7]
     parts = refs[7:9]
     kept_ref = refs[9]
-    leaving = refs[10 : 10 + moved]
-    outs = refs[10 + moved :]
+    outs = refs[10:]
     along_ref, slope_ref, gb_ref, gc_ref, ga_ref = outs[:5]
     totals = outs[5:7]
-    arriving = outs[7 : 7 + moved]
-    scratch = outs[7 + moved :]
-    landing = scratch[: len(streams) * len(places)]
+    scratch = outs[7:]
+    landing = scratch[:marks]
     (wide_b, wide_c, part_b, part_c, kept_buf, flow_ref, message, inflows,
-     kept_sems, share_sems, moved_sems, send_sems, recv_sems) = scratch[len(streams) * len(places) :]
+     kept_sems, share_sems, send_sems, recv_sems) = scratch[marks:]
     blocks = lax.axis_size("ctx")
     position = lax.axis_index("ctx")
     span = kept_buf.shape[1] - 1
     steps = step_ref.shape[0] // span
-    flow = ReduceFlow(places, streams, parts, totals, landing, send_sems, recv_sems)
+    flow = ReduceFlow(places, streams, range(len(places)), parts, totals, landing, send_sems, recv_sems)
 
     def kept_copy(number, slot):
         return pltpu.make_async_copy(
@@ -703,21 +757,6 @@
         end = jnp.where(index > position, folded, end)
     flow_ref[...] = end
     flow.advance(0)
-    last = ("ctx", blocks.bit_length() - 2)
-    moves = []
-    for k in range(moved):
-        moves.append(
-            pltpu.make_async_remote_copy(
-                src_ref=leaving[k],
-                dst_ref=arriving[k],
-                send_sem=moved_sems.at[0, k],
-                recv_sem=moved_sems.at[1, k],
-                device_id=partner(last),
-                device_id_type=MESH,
-            )
-        )
-        moves[-1].start()
-
     def hook(order):
         @pl.when(order == 2)
         def _():
@@ -729,36 +768,34 @@
 
     adjoint_pass(width, step_ref, push_ref, grad_ref, wide_b, wide_c, rate_ref, flow_ref, kept_buf, kept_copy,
                  along_ref, slope_ref, gb_ref, gc_ref, ga_ref, part_b, part_c, hook)
-    for stage in range(3, len(places)):
+    for stage in range(3, len(streams[0][2])):
         flow.advance(stage)
     flow.finish()
     for copy in copies:
         copy.wait_send()
-    for move in moves:
-        move.wait()
-
-
-def scan_backward(sizes, step, push, grad, b_turned, c_turned, rates, products, parts, kept, leaving, identity, span=64):
+
+
+def scan_backward(sizes, step, push, grad, b_turned, c_turned, rates, products, parts, kept, identity, span=64):
     places = bit_positions(sizes)
     stages = len(places)
-    streams = streams_of(places, parts, False)
+    far = sorted(far_of(places))
+    streams = halves(parts, *[tuple(order[: stages - len(far)]) for order in orders_of(places)])
     divided = [part.reshape((2,) * stages + (-1, part.shape[1])) for part in parts]
     tokens, channels = step.shape
     blocks = sizes[0][1]
     inside = pl.BlockSpec(memory_space=pltpu.VMEM)
     anywhere = pl.BlockSpec(memory_space=pl.ANY)
     half = jnp.bfloat16
-    moved = len(leaving)
+    landing = landing_of(streams, range(stages), divided)
     row_sums = jax.ShapeDtypeStruct((tokens // span, UNROLL, span * NS), jnp.float32)
     out = pl.pallas_call(
-        functools.partial(backward_kernel, places, streams, pick(channels), moved),
-        in_specs=[inside] * 9 + [anywhere] * (1 + moved),
-        out_specs=[inside] * 7 + [anywhere] * moved,
+        functools.partial(backward_kernel, places, streams, len(landing), pick(channels)),
+        in_specs=[inside] * 9 + [anywhere],
+        out_specs=[inside] * 7,
         out_shape=[jax.ShapeDtypeStruct((tokens, channels), jnp.float32)] * 2
         + [row_sums, row_sums, jax.ShapeDtypeStruct((NS, channels), jnp.float32)]
-        + [jax.ShapeDtypeStruct(block.shape[-2:], jnp.float32) for block in divided]
-        + [jax.ShapeDtypeStruct(value.shape, value.dtype) for value in leaving],
-        scratch_shapes=landing_of(places, streams, divided)
+        + [jax.ShapeDtypeStruct((2,) * len(far) + block.shape[-2:], half) for block in divided],
+        scratch_shapes=landing
         + [
             pltpu.VMEM((tokens, NS, LANES), jnp.float32),
             pltpu.VMEM((tokens, NS, LANES), jnp.float32),
@@ -770,45 +807,48 @@
             pltpu.VMEM((blocks, NS, channels), half),
             pltpu.SemaphoreType.DMA((2,)),
             pltpu.SemaphoreType.DMA((2, blocks)),
-            pltpu.SemaphoreType.DMA((2, max(1, moved))),
-            pltpu.SemaphoreType.DMA((len(streams), stages)),
-            pltpu.SemaphoreType.DMA((len(streams), stages)),
-        ],
+        ]
+        + flights(streams),
         compiler_params=pltpu.CompilerParams(
             collective_id=identity, has_side_effects=True, vmem_limit_bytes=56 * 1024 * 1024
         ),
         cost_estimate=cost(tokens, channels, 15),
         name="scan_backward",
-    )(step, push, grad, b_turned, c_turned, rates, products, *divided, kept, *leaving)
+    )(step, push, grad, b_turned, c_turned, rates, products, *divided, kept)
     along, slope, wide_b, wide_c, grad_a = out[:5]
     grad_bs, grad_cs = [values[:, 0].reshape(tokens, NS) for values in (wide_b, wide_c)]
-    return along, slope, grad_bs, grad_cs, grad_a, out[5:7], list(out[7:])
+    return along, slope, grad_bs, grad_cs, grad_a, out[5:7]
 
 
 def expert_kernel(slices, *refs):
     tokens_ref, grads_ref, column_ref, row_ref = refs[:4]
-    weights_in, weights_out = refs[4 : 4 + slices], refs[4 + slices : 4 + 2 * slices]
-    outs = refs[4 + 2 * slices :]
-    picked_ref, back_ref = outs[:2]
-    sums_in, sums_out = outs[2 : 2 + slices], outs[2 + slices : 2 + 2 * slices]
-    (sent, got, answer, returned, w_in, w_out, hidden, total, active, slope, inner,
-     send_sems, recv_sems, weight_sems, sum_sems) = outs[2 + 2 * slices :]
+    even = range(0, slices, 2)
+    odd = range(1, slices, 2)
+    weights_in, weight_out = refs[4 : 4 + len(even)], refs[4 + len(even)]
+    outs = refs[5 + len(even) :]
+    picked_ref, back_ref, own_out = outs[:3]
+    sums_in = outs[3 : 3 + len(even)]
+    (sent, got, answer, returned, w_in, w_out, hidden, total, active, slope, inner, sum_out, pair_out, pair_in, far_out,
+     send_sems, recv_sems, weight_sems, sum_sems, spread_sems, mate_sems, far_sems) = outs[3 + len(even) :]
     experts, room, width = sent.shape[1:]
     places = experts * room
     me = lax.axis_index("exp")
     here = lax.axis_index("ctx")
-
-    loads = []
-    for s in range(slices):
-        loads.append(pltpu.make_async_copy(weights_in[s], w_in.at[s], weight_sems.at[0, s]))
-        loads.append(pltpu.make_async_copy(weights_out[s], w_out.at[s], weight_sems.at[1, s]))
+    levels = slices.bit_length() - 1
+
+    loads = [pltpu.make_async_copy(weight_out, w_out.at[0], weight_sems.at[slices])]
+    for k, s in enumerate(even):
+        loads.append(pltpu.make_async_copy(weights_in[k], w_in.at[s], weight_sems.at[s]))
     for load in loads:
         load.start()
 
     barrier = pltpu.get_barrier_semaphore()
+    mates = [partner(("ctx", level)) for level in range(levels)]
     for step in range(1, experts):
         pl.semaphore_signal(barrier, inc=1, device_id=(here, lax.rem(me + step, experts)), device_id_type=MESH)
-    pl.semaphore_wait(barrier, experts - 1)
+    for mate in mates:
+        pl.semaphore_signal(barrier, inc=1, device_id=mate, device_id_type=MESH)
+    pl.semaphore_wait(barrier, experts - 1 + levels)
 
     def exchange(source, target, kind):
         copies = []
@@ -827,21 +867,45 @@
         target[me] = source[me]
         return copies
 
+    def hand(source, target, sems, level):
+        copy = pltpu.make_async_remote_copy(
+            src_ref=source,
+            dst_ref=target,
+            send_sem=sems.at[0],
+            recv_sem=sems.at[1],
+            device_id=mates[level],
+            device_id_type=MESH,
+        )
+        copy.start()
+        return copy
+
     def arrive(copies):
         for copy in copies:
             copy.wait_recv()
 
+    open_sends = []
+
+    def spread(level):
+        step = 2**level
+        copies = [hand(w_out.at[s], w_out.at[s + step], spread_sems.at[1, s + step], level) for s in range(0, slices, 2 * step)]
+        open_sends.extend(copies)
+        return copies
+
     chooser = (lax.broadcasted_iota(jnp.int32, (places, row_ref.shape[1]), 0) == row_ref[...]).astype(jnp.float32).astype(jnp.bfloat16)
     sent[0] = dot(chooser, tokens_ref[...]).astype(jnp.bfloat16).reshape(experts, room, width)
     first = exchange(sent.at[0], got.at[0], 0)
+    for load in loads:
+        load.wait()
+    widening = [spread(levels - 1)]
+    paired = [hand(w_in.at[s], w_in.at[s + 1], spread_sems.at[0, s], 0) for s in even]
     sent[1] = dot(chooser, grads_ref[...]).astype(jnp.bfloat16).reshape(experts, room, width)
     second = exchange(sent.at[1], got.at[1], 1)
 
-    for load in loads:
-        load.wait()
     arrive(first)
     rows = got[0].reshape(places, width)
-    for s in range(slices):
+    for s in list(even) + list(odd):
+        if s == 1:
+            arrive(paired)
         hidden[...] = dot(rows, w_in[s])
 
         def curve(index, unused):
@@ -853,6 +917,13 @@
             return unused
 
         lax.fori_loop(0, places // ROWS_AT_ONCE, curve, 0)
+
+    for level in reversed(range(levels - 1)):
+        arrive(widening[-1])
+        widening.append(spread(level))
+    for s in list(even) + list(odd):
+        if s == 1:
+            arrive(widening[-1])
         product = dot(active[s], w_out[s])
         total[...] = product if s == 0 else total[...] + product
     answer[0] = total[...].astype(jnp.bfloat16).reshape(experts, room, width)
@@ -860,6 +931,11 @@
 
     arrive(second)
     pulled = got[1].reshape(places, width)
+    joining = []
+    for s in list(odd) + list(even):
+        sum_out[s] = contract(active[s], pulled, 0, 0).astype(jnp.bfloat16)
+        if s % 2:
+            joining.append(hand(sum_out.at[s], pair_out.at[s // 2], mate_sems.at[0, s // 2], 0))
     for s in range(slices):
         inner[s] = (contract(pulled, w_out[s], 1, 1) * slope[s]).astype(jnp.bfloat16)
         product = contract(inner[s], w_in[s], 1, 1)
@@ -867,41 +943,78 @@
     answer[1] = total[...].astype(jnp.bfloat16).reshape(experts, room, width)
     fourth = exchange(answer.at[1], returned.at[1], 3)
 
+    def add_into(target, addend):
+        def some(index, unused):
+            at = pl.ds(pl.multiple_of(index * 4 * ROWS_AT_ONCE, 4 * ROWS_AT_ONCE), 4 * ROWS_AT_ONCE)
+            target[at, :] = (target[at, :].astype(jnp.float32) + addend[at, :].astype(jnp.float32)).astype(jnp.bfloat16)
+            return unused
+
+        lax.fori_loop(0, target.shape[0] // (4 * ROWS_AT_ONCE), some, 0)
+
+    arrive(joining)
+    for k, s in enumerate(even):
+        add_into(sum_out.at[s], pair_out.at[k])
+
+    def pass_on(level):
+        step = 2**level
+        return [
+            hand(sum_out.at[s + step], far_out.at[slices // step // 2 - 1 + s // (2 * step)], far_sems.at[level, s // (2 * step)], level)
+            for s in range(0, slices, 2 * step)
+        ]
+
+    passing = pass_on(1)
+    open_sends.extend(joining)
+    for copy in paired:
+        copy.wait_send()
+    joined = []
+    for s in list(odd) + list(even):
+        w_in[s] = contract(rows, inner[s], 0, 0).astype(jnp.bfloat16)
+        if s % 2:
+            joined.append(hand(w_in.at[s], pair_in.at[s // 2], mate_sems.at[1, s // 2], 0))
+    arrive(joined)
     stores = []
-    for s in range(slices):
-        w_out[s] = contract(active[s], pulled, 0, 0).astype(jnp.bfloat16)
-        stores.append(pltpu.make_async_copy(w_out.at[s], sums_out[s], sum_sems.at[0, s]))
-        stores[-1].start()
-        w_in[s] = contract(rows, inner[s], 0, 0).astype(jnp.bfloat16)
-        stores.append(pltpu.make_async_copy(w_in.at[s], sums_in[s], sum_sems.at[1, s]))
+    for k, s in enumerate(even):
+        add_into(w_in.at[s], pair_in.at[k])
+        stores.append(pltpu.make_async_copy(w_in.at[s], sums_in[k], sum_sems.at[k]))
         stores[-1].start()
 
     finder = (lax.broadcasted_iota(jnp.int32, (column_ref.shape[0], places), 1) == column_ref[...]).astype(jnp.float32).astype(jnp.bfloat16)
     arrive(third)
     picked_ref[...] = dot(finder, returned[0].reshape(places, width)).astype(jnp.bfloat16)
+    for level in range(1, levels):
+        arrive(passing)
+        open_sends.extend(passing)
+        step = 2**level
+        if level + 1 < levels:
+            for s in range(0, slices, 2 * step):
+                add_into(sum_out.at[s], far_out.at[slices // step // 2 - 1 + s // (2 * step)])
+            passing = pass_on(level + 1)
+    own_out[...] = sum_out[0].astype(jnp.float32) + far_out[0].astype(jnp.float32)
     arrive(fourth)
     back_ref[...] = dot(finder, returned[1].reshape(places, width)).astype(jnp.bfloat16)
     for store in stores:
         store.wait()
-    for copies in (first, second, third, fourth):
+    for copies in (first, second, third, fourth, joined, open_sends):
         for copy in copies:
             copy.wait_send()
 
 
-def run_experts(rows, grads, target, weights_in, weights_out, experts, room, identity):
-    slices = len(weights_in)
+def run_experts(rows, grads, target, weights_in, weight_out, experts, room, identity):
+    slices = 2 * len(weights_in)
     tokens, width = rows.shape
-    inner_width = weights_in[0].shape[1]
+    inner_width = weight_out.shape[0]
     places = experts * room
     inside = pl.BlockSpec(memory_space=pltpu.VMEM)
     anywhere = pl.BlockSpec(memory_space=pl.ANY)
     half = jnp.bfloat16
+    count = len(weights_in)
     out = pl.pallas_call(
         functools.partial(expert_kernel, slices),
-        in_specs=[inside] * 4 + [anywhere] * (2 * slices),
-        out_specs=[inside] * 2 + [anywhere] * (2 * slices),
+        in_specs=[inside] * 4 + [anywhere] * (count + 1),
+        out_specs=[inside] * 3 + [anywhere] * count,
         out_shape=[jax.ShapeDtypeStruct(rows.shape, half)] * 2
-        + [jax.ShapeDtypeStruct(weight.shape, half) for weight in weights_in + weights_out],
+        + [jax.ShapeDtypeStruct(weight_out.shape, jnp.float32)]
+        + [jax.ShapeDtypeStruct(weight.shape, half) for weight in weights_in],
         scratch_shapes=[pltpu.VMEM((2, experts, room, width), half)] * 4
         + [
             pltpu.VMEM((slices, width, inner_width), half),
@@ -911,17 +1024,24 @@
             pltpu.VMEM((slices, places, inner_width), half),
             pltpu.VMEM((slices, places, inner_width), jnp.float32),
             pltpu.VMEM((slices, places, inner_width), half),
+            pltpu.VMEM((slices, inner_width, width), half),
+            pltpu.VMEM((count, inner_width, width), half),
+            pltpu.VMEM((count, width, inner_width), half),
+            pltpu.VMEM((count, inner_width, width), half),
             pltpu.SemaphoreType.DMA((4, experts)),
             pltpu.SemaphoreType.DMA((4, experts)),
-            pltpu.SemaphoreType.DMA((2, slices)),
-            pltpu.SemaphoreType.DMA((2, slices)),
+            pltpu.SemaphoreType.DMA((slices + 1,)),
+            pltpu.SemaphoreType.DMA((count,)),
+            pltpu.SemaphoreType.DMA((2, slices, 2)),
+            pltpu.SemaphoreType.DMA((2, count, 2)),
+            pltpu.SemaphoreType.DMA((slices, count, 2)),
         ],
         compiler_params=pltpu.CompilerParams(
-            collective_id=identity, has_side_effects=True, vmem_limit_bytes=52 * 1024 * 1024
+            collective_id=identity, has_side_effects=True, vmem_limit_bytes=60 * 1024 * 1024
         ),
         name="run_experts",
-    )(rows, grads, target[:, None], target[None, :], *weights_in, *weights_out)
-    return out[0], out[1], list(out[2 : 2 + slices]), list(out[2 + slices :])
+    )(rows, grads, target[:, None], target[None, :], *weights_in, weight_out)
+    return out[0], out[1], list(out[3:]), out[2]
 
 
 def flipped(value, level):
@@ -932,21 +1052,20 @@
 def spread_slices(own):
     levels = lax.axis_size("ctx").bit_length() - 1
     slices = {0: own}
-    for level in reversed(range(levels)):
+    for level in reversed(range(1, levels)):
         for offset in sorted(slices):
             slices[offset + (1 << level)] = flipped(slices[offset], level)
     return [slices[offset] for offset in sorted(slices)]
 
 
-def collect_slices(sums, levels):
-    for level in levels:
-        step = 1 << level
-        kept = {}
-        for offset in range(0, len(sums), 2 * step):
-            arrived = flipped(sums[offset + step].astype(jnp.bfloat16), level)
-            kept[offset] = sums[offset].astype(jnp.float32) + arrived.astype(jnp.float32)
-        sums = [kept.get(offset) for offset in range(len(sums))]
-    return sums
+def collect_slices(sums):
+    levels = lax.axis_size("ctx").bit_length() - 1
+    for level in range(1, levels):
+        arrived = [flipped(values, level).astype(jnp.float32) for values in sums[1::2]]
+        sums = [values.astype(jnp.float32) + other for values, other in zip(sums[::2], arrived)]
+        if level + 1 < levels:
+            sums = [values.astype(jnp.bfloat16) for values in sums]
+    return sums[0]
 
 
 def body(
@@ -987,12 +1106,11 @@
     sizes = [(name, lax.axis_size(name)) for name in ("ctx", "exp")]
     tail_ids = segments[0, -EDGE:, None].astype(jnp.bfloat16)
     edge = jnp.concatenate([inputs[0, -EDGE:], jnp.broadcast_to(tail_ids, (EDGE, LANES))], axis=1)
-    (full_conv, full_small), prior = gather_all(
-        sizes, (in_proj[:, :DI], jnp.concatenate(columns, axis=1)), edge, 0
-    )
-    later_in, later_out, full_small = lax.optimization_barrier((expert_in[0], expert_out[0], full_small))
+    (full_conv, full_small), partial, prior = gather_all(
+        sizes, (in_proj[:, :DI], jnp.concatenate(columns, axis=1)), (in_proj[:, DI:], out_proj), edge, 0
+    )
+    later_in, full_small = lax.optimization_barrier((expert_in[0], full_small))
     weights_in = spread_slices(later_in)
-    weights_out = spread_slices(later_out)
     full_xproj, full_dt, full_taps, full_bias, full_dtbias, full_decay, full_skip, gains, full_router = [
         full_small[:, end - width : end] for end, width in zip(ends, widths)
     ]
@@ -1034,12 +1152,13 @@
     a_swap = -jnp.exp(full_decay.astype(jnp.float32)).T
     earlier = jnp.concatenate([prior_ids[KC - 2 :], seg_row[:-1]])
     keep_mask = (earlier == seg_row).astype(jnp.float32)
+    push = step_size * xs_wide
     masked_step = jnp.where(keep_mask[:, None] > 0, step_size, 1e30)
-    push = step_size * xs_wide
     rates = a_swap * LOG2E
     b_turned, c_turned = b_rows.T, c_rows.T
+    push, *weights_in = lax.optimization_barrier((push, *weights_in))
     scan_rows, start_state, products, kept, (full_gate, full_out) = scan_forward(
-        sizes, masked_step, push, b_turned, c_turned, rates, (in_proj[:, DI:], out_proj), 3
+        sizes, masked_step, push, b_turned, c_turned, rates, partial, 3
     )
     gate_z = dot(normed_one, full_gate)
     skip_wide = full_skip.astype(jnp.float32)
@@ -1064,17 +1183,15 @@
     target = route_ids * room + slot_index
     grad_out = cotangent[0].astype(jnp.float32)
     grad_pick = (grad_out * gate_val[:, None]).astype(jnp.bfloat16)
-    picked, grad_from_experts, grad_expert_in, grad_expert_out = run_experts(
-        normed_two, grad_pick, target, weights_in, weights_out, experts, room, 2
-    )
+    picked, grad_from_experts, grad_expert_in, grad_w_out = run_experts(
+        normed_two, grad_pick, target, weights_in, expert_out[0], experts, room, 2
+    )
+    grad_w_in = collect_slices(grad_expert_in)
     picked = picked.astype(jnp.float32)
     grad_from_experts = grad_from_experts.astype(jnp.float32)
     outcome = residual + gate_val[:, None] * picked
     out_block = outcome.astype(jnp.bfloat16)[None]
     grad_gate = jnp.sum(grad_out * picked, axis=1)
-    levels = lax.axis_size("ctx").bit_length() - 1
-    grad_expert_in = collect_slices(grad_expert_in, range(1))
-    grad_expert_out = collect_slices(grad_expert_out, range(1))
     grad_probs = grad_gate[:, None] * one_float
     grad_logits = (
         probability * (grad_probs - jnp.sum(grad_probs * probability, axis=1, keepdims=True))
@@ -1091,14 +1208,8 @@
     grad_y, grad_z = gated_pull(grad_gated)
     grad_skip = jnp.sum(grad_y * xs_wide, axis=0)
     grad_z = grad_z.astype(jnp.bfloat16)
-    grad_y, grad_expert_in, grad_expert_out = lax.optimization_barrier(
-        (grad_y, grad_expert_in, grad_expert_out)
-    )
-    grad_expert_in = collect_slices(grad_expert_in, range(1, levels - 1))
-    grad_expert_out = collect_slices(grad_expert_out, range(1, levels - 1))
-    last = 1 << (levels - 1)
-    leaving = [values[last].astype(jnp.bfloat16) for values in (grad_expert_in, grad_expert_out)]
-    along_b, slope, grad_bs, grad_cs, grad_a, (own_gate, own_out), arrived = scan_backward(
+    grad_y, grad_w_in = lax.optimization_barrier((grad_y, grad_w_in))
+    along_b, slope, grad_bs, grad_cs, grad_a, partial_sums = scan_backward(
         sizes,
         masked_step,
         push,
@@ -1109,13 +1220,8 @@
         products,
         (dot(normed_one.T, grad_z).astype(jnp.bfloat16), grad_out_proj.astype(jnp.bfloat16)),
         kept,
-        leaving,
         4,
     )
-    grad_w_in, grad_w_out = [
-        values[0].astype(jnp.float32) + other.astype(jnp.float32)
-        for values, other in zip((grad_expert_in, grad_expert_out), arrived)
-    ]
     grad_step_all = along_b * xs_wide + slope * (1.0 / LOG2E)
     grad_xss = along_b * step_size
     grad_log_decay = (grad_a * a_swap).T
@@ -1158,12 +1264,13 @@
         grad_router.reshape(-1, experts // 2),
     )
 
-    own_conv, own_small = reduce_all(
+    own_conv, own_small, own_gate, own_out = reduce_all(
         sizes,
         (
             dot(normed_one.T, grad_conv_in).astype(jnp.bfloat16),
             jnp.concatenate(sums, axis=1).astype(jnp.bfloat16),
         ),
+        partial_sums,
         1,
     )
     own_x, own_dt, own_taps, own_bias, own_dtbias, own_decay, own_skip, own_gains, own_router = [

time: 443 us -> 395 us (0.89)
  Pallas kernels: 301 us -> 251 us
  local copies, waits for them, and re-layouts: 41.6 us -> 47.1 us
    pallas_call x3, Pallas kernels: 175 us -> 134 us  [the longest x1 65.5 us: scan_backward(): pl.pallas_call(functools.partial(backward_kernel, places, streams, len(la...]
    pallas_call x1, Pallas kernels: 55.5 us -> 41.6 us  [scan_forward(): pl.pallas_call(functools.partial(forward_kernel, places, streams, pick(ch...]
    pallas_call x1, Pallas kernels: 69.7 us -> 75.8 us  [run_experts(): pl.pallas_call(functools.partial(expert_kernel, slices), in_specs=[inside...]
    add x4 -> x1, other arithmetic: 7.49 us -> 2.98 us  [collect_slices(): values.astype(jnp.float32) + other]
    unnamed x141 -> x160, local copies, waits for them, and re-layouts: 10.6 us -> 12 us
  transfers between devices with their start and end apart: 11 -> 3, of which waited for: 2 -> 2; matrix products, arithmetic and copies ran while one was open for 15% -> 16% of each run, Pallas kernels for 13% -> 0%
where the time goes in v1:
time: 395 us; the launch traced here: 390 us
  Pallas kernels  251 us (64%)
  matrix products  50.3 us (13%)
  local copies, waits for them, and re-layouts  47.1 us (12%)
  other arithmetic  32.5 us (8%)
    pallas_call x1, Pallas kernels, run_experts(): pl.pallas_call(functools.partial(expert_kernel, slices), in_specs=[inside...  75.8 us
    pallas_call x1, Pallas kernels, scan_backward(): pl.pallas_call(functools.partial(backward_kernel, places, streams, len(la...  65.5 us
    pallas_call x1, Pallas kernels, scan_forward(): pl.pallas_call(functools.partial(forward_kernel, places, streams, pick(ch...  41.6 us
    pallas_call x1, Pallas kernels, gather_all(): pl.pallas_call(functools.partial(gather_kernel, places, streams, late, fa...  35.1 us
    pallas_call x1, Pallas kernels, reduce_all(): pl.pallas_call(functools.partial(reduce_kernel, places, streams, late, fa...  33.3 us
    dot_general x7, matrix products, dot(): return jnp.dot(left, right, preferred_element_type=jnp.float32)  21.4 us
    unnamed x160, local copies, waits for them, and re-layouts  12 us
    concatenate x6, local copies, waits for them, and re-layouts, body(): jnp.concatenate(sums, axis=1).astype(jnp.bfloat16)  11.1 us
  transfers between devices with their start and end apart: 3, of which 2 were waited for; matrix products, arithmetic and copies ran while one was open for 16% of the time, Pallas kernels for 0%

profile of v1, /device:TPU:0, one launch (start us, length us, event | category | flops | bytes accessed | tf_op | source)
XLA Modules:
  0.0 389.9 jit_solution(14778644726718848823)
XLA Ops:
  0.7 1.6 fusion.90
  10.7 1.5 concatenate.58.refs_1_
  12.2 35.1 %gather_all.1 = (bf16[2,2,2,2,2,24,1536]{6,5,4,3,2,1,0:T(8,128)(2,1)}, bf16[2,2,2,2,2,48,156]{6,5,4,3,2,1,0:T(8,128)(2,1)}, bf16[2,2,24,1536]{3,2,1,0:T(8,128)(2...) custom-call(bf16[24,1536]{1,0:T(8,128)(2,1)} %get-tuple-element.187.refs_0_, bf16[48,156]{1,0:T(8,128)(2,1)} %concatenate.58.refs_1_, ...), custom_call_target="tpu_custom_call" | custom-call | tf_op jit(solution)/shard_map/gather_all/pallas_call | solution.py:221
  47.3 1.1 collective-permute-start
  48.5 1.3 fusion.22
  49.7 1.3 slice_reduce_fusion.4
  51.0 1.3 fusion.89
  53.6 4.0 %convolution_convert_fusion.3 = bf16[384,1536]{1,0:T(8,128)(2,1)} fusion(bf16[768,1536]{1,0:T(8,128)(2,1)} %bitcast.130, bf16[1,384,768]{2,1,0:T(8,128)(2,1)S(1)} %copy-done.26, f32[768]{0:T(1024)S(1)} %reshape.354, f32[384]{0:T(512)S(1)} %fusion.74), kind=kOutput, calls=%fused_computation.12 | convolution fusion | flops 907739136 | bytes 4133376 | tf_op jit(solution)/shard_map/dot_general | solution.py:370
  58.1 1.5 slice_reduce_fusion.3
  60.3 1.6 maximum_convert_fusion
  62.8 3.7 multiply_convert_fusion.1
  70.3 4.7 %convert_multiply_fusion.3 = (f32[384,1536]{1,0:T(8,128)}, f32[384,1536]{1,0:T(8,128)}, f32[384,1536]{1,0:T(8,128)}) fusion(bf16[384,1536]{1,0:T(8,128)(2,1)S(1)} %get-tuple-element.173, pred[384]{0:T(512)(128)(4,1)S(1)} %get-tuple-element.197, f32[1536]{0:T(1024)S(1)} %get-tuple-element.156, bf16[1536,156]{1,0:T(8,128)(2,1)S(1)} %bitcast.127, ...), kind=kOutput, calls=%fused_computation.4 | convolution fusion | flops 62521344 | bytes 8696320 | tf_op jit(solution)/shard_map/dot_general | solution.py:1148
  76.1 41.6 %scan_forward.1 = (f32[384,1536]{1,0:T(8,128)S(1)}, f32[16,1536]{1,0:T(8,128)}, bf16[4,16,1536]{2,1,0:T(8,128)(2,1)S(1)}, bf16[385,16,1536]{2,1,0:T(8,128)(2,1)}...) custom-call(f32[384,1536]{1,0:T(8,128)} %get-tuple-element.181.refs_0_, ...), custom_call_target="tpu_custom_call" | custom-call | flops 84934656 | bytes 84934656 | tf_op jit(solution)/shard_map/scan_forward/pallas_call | solution.py:685
  117.8 2.7 multiply_convert_fusion
  120.8 1.2 multiply_reduce_fusion.6
  125.4 75.8 %run_experts.1 = (bf16[384,768]{1,0:T(8,128)(2,1)}, bf16[384,768]{1,0:T(8,128)(2,1)}, f32[768,768]{1,0:T(8,128)}, bf16[768,768]{1,0:T(8,128)(2,1)}, bf16[768,768]{1,0:T(8,128)(2,1)}) custom-call(bf16[384,768]{1,0:T(8,128)(2,1)} %copy-done.19, bf16[384,768]{1,0:T(8,128)(2,1)} %fusion.28.refs_1_, s32[384,1]{1,0:T(8,128)} %copy.116.refs_2_, ...), custom_call_target="tpu_custom_call" | custom-call | tf_op jit(solution)/shard_map/run_experts/pallas_call | solution.py:1011
  201.3 1.6 fusion.29
  203.0 2.8 multiply_reduce_fusion.4
  205.7 1.5 collective-permute-start.1
  207.2 1.3 convert_add_fusion.1
  209.4 6.1 %fusion.8 = (bf16[1536]{0:T(1024)(128)(2,1)}, f32[384,1536]{1,0:T(8,128)}, bf16[384,1536]{1,0:T(8,128)(2,1)}) fusion(bf16[384,1536]{1,0:T(8,128)(2,1)S(1)} %copy-done.14, f32[384,1536]{1,0:T(8,128)} %get-tuple-element.200, f32[384,1536]{1,0:T(8,128)S(1)} %copy-done.9, f32[1536]{0:T(1024)S(1)} %get-tuple-element.155, bf16[1536,768]{1,0:T(8,128)(2,1)S(1)} %bitcast.151, ...), kind=kOutput, calls=%fused_computation.22 | convolution fusion | flops 916879872 | bytes 12985344 | tf_op jit(solution)/shard_map/dot_general | solution.py:1206
  215.5 1.4 concatenate.79
  216.9 1.4 stack_reshape.9
  218.3 1.9 convolution_convert_fusion.7
  220.1 1.5 copy.124
  221.7 1.9 concatenate.74
  223.5 4.6 %convolution_convert_fusion.2 = bf16[768,1536]{1,0:T(8,128)(2,1)} fusion(bf16[384,1536]{1,0:T(8,128)(2,1)} %get-tuple-element.175, bf16[1,384,768]{2,1,0:T(8,128)(2,1)} %param.18, f32[768]{0:T(1024)} %copy-done.43, f32[384]{0:T(512)} %copy-done.67), kind=kOutput, calls=%fused_computation.9 | convolution fusion | flops 908328960 | bytes 4133376 | tf_op jit(solution)/shard_map/dot_general | solution.py:370
  228.1 2.8 convolution_convert_fusion.1
  230.9 2.1 fusion.93
  233.1 1.5 collective-permute-done.1
  234.6 3.0 convert_add_fusion
  237.6 65.5 %scan_backward.1 = (f32[384,1536]{1,0:T(8,128)}, f32[384,1536]{1,0:T(8,128)}, f32[6,8,1024]{2,1,0:T(8,128)}, f32[6,8,1024]{2,1,0:T(8,128)}, f32[16,1536]{1,0:T(8...) custom-call(f32[384,1536]{1,0:T(8,128)} %get-tuple-element.181.refs_0_, ...), custom_call_target="tpu_custom_call" | custom-call | flops 141557760 | bytes 141557760 | tf_op jit(solution)/shard_map/scan_backward/pallas_call | solution.py:791
  303.1 1.1 fusion.57
  304.8 4.2 %fusion.87 = (bf16[1536]{0:T(1024)(128)(2,1)S(1)}, bf16[384,1536]{1,0:T(8,128)(2,1)S(1)}) fusion(f32[384,1536]{1,0:T(8,128)} %get-tuple-element.198, f32[384,1536]{1,0:T(8,128)} %get-tuple-element.70, f32[384,1536]{1,0:T(8,128)} %get-tuple-element.69, bf16[384,1536]{1,0:T(8,128)(2,1)S(1)} %copy-done.15), kind=kLoop, calls=%fused_computation.185 | loop fusion | flops 5896704 | bytes 9440256 | tf_op jit(solution)/shard_map/reduce_sum | solution.py:1230
  310.6 6.0 %multiply_reduce_fusion.3 = (f32[1536]{0:T(1024)S(1)}, f32[1536]{0:T(1024)S(1)}, f32[1536]{0:T(1024)S(1)}, f32[1536]{0:T(1024)S(1)}, bf16[1536]{0:T(1024)(128)(2...) fusion(f32[387,1536]{1,0:T(8,128)S(1)} %copy-done.11, ...), kind=kOutput, calls=%fused_computation.28 | convolution fusion | flops 115192320 | bytes 28840960 | tf_op jit(solution)/shard_map/dot_general | solution.py:1241
  316.6 2.5 pad_add_fusion
  319.8 1.0 convolution_convert_fusion.4
  321.9 1.3 collective-permute-start.2
  324.2 1.9 copy.119
  326.0 1.9 copy.120
  328.9 1.5 concatenate.77
  330.3 1.4 concatenate.78
  332.8 4.2 %fusion.19 = (bf16[768]{0:T(1024)(128)(2,1)S(1)}, f32[384]{0:T(512)S(1)}, f32[384,768]{1,0:T(8,128)}) fusion(bf16[1,384,768]{2,1,0:T(8,128)(2,1)S(1)} %copy-done.28, f32[384]{0:T(512)S(1)} %copy-done.68, f32[768]{0:T(1024)S(1)} %copy-done.44, f32[384,768]{1,0:T(8,128)} %fusion.93, bf16[768,1536]{1,0:T(8,128)(2,1)} %bitcast.131, ...), kind=kOutput, calls=%fused_computation.60 | convolution fusion | flops 909507456 | bytes 7701504 | tf_op jit(solution)/shard_map/dot_general | solution.py:370
  337.5 4.7 %concatenate.75.refs_1_ = bf16[2,2,2,2,2,48,156]{6,5,4,3,2,1,0:T(8,128)(2,1)S(1)} concatenate(bf16[2,2,2,2,2,48,80]{6,5,4,3,2,1,0:T(8,128)(2,1)} %bitcast.137, bf16[2,2,2,2,2,48,48]{6,5,4,3,2,1,0:T(8,128)(2,1)} %bitcast.138, bf16[2,2,2,2,2,48,4]{6,5,4,3,2,1,0:T(8,128)(2,1)} %bitcast.139, bf16[2,2,2,2,2,48,1]{6,5,4,3,2,1,0:T(8,128)(2,1)} %concatenate.77, ...), dimensions={6} | concatenate | bytes 958464 | tf_op jit(solution)/shard_map/concatenate | solution.py:1271
  342.2 3.3 convolution_convert_fusion
  345.5 33.3 %reduce_all.1 = (f32[24,1536]{1,0:T(8,128)S(1)}, f32[48,156]{1,0:T(8,128)S(1)}, f32[24,1536]{1,0:T(8,128)S(1)}, f32[48,768]{1,0:T(8,128)S(1)}) custom-call(bf16[2,2,2,2,2,24,1536]{6,5,4,3,2,1,0:T(8,128)(2,1)S(1)} %bitcast.119, bf16[2,2,2,2,2,48,156]{6,5,4,3,2,1,0:T(8,128)(2,1)S(1)} %concatenate.75.refs_1_, bf16[2,2,24,1536]{3,2,1,0:T(8,128)(2,1)S(1)} %copy-done.1, ...), custom_call_target="tpu_custom_call" | custom-call | tf_op jit(solution)/shard_map/reduce_all/pallas_call | solution.py:356
  383.9 2.8 fusion.27
  388.0 1.4 copy.136
  (238 shorter events, 34.3 us)
Async XLA Ops:
  0.6 51.7 %copy-start.69 = (s32[1,384]{1,0:T(1,128)S(1)}, s32[1,384]{1,0:T(1,128)}, u32[]{:S(2)}) copy-start(s32[1,384]{1,0:T(1,128)} %param.19) | copy-start | bytes 4612
  10.7 42.9 %copy-start.26 = (bf16[1,384,768]{2,1,0:T(8,128)(2,1)S(1)}, bf16[1,384,768]{2,1,0:T(8,128)(2,1)}, u32[]{:S(2)}) copy-start(bf16[1,384,768]{2,1,0:T(8,128)(2,1)} %param.18) | copy-start | bytes 1769476
  47.3 6.2 %copy-start.40 = (bf16[16,896]{1,0:T(8,128)(2,1)S(1)}, bf16[16,896]{1,0:T(8,128)(2,1)}, u32[]{:S(2)}) copy-start(bf16[16,896]{1,0:T(8,128)(2,1)} %get-tuple-element.49) | copy-start | bytes 86020
  47.3 28.7 %collective-permute-start = (bf16[768,768]{1,0:T(8,128)(2,1)}, bf16[768,768]{1,0:T(8,128)(2,1)}, u32[]{:S(2)}, u32[]{:S(2)}) collective-permute-start(bf16[768,768]{1,0:T(8,128)(2,1)} %bitcast.141), channel_id=1, source_target_pairs={{0,16},{8,24},{16,0},{24,8},{1,17},{9,25},{17,1},{25,9},{2,18},{10... | collective-permute-start | bytes 3538952 | tf_op jit(solution)/shard_map/ppermute | solution.py:1049
  49.7 7.9 %copy-start.56 = (f32[384]{0:T(512)}, f32[384]{0:T(512)S(1)}, u32[]{:S(2)}) copy-start(f32[384]{0:T(512)S(1)} %fusion.22) | copy-start | bytes 4612
  53.2 155.4 %copy-start.59 = (f32[1536]{0:T(1024)}, f32[1536]{0:T(1024)S(1)}, u32[]{:S(2)}) copy-start(f32[1536]{0:T(1024)S(1)} %get-tuple-element.155) | copy-start | bytes 18436
  53.4 64.3 %copy-start.43 = (f32[768]{0:T(1024)}, f32[768]{0:T(1024)S(1)}, u32[]{:S(2)}) copy-start(f32[768]{0:T(1024)S(1)} %reshape.354) | copy-start | bytes 9220
  53.5 64.3 %copy-start.67 = (f32[384]{0:T(512)}, f32[384]{0:T(512)S(1)}, u32[]{:S(2)}) copy-start(f32[384]{0:T(512)S(1)} %fusion.74) | copy-start | bytes 4612
  59.6 6.9 %copy-start.47 = (f32[1536]{0:T(1024)}, f32[1536]{0:T(1024)S(1)}, u32[]{:S(2)}) copy-start(f32[1536]{0:T(1024)S(1)} %get-tuple-element.158) | copy-start | bytes 18436
  59.6 6.9 %copy-start.49 = (f32[1536]{0:T(1024)}, f32[1536]{0:T(1024)S(1)}, u32[]{:S(2)}) copy-start(f32[1536]{0:T(1024)S(1)} %get-tuple-element.159) | copy-start | bytes 18436
  59.6 6.9 %copy-start.51 = (f32[1536]{0:T(1024)}, f32[1536]{0:T(1024)S(1)}, u32[]{:S(2)}) copy-start(f32[1536]{0:T(1024)S(1)} %get-tuple-element.160) | copy-start | bytes 18436
  59.6 6.9 %copy-start.53 = (f32[1536]{0:T(1024)}, f32[1536]{0:T(1024)S(1)}, u32[]{:S(2)}) copy-start(f32[1536]{0:T(1024)S(1)} %get-tuple-element.161) | copy-start | bytes 18436
  66.5 8.5 %copy-start.12 = (bf16[384,1536]{1,0:T(8,128)(2,1)}, bf16[384,1536]{1,0:T(8,128)(2,1)S(1)}, u32[]{:S(2)}) copy-start(bf16[384,1536]{1,0:T(8,128)(2,1)S(1)} %get-tuple-element.173) | copy-start | bytes 3538948
  67.1 8.0 %copy-start.36 = (f32[384,80]{0,1:T(8,128)}, f32[384,80]{0,1:T(8,128)S(1)}, u32[]{:S(2)}) copy-start(f32[384,80]{0,1:T(8,128)S(1)} %fusion.38) | copy-start | bytes 368644
  69.2 5.9 %copy-start.38 = (bf16[1536,156]{0,1:T(8,128)(2,1)}, bf16[1536,156]{0,1:T(8,128)(2,1)S(1)}, u32[]{:S(2)}) copy-start(bf16[1536,156]{0,1:T(8,128)(2,1)S(1)} %copy.115) | copy-start | bytes 1437700
  70.3 5.7 %copy-start.4 = (f32[16,384]{1,0:T(8,128)}, f32[16,384]{1,0:T(8,128)S(1)}, u32[]{:S(2)}) copy-start(f32[16,384]{1,0:T(8,128)S(1)} %get-tuple-element.188.refs_3_.refs_4_) | copy-start | bytes 73732
  70.3 5.7 %copy-start.5 = (f32[16,384]{1,0:T(8,128)}, f32[16,384]{1,0:T(8,128)S(1)}, u32[]{:S(2)}) copy-start(f32[16,384]{1,0:T(8,128)S(1)} %get-tuple-element.189.refs_2_.refs_3_) | copy-start | bytes 73732
  70.3 5.7 %copy-start.6 = (bf16[2,2,24,1536]{3,2,1,0:T(8,128)(2,1)S(1)}, bf16[2,2,24,1536]{3,2,1,0:T(8,128)(2,1)}, u32[]{:S(2)}) copy-start(bf16[2,2,24,1536]{3,2,1,0:T(8,128)(2,1)} %get-tuple-element.55.refs_5_) | copy-start | bytes 884740
  70.3 5.7 %copy-start.7 = (bf16[2,2,48,768]{3,2,1,0:T(8,128)(2,1)S(1)}, bf16[2,2,48,768]{3,2,1,0:T(8,128)(2,1)}, u32[]{:S(2)}) copy-start(bf16[2,2,48,768]{3,2,1,0:T(8,128)(2,1)} %get-tuple-element.56.refs_6_) | copy-start | bytes 884740
  75.1 42.6 %copy-start = (f32[16,1536]{1,0:T(8,128)}, f32[16,1536]{1,0:T(8,128)S(1)}, u32[]{:S(2)}) copy-start(f32[16,1536]{1,0:T(8,128)S(1)} %bitcast_multiply_fusion.1.refs_4_.refs_5_) | copy-start | bytes 294916
  76.0 41.7 %copy-start.13 = (bf16[384,1536]{1,0:T(8,128)(2,1)S(1)}, bf16[384,1536]{1,0:T(8,128)(2,1)}, u32[]{:S(2)}) copy-start(bf16[384,1536]{1,0:T(8,128)(2,1)} %copy-done.12) | copy-start | bytes 3538948
  76.1 41.7 %copy-start.27 = (bf16[1,384,768]{2,1,0:T(8,128)(2,1)S(1)}, bf16[1,384,768]{2,1,0:T(8,128)(2,1)}, u32[]{:S(2)}) copy-start(bf16[1,384,768]{2,1,0:T(8,128)(2,1)} %param.18) | copy-start | bytes 1769476
  124.3 78.6 %copy-start.41 = (f32[384]{0:T(512)}, f32[384]{0:T(512)S(1)}, u32[]{:S(2)}) copy-start(f32[384]{0:T(512)S(1)} %get-tuple-element.203) | copy-start | bytes 4612
  124.4 78.6 %copy-start.42 = (f32[384]{0:T(512)}, f32[384]{0:T(512)S(1)}, u32[]{:S(2)}) copy-start(f32[384]{0:T(512)S(1)} %fusion.70) | copy-start | bytes 4612
  201.2 6.0 %copy-start.18 = (f32[384,768]{1,0:T(8,128)S(1)}, f32[384,768]{1,0:T(8,128)}, u32[]{:S(2)}) copy-start(f32[384,768]{1,0:T(8,128)} %copy-done.17) | copy-start | bytes 3538948
  201.2 6.0 %copy-start.22 = (bf16[1,384,768]{2,1,0:T(8,128)(2,1)S(1)}, bf16[1,384,768]{2,1,0:T(8,128)(2,1)}, u32[]{:S(2)}) copy-start(bf16[1,384,768]{2,1,0:T(8,128)(2,1)} %param.21) | copy-start | bytes 1769476
  201.3 5.9 %copy-start.30 = (bf16[384,768]{1,0:T(8,128)(2,1)S(1)}, bf16[384,768]{1,0:T(8,128)(2,1)}, u32[]{:S(2)}) copy-start(bf16[384,768]{1,0:T(8,128)(2,1)} %get-tuple-element.62) | copy-start | bytes 1769476
  202.9 5.6 %copy-start.45 = (f32[384]{0:T(512)}, f32[384]{0:T(512)S(1)}, u32[]{:S(2)}) copy-start(f32[384]{0:T(512)S(1)} %fusion.29) | copy-start | bytes 4612
  202.9 5.6 %copy-start.55 = (f32[384]{0:T(512)}, f32[384]{0:T(512)S(1)}, u32[]{:S(2)}) copy-start(f32[384]{0:T(512)S(1)} %fusion.64) | copy-start | bytes 4612
  205.7 28.9 %collective-permute-start.1 = (bf16[768,768]{1,0:T(8,128)(2,1)}, bf16[768,768]{1,0:T(8,128)(2,1)}, u32[]{:S(2)}, u32[]{:S(2)}) collective-permute-start(bf16[768,768]{1,0:T(8,128)(2,1)} %get-tuple-element.65), channel_id=1, source_target_pairs={{0,16},{8,24},{16,0},{24,8},{1,17},{9,25},{17,1},{25,9},{2,18},{10... | collective-permute-start | bytes 3538952 | tf_op jit(solution)/shard_map/ppermute | solution.py:1049
  208.5 7.0 %copy-start.23 = (f32[384,768]{1,0:T(8,128)}, f32[384,768]{1,0:T(8,128)S(1)}, u32[]{:S(2)}) copy-start(f32[384,768]{1,0:T(8,128)S(1)} %get-tuple-element.182) | copy-start | bytes 3538948
  237.6 67.1 %copy-start.15 = (bf16[384,1536]{1,0:T(8,128)(2,1)S(1)}, bf16[384,1536]{1,0:T(8,128)(2,1)}, u32[]{:S(2)}) copy-start(bf16[384,1536]{1,0:T(8,128)(2,1)} %copy-done.12) | copy-start | bytes 3538948
  304.7 5.9 %copy-start.34 = (f32[384,1536]{1,0:T(8,128)S(1)}, f32[384,1536]{1,0:T(8,128)}, u32[]{:S(2)}) copy-start(f32[384,1536]{1,0:T(8,128)} %get-tuple-element.69) | copy-start | bytes 7077892
  304.7 5.8 %copy-start.48 = (f32[1536]{0:T(1024)S(1)}, f32[1536]{0:T(1024)}, u32[]{:S(2)}) copy-start(f32[1536]{0:T(1024)} %copy-done.47) | copy-start | bytes 18436
  304.7 5.8 %copy-start.50 = (f32[1536]{0:T(1024)S(1)}, f32[1536]{0:T(1024)}, u32[]{:S(2)}) copy-start(f32[1536]{0:T(1024)} %copy-done.49) | copy-start | bytes 18436
  304.7 5.8 %copy-start.52 = (f32[1536]{0:T(1024)S(1)}, f32[1536]{0:T(1024)}, u32[]{:S(2)}) copy-start(f32[1536]{0:T(1024)} %copy-done.51) | copy-start | bytes 18436
  304.8 5.8 %copy-start.54 = (f32[1536]{0:T(1024)S(1)}, f32[1536]{0:T(1024)}, u32[]{:S(2)}) copy-start(f32[1536]{0:T(1024)} %copy-done.53) | copy-start | bytes 18436
  304.8 5.8 %copy-start.60 = (f32[1536]{0:T(1024)S(1)}, f32[1536]{0:T(1024)}, u32[]{:S(2)}) copy-start(f32[1536]{0:T(1024)} %copy-done.59) | copy-start | bytes 18436
  304.8 5.8 %copy-start.62 = (f32[384]{0:T(512)S(1)}, f32[384]{0:T(512)}, u32[]{:S(2)}) copy-start(f32[384]{0:T(512)} %copy-done.61) | copy-start | bytes 4612
  304.8 5.8 %copy-start.64 = (f32[384]{0:T(512)S(1)}, f32[384]{0:T(512)}, u32[]{:S(2)}) copy-start(f32[384]{0:T(512)} %copy-done.63) | copy-start | bytes 4612
  304.8 5.8 %copy-start.66 = (f32[384]{0:T(512)S(1)}, f32[384]{0:T(512)}, u32[]{:S(2)}) copy-start(f32[384]{0:T(512)} %copy-done.65) | copy-start | bytes 4612
  320.9 11.9 %copy-start.28 = (bf16[1,384,768]{2,1,0:T(8,128)(2,1)S(1)}, bf16[1,384,768]{2,1,0:T(8,128)(2,1)}, u32[]{:S(2)}) copy-start(bf16[1,384,768]{2,1,0:T(8,128)(2,1)} %param.18) | copy-start | bytes 1769476
  320.9 11.9 %copy-start.29 = (f32[387,1536]{1,0:T(8,128)S(1)}, f32[387,1536]{1,0:T(8,128)}, u32[]{:S(2)}) copy-start(f32[387,1536]{1,0:T(8,128)} %pad_add_fusion) | copy-start | bytes 7133188
  320.9 11.9 %copy-start.44 = (f32[768]{0:T(1024)S(1)}, f32[768]{0:T(1024)}, u32[]{:S(2)}) copy-start(f32[768]{0:T(1024)} %copy-done.43) | copy-start | bytes 9220
  320.9 11.9 %copy-start.68 = (f32[384]{0:T(512)S(1)}, f32[384]{0:T(512)}, u32[]{:S(2)}) copy-start(f32[384]{0:T(512)} %copy-done.67) | copy-start | bytes 4612
  321.9 10.9 %collective-permute-start.2 = (f32[3,1536]{1,0:T(4,128)}, f32[3,1536]{1,0:T(4,128)S(1)}, u32[]{:S(2)}, u32[]{:S(2)}) collective-permute-start(f32[3,1536]{1,0:T(4,128)} %pad_add_fusion.1), channel_id=1, source_target_pairs={{8,0},{16,8},{24,16},{9,1},{17,9},{25,17},{10,2},{18,10},{26,18},{... | collective-permute-start | bytes 55304 | tf_op jit(solution)/shard_map/ppermute | solution.py:48
  345.4 35.7 %copy-start.57 = (f32[384]{0:T(512)S(1)}, f32[384]{0:T(512)}, u32[]{:S(2)}) copy-start(f32[384]{0:T(512)} %copy-done.56) | copy-start | bytes 4612
  345.4 38.4 %copy-start.25 = (f32[384,768]{1,0:T(8,128)S(1)}, f32[384,768]{1,0:T(8,128)}, u32[]{:S(2)}) copy-start(f32[384,768]{1,0:T(8,128)} %copy-done.23) | copy-start | bytes 3538948
  (30 other events, 104.4 us)

commit v2 on v1

--- a/solution.py
+++ b/solution.py
@@ -40,12 +40,6 @@
 
 def pick(channels):
     return 512 if channels % 512 == 0 else 128
-
-
-def shifted(value, axis, steps):
-    count = lax.axis_size(axis)
-    initial, last = (max(0, -steps), min(count, count - steps))
-    return lax.ppermute(value, axis, [(source, source + steps) for source in range(initial, last)])
 
 
 def rms_scale(values, gain):
@@ -320,50 +314,6 @@
 def flights(streams):
     shape = (len(streams), max(len(order) for array, cols, order in streams))
     return [pltpu.SemaphoreType.DMA(shape)] * 2
-
-
-def reduce_kernel(places, streams, late, far, count, extra, marks, *refs):
-    both = count + extra
-    parts, totals, scratch = refs[:both], refs[both : 2 * both], refs[2 * both :]
-    landing, late_landing = scratch[: marks[0]], scratch[marks[0] : marks[1]]
-    send_sems, recv_sems, late_send, late_recv = scratch[marks[1] :]
-    flow = ReduceFlow(
-        places, streams, range(len(places)), parts[:count], totals[:count], landing, send_sems, recv_sems
-    )
-    rest = ReduceFlow(places, late, far, parts[count:], totals[count:], late_landing, late_send, late_recv)
-    meet(places)
-    flow.start()
-    rest.start()
-    for stage in range(len(places)):
-        flow.advance(stage)
-        rest.advance(stage)
-    flow.finish()
-    rest.finish()
-
-
-def reduce_all(sizes, parts, extra, identity):
-    places = bit_positions(sizes)
-    stages = len(places)
-    far = sorted(far_of(places))
-    streams = halves(parts, *[tuple(order) for order in orders_of(places)])
-    late = [(k, slice(0, part.shape[-1]), tuple(far_of(places))) for k, part in enumerate(extra)]
-    divided = [part.reshape((2,) * stages + (-1, part.shape[1])) for part in parts]
-    inside = pl.BlockSpec(memory_space=pltpu.VMEM)
-    landing = landing_of(streams, range(stages), divided)
-    late_landing = landing_of(late, far, extra)
-    marks = len(landing), len(landing) + len(late_landing)
-    total = len(parts) + len(extra)
-    return pl.pallas_call(
-        functools.partial(reduce_kernel, places, streams, late, far, len(parts), len(extra), marks),
-        in_specs=[inside] * total,
-        out_specs=[inside] * total,
-        out_shape=[jax.ShapeDtypeStruct(block.shape[-2:], jnp.float32) for block in divided + list(extra)],
-        scratch_shapes=landing + late_landing + flights(streams) + flights(late),
-        compiler_params=pltpu.CompilerParams(
-            collective_id=identity, has_side_effects=True, vmem_limit_bytes=48 * 1024 * 1024
-        ),
-        name="reduce_all",
-    )(*divided, *extra)
 
 
 def dot(left, right):
@@ -820,6 +770,343 @@
     return along, slope, grad_bs, grad_cs, grad_a, out[5:7]
 
 
+class PackedReduce(ReduceFlow):
+    def __init__(self, places, streams, heads, parts, totals, landing, blocks, send_sems, recv_sems):
+        super().__init__(places, streams, range(len(places)), parts, totals, landing, send_sems, recv_sems)
+        self.heads, self.blocks = heads, blocks
+
+    def side(self, number, stage, value):
+        array, cols, order = self.streams[number]
+        if stage == 0:
+            index = tuple(value if p == order[0] else slice(None) for p in range(self.heads))
+            return self.parts[array].at[index + (slice(None), cols)]
+        left = [p for p in self.dims if p not in order[:stage]]
+        index = tuple(value if p == order[stage] else slice(None) for p in left)
+        held = self.blocks[number] if stage == 1 else self.spot(number, stage - 1)
+        return held.at[index]
+
+    def advance(self, stage):
+        if stage:
+            super().advance(stage)
+            return
+        for number, (array, cols, order) in enumerate(self.streams):
+            self.flight(number, 0).wait_recv()
+            mine = self.side(number, 0, self.bits[order[0]])
+            there, held = self.spot(number, 0), self.blocks[number]
+            tails = len(self.places) - self.heads
+            size = held.shape[-2]
+
+            def add(index, unused, mine=mine, there=there, held=held, tails=tails, size=size):
+                at = tuple(lax.rem(index // 2 ** (self.heads - 2 - k), 2) for k in range(self.heads - 1))
+                value = there[at].astype(jnp.float32) + mine[at].astype(jnp.float32)
+                for block in range(2**tails):
+                    spot = tuple(block // 2 ** (tails - 1 - k) % 2 for k in range(tails))
+                    held[at + spot] = value[block * size : (block + 1) * size].astype(held.dtype)
+                return unused
+
+            lax.fori_loop(0, 2 ** (self.heads - 1), add, 0)
+            self.flight(number, 1).start()
+
+
+def turned(values):
+    return jnp.concatenate([values[:, at : at + LANES].T for at in range(0, values.shape[1], LANES)], axis=0)
+
+
+def finish_kernel(places, streams, third, late, far, marks, *refs):
+    (along_h, slope_h, grad_h, pre_h, conv_h, xs_h, ext_h, gz_h, wc_h, wg_h) = refs[:10]
+    (normed_ref, in_ref, resid_ref, mix_ref, bc_ref, delta_ref, same_ref, chan_ref, decay_ref, wide_ref) = refs[10:20]
+    rest_parts = refs[20:22]
+    (gi_ref, own_conv, own_gate, own_out, own_x, own_dt, own_taps, own_decay, own_rows, own_pair, own_router) = refs[22:33]
+    scratch = refs[33:]
+    landing, scratch = scratch[: marks[0]], scratch[marks[0] :]
+    blocks, scratch = scratch[: marks[1]], scratch[marks[1] :]
+    landing3, scratch = scratch[: marks[2]], scratch[marks[2] :]
+    blocks3, scratch = scratch[: marks[3]], scratch[marks[3] :]
+    late_landing, scratch = scratch[: marks[4]], scratch[marks[4] :]
+    (along, slope, grad, pre, conv, xs, ext, gz, wc, wg, gdt, gci, last, spill, arrived, sums, rows_s, wide_s, gn,
+     part_conv, part_small, part_wide, tot_small, tot_wide,
+     block_sems, whole_sems, spill_sems, send_sems, recv_sems, send3, recv3, late_send, late_recv) = scratch
+    tokens, channels = xs.shape
+    span = tokens // block_sems.shape[1]
+    heads = len([place for place in places if place[0] == "ctx"])
+    flow = PackedReduce(
+        places, streams, heads, (part_conv, part_small), (own_conv, tot_small), landing, blocks, send_sems, recv_sems
+    )
+    flow3 = PackedReduce(places, third, heads, (part_wide,), (tot_wide,), landing3, blocks3, send3, recv3)
+    rest = ReduceFlow(places, late, far, rest_parts, (own_gate, own_out), late_landing, late_send, late_recv)
+
+    streamed = ((along_h, along), (slope_h, slope), (grad_h, grad), (pre_h, pre), (xs_h, xs))
+
+    def block_copy(k, number):
+        rows = pl.ds(number * span, span)
+        source, target = streamed[k]
+        return pltpu.make_async_copy(source.at[rows], target.at[rows], block_sems.at[k, number])
+
+    for number in range(tokens // span):
+        for k in range(len(streamed)):
+            block_copy(k, number).start()
+    wholes = [
+        pltpu.make_async_copy(source, target, whole_sems.at[k])
+        for k, (source, target) in enumerate(((conv_h, conv), (ext_h, ext), (gz_h, gz), (wc_h, wc), (wg_h, wg)))
+    ]
+    for copy in wholes:
+        copy.start()
+    count = lax.axis_size("ctx")
+    here, line = lax.axis_index("ctx"), lax.axis_index("exp")
+    before = (lax.rem(here + count - 1, count), line)
+    meet(places, before, (lax.rem(here + 1, count), line))
+    rest.start()
+
+    sums[...] = jnp.zeros_like(sums)
+    rows_s[...] = jnp.zeros_like(rows_s)
+
+    def first_block(number, unused):
+        for k in range(len(streamed)):
+            block_copy(k, number).wait()
+
+        def some(index, unused_inner):
+            at = pl.ds(pl.multiple_of(number * span + index * 16, 16), 16)
+            for low in range(0, channels, LANES):
+                lanes = slice(low, low + LANES)
+                a, g, x, p = along[at, lanes], grad[at, lanes], xs[at, lanes].astype(jnp.float32), pre[at, lanes]
+                small = jnp.exp(-jnp.abs(p))
+                gated = jnp.where(p >= 0, 1.0, small) / (1.0 + small)
+                step = jnp.maximum(p, 0.0) + jnp.log1p(small)
+                value = (a * x + slope[at, lanes] * (1.0 / LOG2E)) * gated
+                gdt[at, lanes] = value.astype(jnp.bfloat16)
+                sums[0, :, lanes] += value[:8] + value[8:]
+                both = g * x
+                sums[1, :, lanes] += both[:8] + both[8:]
+                along[at, lanes] = chan_ref[4:5, lanes] * g + a * step
+            return unused_inner
+
+        lax.fori_loop(0, span // 16, some, 0)
+        return unused
+
+    lax.fori_loop(0, tokens // span, first_block, 0)
+    rows_s[25:26, :] = jnp.sum(sums[0], axis=0, keepdims=True)
+    rows_s[26:27, :] = jnp.sum(sums[1], axis=0, keepdims=True)
+    rows_s[8:24, :] = decay_ref[...]
+
+    lane = lax.broadcasted_iota(jnp.int32, (tokens, LANES), 1)
+    mixed = pltpu.roll(dot(gdt[...], mix_ref[...]), R, 1)
+    projected = jnp.where(lane < R, mixed, jnp.where(lane < R + 2 * NS, bc_ref[...], 0.0)).astype(jnp.bfloat16)
+    wholes[0].wait()
+    wholes[1].wait()
+    piece = 2 * LANES
+    tail_row = lax.broadcasted_iota(jnp.int32, (tokens, piece), 0)
+
+    def conv_piece(index, unused):
+        lanes = pl.ds(pl.multiple_of(index * piece, piece), piece)
+        some = pl.ds(pl.multiple_of(index * piece, piece), piece)
+        total = along[:, lanes] + contract(projected, mix_ref[some, :], 1, 1)
+        value = conv[:, lanes]
+        gate = 1.0 / (1.0 + jnp.exp(-value))
+        out = total * gate * (1.0 + value * (1.0 - gate))
+        rows_s[24:25, lanes] = jnp.sum(out, axis=0, keepdims=True)
+        before_rows = ext[:, lanes].astype(jnp.float32)
+        rows_s[3:4, lanes] = jnp.sum(out * before_rows[EDGE:], axis=0, keepdims=True)
+        result = chan_ref[3:4, lanes] * out
+        beyond = jnp.zeros((8, piece), jnp.float32)
+        for j in range(1, KC):
+            same = jnp.concatenate([same_ref[j - 1]] * 2, axis=1)
+            masked = out * same
+            shifted_rows = pltpu.roll(before_rows, j, 0)[EDGE:]
+            rows_s[3 - j : 4 - j, lanes] = jnp.sum(masked * shifted_rows, axis=0, keepdims=True)
+            moved = chan_ref[3 - j : 4 - j, lanes] * pltpu.roll(masked, tokens - j, 0)
+            result = result + jnp.where(tail_row < tokens - j, moved, 0.0)
+            beyond = beyond + jnp.where(tail_row < tokens - j, 0.0, moved)[tokens - 8 :]
+        gci[:, lanes] = result.astype(jnp.bfloat16)
+        last[:, lanes] = result[tokens - 16 :]
+        spill[:, lanes] = beyond
+        return unused
+
+    lax.fori_loop(0, channels // piece, conv_piece, 0)
+    handed = pltpu.make_async_remote_copy(
+        src_ref=spill,
+        dst_ref=arrived,
+        send_sem=spill_sems.at[0],
+        recv_sem=spill_sems.at[1],
+        device_id=before,
+        device_id_type=MESH,
+    )
+    handed.start()
+
+    cut = part_small.shape[-2]
+    for index in range(channels // cut):
+        spot = tuple(index // 2 ** (heads - 1 - k) % 2 for k in range(heads))
+        if cut % LANES == 0:
+            some = slice(index * cut, (index + 1) * cut)
+            value = contract(xs[:, some], projected, 0, 0) + contract(gdt[:, some], delta_ref[...], 0, 0)
+        else:
+            pair = slice(index // 2 * 2 * cut, (index // 2 * 2 + 2) * cut)
+            value = contract(xs[:, pair], projected, 0, 0) + contract(gdt[:, pair], delta_ref[...], 0, 0)
+            value = value[index % 2 * cut : (index % 2 + 1) * cut]
+        part_small[spot + (slice(None), slice(0, LANES))] = value.astype(jnp.bfloat16)
+    columns = turned(jnp.concatenate([rows_s[...], jnp.zeros((LANES - rows_s.shape[0], channels), jnp.float32)], axis=0))
+    for index in range(channels // cut):
+        spot = tuple(index // 2 ** (heads - 1 - k) % 2 for k in range(heads))
+        part_small[spot + (slice(None), slice(LANES, 2 * LANES))] = columns[index * cut : (index + 1) * cut].astype(jnp.bfloat16)
+
+    handed.wait_recv()
+    closing = last[...] + jnp.concatenate([jnp.zeros((8, channels), jnp.float32), arrived[...]], axis=0)
+    gci[tokens - 16 :, :] = closing.astype(jnp.bfloat16)
+
+    long = part_conv.shape[-2]
+
+    def product_piece(index, unused):
+        lanes = pl.ds(pl.multiple_of(index * piece, piece), piece)
+        value = contract(normed_ref[...], gci[:, lanes], 0, 0)
+        for block in range(value.shape[0] // long):
+            spot = tuple(block // 2 ** (heads - 1 - k) % 2 for k in range(heads))
+            part_conv[spot + (slice(None), lanes)] = value[block * long : (block + 1) * long].astype(jnp.bfloat16)
+        return unused
+
+    lax.fori_loop(0, channels // piece, product_piece, 0)
+    flow.start()
+
+    for copy in wholes[2:]:
+        copy.wait()
+    width = gn.shape[1]
+
+    def normed_piece(index, unused):
+        lanes = pl.ds(pl.multiple_of(index * piece, piece), piece)
+        gn[:, lanes] = contract(gci[...], wc[lanes, :], 1, 1) + contract(gz[...], wg[lanes, :], 1, 1)
+        return unused
+
+    lax.fori_loop(0, width // piece, normed_piece, 0)
+    wide_s[...] = wide_ref[...]
+    gain = wide_ref[0:1, :]
+
+    def back(index, total):
+        at = pl.ds(pl.multiple_of(index * 16, 16), 16)
+        x, g = in_ref[at, :].astype(jnp.float32), gn[at, :]
+        scale = lax.rsqrt(jnp.mean(x * x, axis=-1, keepdims=True) + EPS)
+        scaled = g * gain
+        share_of = jnp.mean(x * scaled, axis=-1, keepdims=True)
+        gi_ref[at, :] = resid_ref[at, :] + scale * scaled - x * (scale * scale * scale * share_of)
+        value = g * (x * scale)
+        return total + value[:8] + value[8:]
+
+    total = lax.fori_loop(0, tokens // 16, back, jnp.zeros((8, width), jnp.float32))
+    wide_s[0:1, :] = jnp.sum(total, axis=0, keepdims=True)
+    flow.advance(0)
+    filler = jnp.zeros((LANES - wide_s.shape[0], width), jnp.float32)
+    columns = turned(jnp.concatenate([wide_s[...], filler], axis=0))
+    short = part_wide.shape[-2]
+    for block in range(width // short):
+        spot = tuple(block // 2 ** (heads - 1 - k) % 2 for k in range(heads))
+        part_wide[spot] = columns[block * short : (block + 1) * short].astype(jnp.bfloat16)
+    flow3.start()
+    rest.advance(0)
+    for stage in range(1, len(places)):
+        flow.advance(stage)
+        flow3.advance(stage - 1)
+        rest.advance(stage)
+    flow3.advance(len(places) - 1)
+
+    def columns_of(values):
+        return jnp.concatenate([values, jnp.zeros((LANES - values.shape[0], LANES), jnp.float32)], axis=0).T
+
+    size = tot_small.shape[0]
+    first, second, wide = tot_small[:, :LANES], tot_small[:, LANES:], tot_wide[...]
+    own_x[...] = first[:, : R + 2 * NS]
+    own_dt[...] = columns_of(first)[R + 2 * NS :, :size]
+    own_taps[...] = second[:, :KC]
+    own_decay[...] = pltpu.roll(second, LANES - 8, 1)[:, :NS]
+    own_rows[...] = columns_of(second)[24:32, :size]
+    own_pair[...] = columns_of(wide)[0:8, : wide.shape[0]]
+    own_router[...] = pltpu.roll(wide, LANES - 8, 1)[:, : own_router.shape[1]]
+    flow.finish()
+    flow3.finish()
+    rest.finish()
+    handed.wait_send()
+
+
+def finish(sizes, streamed, inside_values, parts, experts, identity, span=64):
+    places = bit_positions(sizes)
+    stages = len(places)
+    far = sorted(far_of(places))
+    heads = sizes[0][1].bit_length() - 1
+    tails = stages - heads
+    along, slope, grad, pre, conv, xs, ext, gz, wc, wg = streamed
+    normed = inside_values[0]
+    tokens, channels = xs.shape
+    width = normed.shape[1]
+    devices = 2**stages
+    half, wide = jnp.bfloat16, jnp.float32
+    rows, thin = channels // devices, width // devices
+    orders = [tuple(order) for order in orders_of(places)]
+    conv_like = jax.ShapeDtypeStruct((width, channels), half)
+    small_like = jax.ShapeDtypeStruct((channels, 2 * LANES), half)
+    wide_like = jax.ShapeDtypeStruct((width, LANES), half)
+    streams = halves((conv_like, small_like), *orders)
+    third = halves((wide_like,), *orders)
+    late = [(k, slice(0, part.shape[-1]), tuple(far_of(places))) for k, part in enumerate(parts)]
+
+    def room(of, sizes_of):
+        landing, blocks = [], []
+        for array, cols, order in of:
+            size, many = sizes_of[array], cols.stop - cols.start
+            landing.append(pltpu.VMEM((2,) * (heads - 1) + (size * 2**tails, many), half))
+            landing += [pltpu.VMEM((2,) * (stages - stage - 1) + (size, many), half) for stage in range(1, stages)]
+            blocks.append(pltpu.VMEM((2,) * (stages - 1) + (size, many), half))
+        return landing, blocks
+
+    landing, blocks = room(streams, (thin, rows))
+    landing3, blocks3 = room(third, (thin,))
+    late_landing = landing_of(late, far, parts)
+    marks = [len(landing), len(blocks), len(landing3), len(blocks3), len(late_landing)]
+    inside = pl.BlockSpec(memory_space=pltpu.VMEM)
+    anywhere = pl.BlockSpec(memory_space=pl.ANY)
+    return pl.pallas_call(
+        functools.partial(finish_kernel, places, streams, third, late, far, marks),
+        in_specs=[anywhere] * 10 + [inside] * (len(inside_values) + 2),
+        out_specs=[inside] * 11,
+        out_shape=[
+            jax.ShapeDtypeStruct(normed.shape, wide),
+            jax.ShapeDtypeStruct((thin, channels), wide),
+            jax.ShapeDtypeStruct(parts[0].shape[-2:], wide),
+            jax.ShapeDtypeStruct(parts[1].shape[-2:], wide),
+            jax.ShapeDtypeStruct((rows, R + 2 * NS), wide),
+            jax.ShapeDtypeStruct((R, rows), wide),
+            jax.ShapeDtypeStruct((rows, KC), wide),
+            jax.ShapeDtypeStruct((rows, NS), wide),
+            jax.ShapeDtypeStruct((8, rows), wide),
+            jax.ShapeDtypeStruct((8, thin), wide),
+            jax.ShapeDtypeStruct((thin, experts), wide),
+        ],
+        scratch_shapes=landing + blocks + landing3 + blocks3 + late_landing
+        + [pltpu.VMEM(value.shape, value.dtype) for value in streamed]
+        + [
+            pltpu.VMEM((tokens, channels), half),
+            pltpu.VMEM((tokens, channels), half),
+            pltpu.VMEM((16, channels), wide),
+            pltpu.VMEM((8, channels), wide),
+            pltpu.VMEM((8, channels), wide),
+            pltpu.VMEM((2, 8, channels), wide),
+            pltpu.VMEM((32, channels), wide),
+            pltpu.VMEM(inside_values[-1].shape, wide),
+            pltpu.VMEM((tokens, width), wide),
+            pltpu.VMEM((2,) * heads + (thin * 2**tails, channels), half),
+            pltpu.VMEM((2,) * heads + (rows * 2**tails, 2 * LANES), half),
+            pltpu.VMEM((2,) * heads + (thin * 2**tails, LANES), half),
+            pltpu.VMEM((rows, 2 * LANES), wide),
+            pltpu.VMEM((thin, LANES), wide),
+            pltpu.SemaphoreType.DMA((5, tokens // span)),
+            pltpu.SemaphoreType.DMA((5,)),
+            pltpu.SemaphoreType.DMA((2,)),
+        ]
+        + flights(streams)
+        + flights(third)
+        + flights(late),
+        compiler_params=pltpu.CompilerParams(
+            collective_id=identity, has_side_effects=True, vmem_limit_bytes=56 * 1024 * 1024
+        ),
+        name="finish",
+    )(*streamed, *inside_values, *parts)
+
+
 def expert_kernel(slices, *refs):
     tokens_ref, grads_ref, column_ref, row_ref = refs[:4]
     even = range(0, slices, 2)
@@ -1090,56 +1377,57 @@
 ):
     experts = router.shape[1]
     half_rows = norm_gain.shape[0]
-    columns = (
-        x_proj,
-        dt_proj.T,
-        conv_taps,
-        conv_bias[:, None],
-        dt_bias[:, None],
-        log_decay,
-        skip_gain[:, None],
-        jnp.concatenate([norm_gain, moe_gain])[:, None],
-        router.reshape(2 * half_rows, experts // 2),
-    )
-    widths = [part.shape[1] for part in columns]
-    ends = [sum(widths[: k + 1]) for k in range(len(widths))]
+    half = jnp.bfloat16
+    channel_part = jnp.concatenate(
+        [
+            x_proj,
+            dt_proj.T,
+            conv_taps,
+            jnp.zeros((2 * half_rows, 4), half),
+            log_decay,
+            jnp.stack([conv_bias, dt_bias, skip_gain], axis=1),
+            jnp.zeros((2 * half_rows, LANES - 27), half),
+        ],
+        axis=1,
+    )
+    width_part = jnp.concatenate(
+        [
+            jnp.stack([norm_gain, moe_gain], axis=1),
+            jnp.zeros((half_rows, 6), half),
+            router,
+            jnp.zeros((half_rows, LANES - 8 - experts), half),
+        ],
+        axis=1,
+    )
     sizes = [(name, lax.axis_size(name)) for name in ("ctx", "exp")]
     tail_ids = segments[0, -EDGE:, None].astype(jnp.bfloat16)
     edge = jnp.concatenate([inputs[0, -EDGE:], jnp.broadcast_to(tail_ids, (EDGE, LANES))], axis=1)
-    (full_conv, full_small), partial, prior = gather_all(
-        sizes, (in_proj[:, :DI], jnp.concatenate(columns, axis=1)), (in_proj[:, DI:], out_proj), edge, 0
-    )
-    later_in, full_small = lax.optimization_barrier((expert_in[0], full_small))
+    (full_conv, full_channel, full_width), partial, prior = gather_all(
+        sizes, (in_proj[:, :DI], channel_part, width_part), (in_proj[:, DI:], out_proj), edge, 0
+    )
+    later_in, full_channel = lax.optimization_barrier((expert_in[0], full_channel))
     weights_in = spread_slices(later_in)
-    full_xproj, full_dt, full_taps, full_bias, full_dtbias, full_decay, full_skip, gains, full_router = [
-        full_small[:, end - width : end] for end, width in zip(ends, widths)
-    ]
-    full_dt = full_dt.T
-    full_bias, full_dtbias, full_skip = full_bias[:, 0], full_dtbias[:, 0], full_skip[:, 0]
-    gains = gains.reshape(-1, 2, half_rows)
-    full_norm, full_moe = gains[:, 0].reshape(-1), gains[:, 1].reshape(-1)
-    full_router = full_router.reshape(-1, experts)
+    mix = full_channel[:, :LANES]
+    full_xproj, full_dt = mix[:, : R + 2 * NS], mix[:, R + 2 * NS :].T
+    by_channel = full_channel[:, LANES:].T
+    full_taps, full_decay = by_channel[:KC].T, by_channel[8 : 8 + NS].T
+    full_bias, full_dtbias, full_skip = by_channel[24], by_channel[25], by_channel[26]
+    full_norm, full_moe, full_router = full_width[:, 0], full_width[:, 1], full_width[:, 8 : 8 + experts]
     tokens_here = inputs.shape[1]
     capacity = 5 * tokens_here // (4 * experts)
     flat_in = inputs[0].astype(jnp.float32)
     seg_row = segments[0]
     position = lax.axis_index("ctx")
-    norm_one_value, norm_one_pull = jax.vjp(rms_scale, flat_in, full_norm.astype(jnp.float32))
-    normed_one = norm_one_value.astype(jnp.bfloat16)
+    normed_one = rms_scale(flat_in, full_norm.astype(jnp.float32)).astype(jnp.bfloat16)
     conv_in = dot(normed_one, full_conv).astype(jnp.bfloat16)
     edge_one = rms_scale(prior[:, :D].astype(jnp.float32), full_norm.astype(jnp.float32)).astype(jnp.bfloat16)
-    edge_rows = dot(edge_one, full_conv)[EDGE - (KC - 1) :].astype(jnp.bfloat16)
+    edge_all = dot(edge_one, full_conv).astype(jnp.bfloat16)
+    edge_rows = edge_all[EDGE - (KC - 1) :]
     prior_ids = jnp.where(position > 0, prior[EDGE - (KC - 1) :, D].astype(jnp.int32), -1)
     ext_ids = jnp.concatenate([prior_ids, seg_row])
     ext_rows = jnp.concatenate([edge_rows, conv_in], axis=0).astype(jnp.float32)
-    conv_out, conv_pull = jax.vjp(
-        lambda rows_in, taps_in, bias_in: conv_local(rows_in, taps_in, bias_in, ext_ids),
-        ext_rows,
-        full_taps.astype(jnp.float32),
-        full_bias.astype(jnp.float32),
-    )
-    silu_value, silu_pull = jax.vjp(jax.nn.silu, conv_out)
-    xs_val = silu_value.astype(jnp.bfloat16)
+    conv_out = conv_local(ext_rows, full_taps.astype(jnp.float32), full_bias.astype(jnp.float32), ext_ids)
+    xs_val = jax.nn.silu(conv_out).astype(jnp.bfloat16)
     xs_wide = xs_val.astype(jnp.float32)
     projected = jnp.dot(xs_val, full_xproj, preferred_element_type=jnp.float32)
     delta_low = projected[:, :R].astype(jnp.bfloat16)
@@ -1196,7 +1484,7 @@
     grad_logits = (
         probability * (grad_probs - jnp.sum(grad_probs * probability, axis=1, keepdims=True))
     ).astype(jnp.bfloat16)
-    grad_router = jnp.dot(normed_two.T, grad_logits, preferred_element_type=jnp.float32)
+    grad_router = contract(grad_logits, normed_two, 0, 0)
     grad_normed_two = grad_from_experts + jnp.dot(
         grad_logits, full_router.T, preferred_element_type=jnp.float32
     )
@@ -1206,7 +1494,6 @@
     grad_gated = jnp.dot(grad_mixed, full_out.T, preferred_element_type=jnp.float32)
     grad_out_proj = jnp.dot(gated.T, grad_mixed, preferred_element_type=jnp.float32)
     grad_y, grad_z = gated_pull(grad_gated)
-    grad_skip = jnp.sum(grad_y * xs_wide, axis=0)
     grad_z = grad_z.astype(jnp.bfloat16)
     grad_y, grad_w_in = lax.optimization_barrier((grad_y, grad_w_in))
     along_b, slope, grad_bs, grad_cs, grad_a, partial_sums = scan_backward(
@@ -1222,75 +1509,57 @@
         kept,
         4,
     )
-    grad_step_all = along_b * xs_wide + slope * (1.0 / LOG2E)
-    grad_xss = along_b * step_size
-    grad_log_decay = (grad_a * a_swap).T
-    soft_slope = jax.nn.sigmoid(dt_pre)
-    grad_pre_wide = grad_step_all * soft_slope
-    grad_dt_bias = jnp.sum(grad_pre_wide, axis=0)
-    grad_dt_pre = grad_pre_wide.astype(jnp.bfloat16)
-    grad_dt_proj = jnp.dot(delta_low.T, grad_dt_pre, preferred_element_type=jnp.float32)
-    grad_delta = jnp.dot(grad_dt_pre, full_dt.T, preferred_element_type=jnp.float32)
-    grad_projected = jnp.concatenate(
-        [grad_delta, grad_bs, grad_cs], axis=1
-    ).astype(jnp.bfloat16)
-    grad_x_proj = jnp.dot(xs_val.T, grad_projected, preferred_element_type=jnp.float32)
-    grad_xs_total = (
-        skip_wide * grad_y
-        + grad_xss
-        + jnp.dot(grad_projected, full_xproj.T, preferred_element_type=jnp.float32)
-    )
-    grad_conv = silu_pull(grad_xs_total)[0]
-    grad_ext, grad_taps, grad_cbias = conv_pull(grad_conv)
-    from_next = shifted(grad_ext[: KC - 1], "ctx", -1)
-    grad_conv_in = grad_ext[KC - 1 :] + jnp.concatenate(
-        [jnp.zeros((tokens_here - (KC - 1), DI), jnp.float32), from_next], axis=0
-    )
-    grad_conv_in = grad_conv_in.astype(jnp.bfloat16)
-    grad_normed_one = dot(grad_conv_in, full_conv.T) + dot(grad_z, full_gate.T)
-    grad_inputs_norm, grad_norm_gain = norm_one_pull(grad_normed_one)
-    grad_inputs = grad_resid + grad_inputs_norm
-    sums = (
-        grad_x_proj,
-        grad_dt_proj.T,
-        grad_taps,
-        grad_cbias[:, None],
-        grad_dt_bias[:, None],
-        grad_log_decay,
-        grad_skip[:, None],
-        jnp.stack(
-            [grad_norm_gain.reshape(-1, half_rows), grad_moe_gain.reshape(-1, half_rows)], axis=1
-        ).reshape(-1, 1),
-        grad_router.reshape(-1, experts // 2),
-    )
-
-    own_conv, own_small, own_gate, own_out = reduce_all(
+    same_rows = jnp.stack(
+        [(ext_ids[KC - 1 - j : KC - 1 - j + tokens_here] == seg_row).astype(jnp.float32) for j in range(1, KC)]
+    )
+    wide_rows = jnp.concatenate(
+        [full_norm.astype(jnp.float32)[None], grad_moe_gain[None], jnp.zeros((6, D), jnp.float32), grad_router]
+    )
+    grad_inputs, own_conv, own_gate, own_out, own_x, own_dt, own_taps, own_decay, own_rows, own_pair, own_router = finish(
         sizes,
         (
-            dot(normed_one.T, grad_conv_in).astype(jnp.bfloat16),
-            jnp.concatenate(sums, axis=1).astype(jnp.bfloat16),
+            along_b,
+            slope,
+            grad_y,
+            dt_pre,
+            conv_out,
+            xs_val,
+            jnp.concatenate([edge_all, conv_in], axis=0),
+            grad_z,
+            full_conv,
+            full_gate,
+        ),
+        (
+            normed_one,
+            inputs[0],
+            grad_resid,
+            mix,
+            jnp.pad(jnp.concatenate([grad_bs, grad_cs], axis=1), ((0, 0), (R, LANES - R - 2 * NS))),
+            jnp.pad(delta_low, ((0, 0), (R + 2 * NS, 0))),
+            jnp.broadcast_to(same_rows[:, :, None], (KC - 1, tokens_here, LANES)),
+            jnp.concatenate([by_channel[:KC], by_channel[26:27], jnp.zeros((3, DI), half)]).astype(jnp.float32),
+            grad_a * a_swap,
+            wide_rows,
         ),
         partial_sums,
+        experts,
         1,
     )
-    own_x, own_dt, own_taps, own_bias, own_dtbias, own_decay, own_skip, own_gains, own_router = [
-        own_small[:, end - width : end] for end, width in zip(ends, widths)
-    ]
     return (
         out_block,
         grad_inputs[None],
-        own_gains[:half_rows, 0],
+        own_pair[0],
         jnp.concatenate([own_conv, own_gate], axis=1),
         own_taps,
-        own_bias[:, 0],
+        own_rows[0],
         own_x,
-        own_dt.T,
-        own_dtbias[:, 0],
+        own_dt,
+        own_rows[1],
         own_decay,
-        own_skip[:, 0],
+        own_rows[2],
         own_out,
-        own_gains[half_rows:, 0],
-        own_router.reshape(half_rows, experts),
+        own_pair[1],
+        own_router,
         grad_w_in[None],
         grad_w_out[None],
     )

time: 395 us -> 393 us (level)
  the two profiles are of different devices: /device:TPU:0 before, /device:TPU:8 now
where the time goes in v2:
time: 393 us; the launch traced here: 385 us
  Pallas kernels  273 us (69%)
  local copies, waits for them, and re-layouts  39.2 us (10%)
  other arithmetic  31.6 us (8%)
  matrix products  25.2 us (6%)
  waiting for transfers between devices  12.6 us (3%)
    pallas_call x1, Pallas kernels, run_experts(): pl.pallas_call(functools.partial(expert_kernel, slices), in_specs=[inside...  80.2 us
    pallas_call x1, Pallas kernels, scan_backward(): pl.pallas_call(functools.partial(backward_kernel, places, streams, len(la...  64.3 us
    pallas_call x1, Pallas kernels, finish(): pl.pallas_call(functools.partial(finish_kernel, places, streams, third, l...  52.9 us
    pallas_call x1, Pallas kernels, scan_forward(): pl.pallas_call(functools.partial(forward_kernel, places, streams, pick(ch...  45.3 us
    pallas_call x1, Pallas kernels, gather_all(): pl.pallas_call(functools.partial(gather_kernel, places, streams, late, fa...  30.8 us
    unnamed x106, local copies, waits for them, and re-layouts  17 us
    ppermute x2, waiting for transfers between devices, flipped(): lax.ppermute(value, 'ctx', [(source, source ^ 1 << level) for source in r...  12.6 us
    dot_general x4, matrix products, dot(): return jnp.dot(left, right, preferred_element_type=jnp.float32)  8.26 us
  transfers between devices with their start and end apart: 2, of which 1 were waited for; matrix products, arithmetic and copies ran while one was open for 13% of the time, Pallas kernels for 0%

profile of v2, /device:TPU:8, one launch (start us, length us, event | category | flops | bytes accessed | tf_op | source)
XLA Modules:
  0.0 385.3 jit_solution(9047945974006889527)
XLA Ops:
  0.7 1.6 fusion.68
  12.0 1.4 concatenate.39.refs_1_
  13.4 30.8 %gather_all.1 = (bf16[2,2,2,2,2,24,1536]{6,5,4,3,2,1,0:T(8,128)(2,1)}, bf16[2,2,2,2,2,48,256]{6,5,4,3,2,1,0:T(8,128)(2,1)}, bf16[2,2,2,2,2,24,128]{6,5,4,3,2,1,0...) custom-call(bf16[24,1536]{1,0:T(8,128)(2,1)} %get-tuple-element.200.refs_, ...), custom_call_target="tpu_custom_call" | custom-call | tf_op jit(solution)/shard_map/gather_all/pallas_call | solution.py:215
  44.7 1.8 fusion.15
  46.5 1.3 slice_reduce_fusion.7
  47.8 2.4 copy.115
  50.2 1.0 slice_bitcast_fusion
  53.3 0.9 reduce-window.6
  57.9 0.9 fusion.38
  59.4 1.1 fusion.17.refs_10_
  60.5 2.2 convolution_convert_fusion.2
  64.7 1.6 maximum_convert_fusion
  66.4 3.2 multiply_convert_fusion.1
  70.3 4.8 %convert_multiply_fusion.1 = (f32[384,1536]{1,0:T(8,128)}, f32[384,1536]{1,0:T(8,128)}, f32[384,1536]{1,0:T(8,128)}) fusion(bf16[384,1536]{1,0:T(8,128)(2,1)S(1)} %get-tuple-element.187.refs_5_, pred[384]{0:T(512)(128)(4,1)S(1)} %get-tuple-element.213, f32[1536]{0:T(1024)S(1)} %copy-done.30, bf16[1536,256]{1,0:T(8,128)(2,1)S(1)} %bitcast.92, ...), kind=kOutput, calls=%fused_computation.6 | convolution fusion | flops 62521344 | bytes 8696320 | tf_op jit(solution)/shard_map/dot_general | solution.py:1436
  75.1 0.8 slice.209
  76.7 0.8 copy.119.refs_2_
  78.6 2.4 pad_maximum_fusion.refs_6_
  81.6 0.8 fusion.37.refs_4_.refs_5_
  82.6 45.3 %scan_forward.1 = (f32[384,1536]{1,0:T(8,128)S(1)}, f32[16,1536]{1,0:T(8,128)}, bf16[4,16,1536]{2,1,0:T(8,128)(2,1)S(1)}, bf16[385,16,1536]{2,1,0:T(8,128)(2,1)}...) custom-call(f32[384,1536]{1,0:T(8,128)} %get-tuple-element.192.refs_0_, ...), custom_call_target="tpu_custom_call" | custom-call | flops 84934656 | bytes 84934656 | tf_op jit(solution)/shard_map/scan_forward/pallas_call | solution.py:635
  127.9 2.8 multiply_convert_fusion
  131.1 1.0 copy-done.43
  132.1 1.2 multiply_reduce_fusion.2
  134.3 1.0 fusion.18.refs_1_
  135.3 80.2 %run_experts.1 = (bf16[384,768]{1,0:T(8,128)(2,1)}, bf16[384,768]{1,0:T(8,128)(2,1)}, f32[768,768]{1,0:T(8,128)}, bf16[768,768]{1,0:T(8,128)(2,1)}, bf16[768,768]{1,0:T(8,128)(2,1)}) custom-call(bf16[384,768]{1,0:T(8,128)(2,1)} %copy-done.13, bf16[384,768]{1,0:T(8,128)(2,1)} %fusion.18.refs_1_, s32[384,1]{1,0:T(8,128)} %copy.119.refs_2_, ...), custom_call_target="tpu_custom_call" | custom-call | tf_op jit(solution)/shard_map/run_experts/pallas_call | solution.py:1298
  215.6 1.4 fusion.19
  217.1 1.9 multiply_reduce_fusion
  219.0 1.1 collective-permute-start.1
  220.1 1.3 convert_add_fusion.1
  222.3 5.1 %fusion.3 = (bf16[384,1536]{1,0:T(8,128)(2,1)S(1)}, f32[384,1536]{1,0:T(8,128)}) fusion(f32[384,1536]{1,0:T(8,128)} %get-tuple-element.216, f32[384,1536]{1,0:T(8,128)S(1)} %copy-done.8, bf16[384,1536]{1,0:T(8,128)(2,1)S(1)} %copy-done.11, f32[1536]{0:T(1024)S(1)} %copy-done.37, bf16[1536,768]{1,0:T(8,128)(2,1)S(1)} %bitcast.114, ...), kind=kOutput, calls=%fused_computation.11 | convolution fusion | flops 915701760 | bytes 12982272 | tf_op jit(solution)/shard_map/dot_general | solution.py:1494
  227.7 0.8 pad_maximum_fusion.2.refs_19_
  228.5 2.9 convolution_convert_fusion.1
  231.4 2.9 convolution_convert_fusion
  234.2 12.6 %collective-permute-done.1 = bf16[768,768]{1,0:T(8,128)(2,1)S(1)} collective-permute-done((bf16[768,768]{1,0:T(8,128)(2,1)S(1)}, bf16[768,768]{1,0:T(8,128)(2,1)S(1)}, u32[]{:S(2)}, u32[]{:S(2)}) %collective-permute-start.1) | collective-permute-done | bytes 1179680 | tf_op jit(solution)/shard_map/ppermute | solution.py:1336
  246.8 1.7 convert_add_fusion
  248.5 64.3 %scan_backward.1 = (f32[384,1536]{1,0:T(8,128)}, f32[384,1536]{1,0:T(8,128)}, f32[6,8,1024]{2,1,0:T(8,128)}, f32[6,8,1024]{2,1,0:T(8,128)}, f32[16,1536]{1,0:T(8...) custom-call(f32[384,1536]{1,0:T(8,128)} %get-tuple-element.192.refs_0_, ...), custom_call_target="tpu_custom_call" | custom-call | flops 141557760 | bytes 141557760 | tf_op jit(solution)/shard_map/scan_backward/pallas_call | solution.py:741
  312.8 1.6 fusion.36.refs_18_
  314.4 1.1 slice_reduce_fusion
  315.8 0.9 select_maximum_fusion.refs_14_
  316.6 1.0 broadcast_in_dim.94.refs_16_
  317.6 52.9 %finish.1 = (f32[384,768]{1,0:T(8,128)}, f32[24,1536]{1,0:T(8,128)}, f32[24,1536]{1,0:T(8,128)}, f32[48,768]{1,0:T(8,128)}, f32[48,80]{1,0:T(8,128)}, /*index=5*...) custom-call(f32[384,1536]{1,0:T(8,128)} %get-tuple-element.78.refs_0, ...), custom_call_target="tpu_custom_call" | custom-call | tf_op jit(solution)/shard_map/finish/pallas_call | solution.py:1062
  370.6 1.6 copy.121
  372.1 1.4 copy.122
  373.5 1.4 copy.120
  374.9 1.3 slice_bitcast_fusion.5
  376.2 1.3 slice_bitcast_fusion.4
  377.4 1.7 pad_maximum_fusion.1
  379.2 2.4 copy.131
  383.4 1.4 copy.135
  (164 shorter events, 26.6 us)
Async XLA Ops:
  0.6 52.0 %copy-start.39 = (s32[1,384]{1,0:T(1,128)S(1)}, s32[1,384]{1,0:T(1,128)}, u32[]{:S(2)}) copy-start(s32[1,384]{1,0:T(1,128)} %param.19) | copy-start | bytes 4612
  0.7 52.6 %copy-start.35 = (s32[1,384,1]{1,2,0:T(1,128)S(1)}, s32[1,384,1]{1,2,0:T(1,128)}, u32[]{:S(2)}) copy-start(s32[1,384,1]{1,2,0:T(1,128)} %param.20) | copy-start | bytes 4612
  11.3 48.1 %copy-start.15 = (bf16[1,384,768]{2,1,0:T(8,128)(2,1)S(1)}, bf16[1,384,768]{2,1,0:T(8,128)(2,1)}, u32[]{:S(2)}) copy-start(bf16[1,384,768]{2,1,0:T(8,128)(2,1)} %param.18) | copy-start | bytes 1769476
  44.2 11.5 %copy-start.20 = (bf16[2,2,2,2,2,24,128]{6,5,4,3,2,1,0:T(8,128)(2,1)S(1)}, bf16[2,2,2,2,2,24,128]{6,5,4,3,2,1,0:T(8,128)(2,1)}, u32[]{:S(2)}) copy-start(bf16[2,2,2,2,2,24,128]{6,5,4,3,2,1,0:T(8,128)(2,1)} %get-tuple-element.60) | copy-start | bytes 589828
  44.2 38.3 %collective-permute-start = (bf16[768,768]{1,0:T(8,128)(2,1)}, bf16[768,768]{1,0:T(8,128)(2,1)}, u32[]{:S(2)}, u32[]{:S(2)}) collective-permute-start(bf16[768,768]{1,0:T(8,128)(2,1)} %bitcast.102), channel_id=1, source_target_pairs={{0,16},{8,24},{16,0},{24,8},{1,17},{9,25},{17,1},{25,9},{2,18},{10... | collective-permute-start | bytes 3538952 | tf_op jit(solution)/shard_map/ppermute | solution.py:1336
  47.8 12.7 %copy-start.12 = (bf16[2,2,2,2,2,24,1536]{6,5,4,3,2,1,0:T(8,128)(2,1)S(1)}, bf16[2,2,2,2,2,24,1536]{6,5,4,3,2,1,0:T(8,128)(2,1)}, u32[]{:S(2)}) copy-start(bf16[2,2,2,2,2,24,1536]{6,5,4,3,2,1,0:T(8,128)(2,1)} %get-tuple-element.61) | copy-start | bytes 7077892
  51.2 0.8 copy-start.26
  60.5 2.2 copy-start.29
  62.7 1.1 copy-start.28
  62.7 1.2 copy-start.34
  62.7 1.3 copy-start.36
  63.1 3.2 copy-start.31
  66.3 3.3 copy-start.18
  66.3 4.0 %copy-start.30 = (f32[1536]{0:T(1024)S(1)}, f32[1536]{0:T(1024)}, u32[]{:S(2)}) copy-start(f32[1536]{0:T(1024)} %get-tuple-element.181) | copy-start | bytes 18436
  69.6 5.5 %copy-start.9 = (bf16[384,1536]{1,0:T(8,128)(2,1)}, bf16[384,1536]{1,0:T(8,128)(2,1)S(1)}, u32[]{:S(2)}) copy-start(bf16[384,1536]{1,0:T(8,128)(2,1)S(1)} %get-tuple-element.187.refs_5_) | copy-start | bytes 3538948
  70.1 12.4 %copy-start.3 = (f32[16,384]{1,0:T(8,128)}, f32[16,384]{1,0:T(8,128)S(1)}, u32[]{:S(2)}) copy-start(f32[16,384]{1,0:T(8,128)S(1)} %get-tuple-element.201.refs_3_.refs_4_) | copy-start | bytes 73732
  70.1 12.4 %copy-start.4 = (f32[16,384]{1,0:T(8,128)}, f32[16,384]{1,0:T(8,128)S(1)}, u32[]{:S(2)}) copy-start(f32[16,384]{1,0:T(8,128)S(1)} %get-tuple-element.202.refs_2_.refs_3_) | copy-start | bytes 73732
  70.3 6.4 %copy-start.38 = (s32[384,1]{0,1:T(1,128)S(1)}, s32[384,1]{0,1:T(1,128)}, u32[]{:S(2)}) copy-start(s32[384,1]{0,1:T(1,128)} %bitcast_add_fusion.1) | copy-start | bytes 4612
  75.1 7.4 %copy-start.5 = (bf16[2,2,24,1536]{3,2,1,0:T(8,128)(2,1)S(1)}, bf16[2,2,24,1536]{3,2,1,0:T(8,128)(2,1)}, u32[]{:S(2)}) copy-start(bf16[2,2,24,1536]{3,2,1,0:T(8,128)(2,1)} %get-tuple-element.64.refs_5_) | copy-start | bytes 884740
  75.1 7.4 %copy-start.6 = (bf16[2,2,48,768]{3,2,1,0:T(8,128)(2,1)S(1)}, bf16[2,2,48,768]{3,2,1,0:T(8,128)(2,1)}, u32[]{:S(2)}) copy-start(bf16[2,2,48,768]{3,2,1,0:T(8,128)(2,1)} %get-tuple-element.65.refs_6_) | copy-start | bytes 884740
  82.5 45.4 %copy-start.1 = (f32[16,1536]{1,0:T(8,128)}, f32[16,1536]{1,0:T(8,128)S(1)}, u32[]{:S(2)}) copy-start(f32[16,1536]{1,0:T(8,128)S(1)} %fusion.37.refs_4_.refs_5_) | copy-start | bytes 294916
  82.5 45.4 %copy-start.10 = (bf16[384,1536]{1,0:T(8,128)(2,1)S(1)}, bf16[384,1536]{1,0:T(8,128)(2,1)}, u32[]{:S(2)}) copy-start(bf16[384,1536]{1,0:T(8,128)(2,1)} %copy-done.9) | copy-start | bytes 3538948
  82.5 45.4 %copy-start.16 = (bf16[1,384,768]{2,1,0:T(8,128)(2,1)S(1)}, bf16[1,384,768]{2,1,0:T(8,128)(2,1)}, u32[]{:S(2)}) copy-start(bf16[1,384,768]{2,1,0:T(8,128)(2,1)} %param.18) | copy-start | bytes 1769476
  82.5 45.4 %copy-start.37 = (f32[1536]{0:T(1024)S(1)}, f32[1536]{0:T(1024)}, u32[]{:S(2)}) copy-start(f32[1536]{0:T(1024)} %get-tuple-element.180) | copy-start | bytes 18436
  127.9 2.8 copy-start
  127.9 2.8 copy-start.2
  127.9 3.2 copy-start.7
  127.9 4.2 %copy-start.41 = (bf16[2,2,2,2,2,48,768]{6,5,4,3,2,1,0:T(8,128)(2,1)S(1)}, bf16[2,2,2,2,2,48,768]{6,5,4,3,2,1,0:T(8,128)(2,1)}, u32[]{:S(2)}) copy-start(bf16[2,2,2,2,2,48,768]{6,5,4,3,2,1,0:T(8,128)(2,1)} %get-tuple-element.68) | copy-start | bytes 7077892
  131.1 1.0 copy-start.43
  133.3 1.1 copy-start.17
  133.5 1.9 copy-start.13
  215.6 3.4 copy-start.40
  215.6 4.5 %copy-start.21 = (bf16[384,768]{1,0:T(8,128)(2,1)S(1)}, bf16[384,768]{1,0:T(8,128)(2,1)}, u32[]{:S(2)}) copy-start(bf16[384,768]{1,0:T(8,128)(2,1)} %get-tuple-element.71) | copy-start | bytes 1769476
  217.1 4.4 %copy-start.42 = (bf16[2,2,2,2,2,48,768]{6,5,4,3,2,1,0:T(8,128)(2,1)S(1)}, bf16[2,2,2,2,2,48,768]{6,5,4,3,2,1,0:T(8,128)(2,1)}, u32[]{:S(2)}) copy-start(bf16[2,2,2,2,2,48,768]{6,5,4,3,2,1,0:T(8,128)(2,1)} %get-tuple-element.68) | copy-start | bytes 7077892
  219.0 27.8 %collective-permute-start.1 = (bf16[768,768]{1,0:T(8,128)(2,1)S(1)}, bf16[768,768]{1,0:T(8,128)(2,1)S(1)}, u32[]{:S(2)}, u32[]{:S(2)}) collective-permute-start(bf16[768,768]{1,0:T(8,128)(2,1)S(1)} %copy-done.40), channel_id=1, source_target_pairs={{0,16},{8,24},{16,0},{24,8},{1,17},{9,25},{17,1},{25,9},{2,18},{10... | collective-permute-start | bytes 3538952 | tf_op jit(solution)/shard_map/ppermute | solution.py:1336
  220.1 1.9 copy-start.8
  220.1 2.2 copy-start.11
  221.4 9.9 %copy-start.19 = (f32[384,768]{1,0:T(8,128)}, f32[384,768]{1,0:T(8,128)S(1)}, u32[]{:S(2)}) copy-start(f32[384,768]{1,0:T(8,128)S(1)} %get-tuple-element.193.refs_12_) | copy-start | bytes 3538948
  222.3 5.2 %copy-start.14 = (bf16[384,768]{1,0:T(8,128)(2,1)S(1)}, bf16[384,768]{1,0:T(8,128)(2,1)}, u32[]{:S(2)}) copy-start(bf16[384,768]{1,0:T(8,128)(2,1)} %copy-done.13) | copy-start | bytes 1769476
  222.3 6.2 %copy-start.23 = (bf16[384,768]{1,0:T(8,128)(2,1)S(1)}, bf16[384,768]{1,0:T(8,128)(2,1)}, u32[]{:S(2)}) copy-start(bf16[384,768]{1,0:T(8,128)(2,1)} %fusion.17.refs_10_) | copy-start | bytes 1769476
  227.5 3.9 %copy-start.25 = (bf16[384,1536]{1,0:T(8,128)(2,1)}, bf16[384,1536]{1,0:T(8,128)(2,1)S(1)}, u32[]{:S(2)}) copy-start(bf16[384,1536]{1,0:T(8,128)(2,1)S(1)} %get-tuple-element.189.refs_7_) | copy-start | bytes 3538948
  228.5 2.9 copy-start.44
  231.4 15.4 %copy-start.24 = (bf16[768,768]{1,0:T(8,128)(2,1)S(1)}, bf16[768,768]{1,0:T(8,128)(2,1)}, u32[]{:S(2)}) copy-start(bf16[768,768]{1,0:T(8,128)(2,1)} %get-tuple-element.73) | copy-start | bytes 3538948
  370.5 11.0 %copy-start.33 = (f32[48,80]{1,0:T(8,128)S(1)}, f32[48,80]{1,0:T(8,128)}, u32[]{:S(2)}) copy-start(f32[48,80]{1,0:T(8,128)} %get-tuple-element.246) | copy-start | bytes 46084
  370.5 11.6 %copy-start.32 = (f32[48,48]{1,0:T(8,128)S(1)}, f32[48,48]{1,0:T(8,128)}, u32[]{:S(2)}) copy-start(f32[48,48]{1,0:T(8,128)} %get-tuple-element.247) | copy-start | bytes 27652
  370.5 12.2 %copy-start.27 = (f32[48,768]{1,0:T(8,128)S(1)}, f32[48,768]{1,0:T(8,128)}, u32[]{:S(2)}) copy-start(f32[48,768]{1,0:T(8,128)} %get-tuple-element.251) | copy-start | bytes 442372
  370.6 12.9 %copy-start.22 = (f32[768,768]{1,0:T(8,128)S(1)}, f32[768,768]{1,0:T(8,128)}, u32[]{:S(2)}) copy-start(f32[768,768]{1,0:T(8,128)} %get-tuple-element.97) | copy-start | bytes 7077892
